TPU v7x, 32 devices: a whole 2x2x4 slice. The times are simulated.
32 devices in a mesh: seq: 4 (over x, core), ctx: 8 (over z, y).
Axes of the slice: x: 2, y: 2, z: 4, core: 2. Of those that a mesh axis runs over, the one named last changes fastest.
Arguments:
- tokens: bfloat16 [4096, 2048], P(('seq', 'ctx')), may hold values from -6 to 6
- prefix: int32 [4], P('seq'), may hold values from 102 to 512
- span_order: int32 [4, 16], P('seq'), may hold values from 0 to 15, as said below
- w_query: bfloat16 [2048, 2048], P(('seq', 'ctx')), may hold values from -0.125 to 0.125
- w_key: bfloat16 [1024, 2048], P(('seq', 'ctx')), may hold values from -0.125 to 0.125
- w_value: bfloat16 [1024, 2048], P(('seq', 'ctx')), may hold values from -0.125 to 0.125
- w_out: bfloat16 [2048, 2048], P(('seq', 'ctx')), may hold values from -6 to 6
- w_headgate: bfloat16 [16, 2048], P(None, ('seq', 'ctx')), may hold values from -0.125 to 0.125
- attn_gain: bfloat16 [2048], P(('seq', 'ctx')), may hold values from 0.25 to 1.75
- query_gain: bfloat16 [128], P(('seq', 'ctx')), may hold values from 0.25 to 1.75
- key_gain: bfloat16 [128], P(('seq', 'ctx')), may hold values from 0.25 to 1.75
- mlp_gain: bfloat16 [2048], P(('seq', 'ctx')), may hold values from 0.25 to 1.75
- w_gate: bfloat16 [6144, 2048], P(('seq', 'ctx')), may hold values from -0.125 to 0.125
- w_up: bfloat16 [6144, 2048], P(('seq', 'ctx')), may hold values from -0.125 to 0.125
- w_down: bfloat16 [6144, 2048], P(('seq', 'ctx')), may hold values from -0.078125 to 0.078125
- cotangent: bfloat16 [4096, 2048], P(('seq', 'ctx')), may hold values from -6 to 6
Outputs:
- output: bfloat16 [4096, 2048], P(('seq', 'ctx'))
- grad_tokens: float32 [4096, 2048], P(('seq', 'ctx'))
- grad_w_query: float32 [2048, 2048], P(('seq', 'ctx'))
- grad_w_key: float32 [1024, 2048], P(('seq', 'ctx'))
- grad_w_value: float32 [1024, 2048], P(('seq', 'ctx'))
- grad_w_out: float32 [2048, 2048], P(('seq', 'ctx'))
- grad_w_headgate: float32 [16, 2048], P(None, ('seq', 'ctx'))
- grad_attn_gain: float32 [2048], P(('seq', 'ctx'))
- grad_query_gain: float32 [128], P(('seq', 'ctx'))
- grad_key_gain: float32 [128], P(('seq', 'ctx'))
- grad_mlp_gain: float32 [2048], P(('seq', 'ctx'))
- grad_w_gate: float32 [6144, 2048], P(('seq', 'ctx'))
- grad_w_up: float32 [6144, 2048], P(('seq', 'ctx'))
- grad_w_down: float32 [6144, 2048], P(('seq', 'ctx'))
Inputs may be any that keep to these rules, and one draw needn't show every extreme that they name: `span_order`: for every sequence, slots 2c and 2c+1 (the spans of ctx index c) hold a span position p below 8 and its mirror 1024 // 64 - 1 - p; every span position appears exactly once.
All inputs are finite; a program needn't handle non-finite values.
Results may differ from a plain program's by a relative error of at most 0.022.
Values may be sent and summed in bfloat16 or wider, within the bound.
No kernel may reach another device: no remote copies, remote signals or barrier semaphores. Data moves between devices by JAX's collectives and lax.ppermute only.
A program may use at most 320 MiB of HBM per device.

v0:
```python
import jax
import jax.numpy as jnp
from jax import lax
from jax.sharding import PartitionSpec as P

H = 16
KVH = 8
HD = 128


EPS = 1e-06
ROPE_BASE = 1000000.0
NEG = -1e30


def rotate(v, positions, sign):
    half = v.shape[-1] // 2
    inv_freq = 1.0 / ROPE_BASE ** (jnp.arange(half, dtype=jnp.float32) * 2.0 / v.shape[-1])
    angles = positions.astype(jnp.float32)[:, None] * inv_freq[None, :]
    cosine = jnp.cos(angles)[:, None, :]
    sine = sign * jnp.sin(angles)[:, None, :]
    first = v[..., :half]
    second = v[..., half:]
    return jnp.concatenate(
        [first * cosine - second * sine, second * cosine + first * sine], axis=-1
    )


def norm_apply(v, gain):
    factor = lax.rsqrt(jnp.mean(v * v, axis=-1, keepdims=True) + EPS)
    return (v * factor * gain, factor)


def norm_back(v, factor, gain, grad):
    weighted = grad * gain
    grad_v = factor * weighted - v * (factor * factor * factor) * jnp.mean(
        weighted * v, axis=-1, keepdims=True
    )
    return (grad_v, grad * v * factor)


def project(left, right):
    return lax.dot_general(
        left, right, (((1,), (1,)), ((), ())), preferred_element_type=jnp.float32
    )


def outer(left, right):
    return lax.dot_general(
        left, right, (((0,), (0,)), ((), ())), preferred_element_type=jnp.float32
    )


def block_scores(query_block, key_block, allowed, factor):
    scores = (
        jnp.einsum("hgtd,khd->hgtk", query_block, key_block, preferred_element_type=jnp.float32)
        * factor
    )
    return jnp.where(allowed[None, None], scores, NEG)


def per_device(
    tokens,
    prefix,
    span_order,
    w_query,
    w_key,
    w_value,
    w_out,
    w_headgate,
    attn_gain,
    query_gain,
    key_gain,
    mlp_gain,
    w_gate,
    w_up,
    w_down,
    cotangent,
):
    rows = tokens.shape[0]
    span = rows // 2
    length = rows * lax.axis_size("ctx")
    heads = H
    kv_heads = KVH
    head = HD
    group = heads // kv_heads
    pair = 2
    pairs = kv_heads // pair
    factor = head ** (-0.5)
    order = span_order[0]
    offsets = jnp.arange(span, dtype=jnp.int32)
    every_pos = (order[:, None] * span + offsets[None, :]).reshape(length)
    mine = lax.dynamic_slice_in_dim(every_pos, lax.axis_index("ctx") * rows, rows)
    limit = jnp.maximum(mine, prefix[0] - 1)
    allowed = every_pos[None, :] <= limit[:, None]
    wq, wk, wv, wo, wgt, g1, gq, gk, g2 = (
        lax.all_gather(w_query, ("seq", "ctx"), axis=0, tiled=True),
        lax.all_gather(w_key, ("seq", "ctx"), axis=0, tiled=True),
        lax.all_gather(w_value, ("seq", "ctx"), axis=0, tiled=True),
        lax.all_gather(w_out, ("seq", "ctx"), axis=0, tiled=True),
        lax.all_gather(w_headgate, ("seq", "ctx"), axis=1, tiled=True),
        lax.all_gather(attn_gain, ("seq", "ctx"), axis=0, tiled=True),
        lax.all_gather(query_gain, ("seq", "ctx"), axis=0, tiled=True),
        lax.all_gather(key_gain, ("seq", "ctx"), axis=0, tiled=True),
        lax.all_gather(mlp_gain, ("seq", "ctx"), axis=0, tiled=True),
    )
    x = tokens.astype(jnp.float32)
    xn1_full, scale1 = norm_apply(x, g1.astype(jnp.float32))
    xn1 = xn1_full.astype(jnp.bfloat16)
    query = project(xn1, wq).reshape(rows, heads, head)
    key = project(xn1, wk).reshape(rows, kv_heads, head)
    value = project(xn1, wv).astype(jnp.bfloat16)
    logits = project(xn1, wgt)
    query_normed, query_scale = norm_apply(query, gq.astype(jnp.float32))
    key_normed, key_scale = norm_apply(key, gk.astype(jnp.float32))
    query_rot = rotate(query_normed, mine, 1.0).astype(jnp.bfloat16)
    key_rot = rotate(key_normed, mine, 1.0).astype(jnp.bfloat16).reshape(rows, kv_heads * head)
    keys_all, values_all = (
        lax.all_gather(key_rot, "ctx", axis=0, tiled=True),
        lax.all_gather(value, "ctx", axis=0, tiled=True),
    )
    query_blocks = query_rot.reshape(rows, pairs, pair, group, head).transpose(1, 2, 3, 0, 4)

    def forward_block(index):
        key_block = lax.dynamic_slice_in_dim(keys_all, index * pair * head, pair * head, 1).reshape(
            length, pair, head
        )
        value_block = lax.dynamic_slice_in_dim(
            values_all, index * pair * head, pair * head, 1
        ).reshape(length, pair, head)
        scores = block_scores(query_blocks[index], key_block, allowed, factor)
        lse = jax.nn.logsumexp(scores, axis=-1, keepdims=True)
        probs = jnp.exp(scores - lse).astype(jnp.bfloat16)
        return (
            jnp.einsum("hgtk,khd->hgtd", probs, value_block, preferred_element_type=jnp.float32),
            lse,
        )

    attended_blocks, lse_blocks = lax.map(forward_block, jnp.arange(pairs))
    attended = attended_blocks.transpose(3, 0, 1, 2, 4).reshape(rows, heads, head)
    gates = jax.nn.sigmoid(logits)
    mixed = (attended * gates[:, :, None]).reshape(rows, heads * head).astype(jnp.bfloat16)
    hidden1 = x + jnp.dot(mixed, wo, preferred_element_type=jnp.float32)
    xn2_full, scale2 = norm_apply(hidden1, g2.astype(jnp.float32))
    xn2 = xn2_full.astype(jnp.bfloat16)
    gate_local, up_local, down_local = (
        lax.all_gather(w_gate, "seq", axis=0, tiled=True),
        lax.all_gather(w_up, "seq", axis=0, tiled=True),
        lax.all_gather(w_down, "seq", axis=0, tiled=True),
    )
    xn2_all, grad_y_all = (
        lax.all_gather(xn2, "ctx", axis=0, tiled=True),
        lax.all_gather(cotangent, "ctx", axis=0, tiled=True),
    )
    gate_part = project(xn2_all, gate_local)
    up_part = project(xn2_all, up_local)
    act_part = (jax.nn.silu(gate_part) * up_part).astype(jnp.bfloat16)
    branch = lax.psum_scatter(
        jnp.dot(act_part, down_local, preferred_element_type=jnp.float32).astype(jnp.bfloat16),
        "ctx",
        scatter_dimension=0,
        tiled=True,
    ).astype(jnp.float32)
    output = (hidden1 + branch).astype(jnp.bfloat16)
    gate_all = project(xn2_all, gate_local)
    up_all = project(xn2_all, up_local)
    sig_all = jax.nn.sigmoid(gate_all)
    silu_all = gate_all * sig_all
    act_local = (silu_all * up_all).astype(jnp.bfloat16)
    grad_act_all = project(grad_y_all, down_local)
    grad_gate_local = (grad_act_all * up_all * sig_all * (1.0 + gate_all * (1.0 - sig_all))).astype(
        jnp.bfloat16
    )
    grad_up_local = (grad_act_all * silu_all).astype(jnp.bfloat16)
    grad_xn2 = lax.psum_scatter(
        (
            jnp.dot(grad_gate_local, gate_local, preferred_element_type=jnp.float32)
            + jnp.dot(grad_up_local, up_local, preferred_element_type=jnp.float32)
        ).astype(jnp.bfloat16),
        "ctx",
        scatter_dimension=0,
        tiled=True,
    ).astype(jnp.float32)
    grad_w_gate, grad_w_up, grad_w_down = (
        lax.psum_scatter(
            outer(grad_gate_local, xn2_all).astype(jnp.bfloat16),
            "seq",
            scatter_dimension=0,
            tiled=True,
        ).astype(jnp.float32),
        lax.psum_scatter(
            outer(grad_up_local, xn2_all).astype(jnp.bfloat16),
            "seq",
            scatter_dimension=0,
            tiled=True,
        ).astype(jnp.float32),
        lax.psum_scatter(
            outer(act_local, grad_y_all).astype(jnp.bfloat16),
            "seq",
            scatter_dimension=0,
            tiled=True,
        ).astype(jnp.float32),
    )
    grad_h1_norm, gain2_terms = norm_back(hidden1, scale2, g2.astype(jnp.float32), grad_xn2)
    grad_hidden1 = cotangent.astype(jnp.float32) + grad_h1_norm
    grad_gain2 = jnp.sum(gain2_terms, axis=0)
    grad_branch = grad_hidden1.astype(jnp.bfloat16)
    grad_w_out = outer(mixed, grad_branch)
    grad_mixed = project(grad_branch, wo).reshape(rows, heads, head)
    grad_att = (grad_mixed * gates[:, :, None]).astype(jnp.bfloat16)
    grad_logits = (jnp.sum(grad_mixed * attended, axis=-1) * gates * (1.0 - gates)).astype(
        jnp.bfloat16
    )
    grad_blocks = grad_att.reshape(rows, pairs, pair, group, head).transpose(1, 2, 3, 0, 4)

    def backward_block(index):
        key_block = lax.dynamic_slice_in_dim(keys_all, index * pair * head, pair * head, 1).reshape(
            length, pair, head
        )
        value_block = lax.dynamic_slice_in_dim(
            values_all, index * pair * head, pair * head, 1
        ).reshape(length, pair, head)
        query_block = query_blocks[index]
        grad_out = grad_blocks[index]
        scores = block_scores(query_block, key_block, allowed, factor)
        probs = jnp.exp(scores - lse_blocks[index])
        grad_probs = jnp.einsum(
            "hgtd,khd->hgtk", grad_out, value_block, preferred_element_type=jnp.float32
        )
        delta = jnp.sum(probs * grad_probs, axis=-1, keepdims=True)
        grad_scores = (probs * (grad_probs - delta)).astype(jnp.bfloat16)
        grad_query = (
            jnp.einsum("hgtk,khd->hgtd", grad_scores, key_block, preferred_element_type=jnp.float32)
            * factor
        )
        grad_key = (
            jnp.einsum(
                "hgtk,hgtd->khd", grad_scores, query_block, preferred_element_type=jnp.float32
            )
            * factor
        )
        grad_value = jnp.einsum(
            "hgtk,hgtd->khd",
            probs.astype(jnp.bfloat16),
            grad_out,
            preferred_element_type=jnp.float32,
        )
        return (grad_query, grad_key, grad_value)

    grad_query_blocks, grad_key_all, grad_value_all = lax.map(backward_block, jnp.arange(pairs))
    grad_key_sum, grad_value_sum = (
        lax.psum_scatter(
            grad_key_all.astype(jnp.bfloat16), "ctx", scatter_dimension=1, tiled=True
        ).astype(jnp.float32),
        lax.psum_scatter(
            grad_value_all.astype(jnp.bfloat16), "ctx", scatter_dimension=1, tiled=True
        ).astype(jnp.float32),
    )
    grad_value_rows = (
        grad_value_sum.astype(jnp.bfloat16).transpose(1, 0, 2, 3).reshape(rows, kv_heads * head)
    )
    grad_key_rot = (
        grad_key_sum.astype(jnp.bfloat16)
        .astype(jnp.float32)
        .transpose(1, 0, 2, 3)
        .reshape(rows, kv_heads, head)
    )
    grad_key_normed = rotate(grad_key_rot, mine, -1.0)
    grad_key_pre, key_gain_terms = norm_back(
        key, key_scale, gk.astype(jnp.float32), grad_key_normed
    )
    grad_key_rows = grad_key_pre.astype(jnp.bfloat16).reshape(rows, kv_heads * head)
    grad_key_gain = jnp.sum(key_gain_terms, axis=(0, 1))
    grad_query_rot = (
        grad_query_blocks.transpose(3, 0, 1, 2, 4)
        .reshape(rows, heads, head)
        .astype(jnp.bfloat16)
        .astype(jnp.float32)
    )
    grad_query_normed = rotate(grad_query_rot, mine, -1.0)
    grad_query_pre, query_gain_terms = norm_back(
        query, query_scale, gq.astype(jnp.float32), grad_query_normed
    )
    grad_query_rows = grad_query_pre.astype(jnp.bfloat16).reshape(rows, heads * head)
    grad_query_gain = jnp.sum(query_gain_terms, axis=(0, 1))
    grad_w_query = outer(grad_query_rows, xn1)
    grad_w_key = outer(grad_key_rows, xn1)
    grad_w_value = outer(grad_value_rows, xn1)
    grad_w_headgate = outer(grad_logits, xn1)
    grad_xn1 = jnp.dot(grad_query_rows, wq, preferred_element_type=jnp.float32) + jnp.dot(
        grad_key_rows, wk, preferred_element_type=jnp.float32
    )
    grad_xn1 = (
        grad_xn1
        + jnp.dot(grad_value_rows, wv, preferred_element_type=jnp.float32)
        + jnp.dot(grad_logits, wgt, preferred_element_type=jnp.float32)
    )
    grad_x_norm, gain1_terms = norm_back(x, scale1, g1.astype(jnp.float32), grad_xn1)
    grad_tokens = grad_hidden1 + grad_x_norm
    grad_gain1 = jnp.sum(gain1_terms, axis=0)
    summed = (
        lax.psum_scatter(grad_w_query, ("seq", "ctx"), scatter_dimension=0, tiled=True),
        lax.psum_scatter(grad_w_key, ("seq", "ctx"), scatter_dimension=0, tiled=True),
        lax.psum_scatter(grad_w_value, ("seq", "ctx"), scatter_dimension=0, tiled=True),
        lax.psum_scatter(grad_w_out, ("seq", "ctx"), scatter_dimension=0, tiled=True),
        lax.psum_scatter(grad_w_headgate, ("seq", "ctx"), scatter_dimension=1, tiled=True),
        lax.psum_scatter(grad_gain1, ("seq", "ctx"), scatter_dimension=0, tiled=True),
        lax.psum_scatter(grad_query_gain, ("seq", "ctx"), scatter_dimension=0, tiled=True),
        lax.psum_scatter(grad_key_gain, ("seq", "ctx"), scatter_dimension=0, tiled=True),
        lax.psum_scatter(grad_gain2, ("seq", "ctx"), scatter_dimension=0, tiled=True),
    )
    g_wq, g_wk, g_wv, g_wo, g_wgt, g_g1, g_gq, g_gk, g_g2 = summed
    return (
        output,
        grad_tokens,
        g_wq,
        g_wk,
        g_wv,
        g_wo,
        g_wgt,
        g_g1,
        g_gq,
        g_gk,
        g_g2,
        grad_w_gate,
        grad_w_up,
        grad_w_down,
    )


def solution(mesh):
    in_specs = (
        P(("seq", "ctx"), None),
        P("seq"),
        P("seq", None),
        P(("seq", "ctx"), None),
        P(("seq", "ctx"), None),
        P(("seq", "ctx"), None),
        P(("seq", "ctx"), None),
        P(None, ("seq", "ctx")),
        P(("seq", "ctx")),
        P(("seq", "ctx")),
        P(("seq", "ctx")),
        P(("seq", "ctx")),
        P(("seq", "ctx"), None),
        P(("seq", "ctx"), None),
        P(("seq", "ctx"), None),
        P(("seq", "ctx"), None),
    )
    out_specs = (
        P(("seq", "ctx"), None),
        P(("seq", "ctx"), None),
        P(("seq", "ctx"), None),
        P(("seq", "ctx"), None),
        P(("seq", "ctx"), None),
        P(("seq", "ctx"), None),
        P(None, ("seq", "ctx")),
        P(("seq", "ctx")),
        P(("seq", "ctx")),
        P(("seq", "ctx")),
        P(("seq", "ctx")),
        P(("seq", "ctx"), None),
        P(("seq", "ctx"), None),
        P(("seq", "ctx"), None),
    )
    return jax.shard_map(
        per_device, mesh=mesh, in_specs=in_specs, out_specs=out_specs, check_vma=False
    )
```

profile of v0, /device:TPU:0, one launch (start us, length us, event | category | flops | bytes accessed | tf_op | source)
XLA Modules:
  0.0 2408.7 jit_solution(2360268205686790698)
XLA Ops:
  12.1 42.2 %all-reduce.9 = (bf16[128]{0:T(256)(128)(2,1)S(1)}, bf16[2048]{0:T(1024)(128)(2,1)S(1)}, bf16[128]{0:T(256)(128)(2,1)S(1)}, bf16[2048]{0:T(1024)(128)(2,1)S(1)}) all-reduce(bf16[128]{0:T(256)(128)(2,1)S(1)} %dynamic-update-slice.1, bf16[2048]{0:T(1024)(128)(2,1)S(1)} %dynamic-update-slice, ...), channel_id=1, replica_groups=mesh['seq'=4,'ctx'=8] {'seq','ctx'}, use_global_device_ids=true, to_apply=%add.1 | all-reduce | flops 4352 | bytes 17408
  56.3 19.2 all-gather.19.cloned.1.call-done
  75.5 4.6 convolution_convert_fusion.4
  82.0 57.1 %all-gather.15.cloned.1.call-done = bf16[1024,2048]{1,0:T(8,128)(2,1)} async-done(((bf16[32,2048]{1,0:T(8,128)(2,1)}), bf16[1024,2048]{1,0:T(8,128)(2,1)}) %all-gather.15.cloned.1.call-update) | async-done | bytes 4194320 | tf_op jit(solution)/shard_map/all_gather | solution.py:98
  147.2 68.2 %all-gather = bf16[32,64,16]{1,2,0:T(8,128)(2,1)S(1)} all-gather(bf16[1,64,16]{1,2,0:T(8,128)(2,1)S(1)} %bitcast.352), channel_id=1, replica_groups=mesh['seq'=4,'ctx'=8] {'seq','ctx'}, dimensions={0}, use_global_device_ids=true | all-gather | bytes 67584 | tf_op jit(solution)/shard_map/all_gather | solution.py:101
  219.9 49.1 %all-gather.13.cloned.1.call-done = bf16[2048,2048]{1,0:T(8,128)(2,1)} async-done(((bf16[64,2048]{1,0:T(8,128)(2,1)}), bf16[2048,2048]{1,0:T(8,128)(2,1)}) %all-gather.13.cloned.1.call-update) | async-done | bytes 8388624 | tf_op jit(solution)/shard_map/all_gather | solution.py:97
  269.0 6.3 fusion.81
  278.1 42.3 %all-gather.17.cloned.1.call-done = bf16[1024,1024]{0,1:T(8,128)(2,1)} async-done(((bf16[128,1024]{0,1:T(8,128)(2,1)}), bf16[1024,1024]{0,1:T(8,128)(2,1)}) %all-gather.17.cloned.1.call-update) | async-done | bytes 2097168 | tf_op jit(solution)/shard_map/all_gather | solution.py:119
  320.5 25.3 %while.34 = (s32[]{:T(128)}, f32[4,2,2,128,128]{4,3,2,1,0:T(8,128)S(1)}, f32[4,2,2,128,1]{3,2,1,4,0:T(2,128)S(1)}, s32[4]{0:T(128)S(1)}, bf16[4,2,2,128,128]{4,3...) while((s32[]{:T(128)}, ...), condition=%wide.region_6.7_spmd.clone.clone, body=%wide.region_3.6_spmd.clone.sunk.clone | while | flops 272240640 | bytes 10121929 | solution.py:139
  348.7 49.9 %all-gather.23.cloned.1.call-done = bf16[2048,2048]{1,0:T(8,128)(2,1)} async-done(((bf16[64,2048]{1,0:T(8,128)(2,1)}), bf16[2048,2048]{1,0:T(8,128)(2,1)}) %all-gather.23.cloned.1.call-update) | async-done | bytes 8388624 | tf_op jit(solution)/shard_map/all_gather | solution.py:100
  398.7 4.7 multiply_reduce_fusion.2
  407.0 20.3 all-gather.27.cloned.1.call-done
  427.4 75.5 %all-gather.25.cloned.1.call-done = bf16[1024,2048]{1,0:T(8,128)(2,1)} async-done(((bf16[128,2048]{1,0:T(8,128)(2,1)}), bf16[1024,2048]{1,0:T(8,128)(2,1)}) %all-gather.25.cloned.1.call-update) | async-done | bytes 4194320 | tf_op jit(solution)/shard_map/all_gather | solution.py:152
  502.9 8.3 fusion.86
  511.2 20.3 all-gather.29.cloned.1.call-done
  531.5 8.2 fusion.87
  539.8 21.7 all-gather.31.cloned.1.call-done
  561.5 75.0 %all-gather.33.cloned.1.call-done = bf16[1024,2048]{1,0:T(8,128)(2,1)} async-done(((bf16[128,2048]{1,0:T(8,128)(2,1)}), bf16[1024,2048]{1,0:T(8,128)(2,1)}) %all-gather.33.cloned.1.call-update) | async-done | bytes 4194320 | tf_op jit(solution)/shard_map/all_gather | solution.py:153
  636.5 10.6 multiply_convert_fusion.1
  650.6 5.2 add_convert_fusion
  655.9 7.8 convolution_convert_fusion
  664.7 78.1 %reduce-scatter.21.cloned.1.call-done = bf16[128,2048]{1,0:T(8,128)(2,1)} async-done(((bf16[1024,2048]{1,0:T(8,128)(2,1)}), bf16[128,2048]{1,0:T(8,128)(2,1)}) %reduce-scatter.21.cloned.1.call-update) | async-done | bytes 524304 | tf_op jit(solution)/shard_map/reduce_scatter | solution.py:175
  744.2 90.2 %reduce-scatter.19.cloned.1.call-done = bf16[128,2048]{1,0:T(8,128)(2,1)} async-done(((bf16[1024,2048]{1,0:T(8,128)(2,1)}), bf16[128,2048]{1,0:T(8,128)(2,1)}) %reduce-scatter.19.cloned.1.call-update) | async-done | bytes 524304 | tf_op jit(solution)/shard_map/reduce_scatter | solution.py:158
  836.9 6.3 fusion.68
  847.5 52.9 %while.35 = (s32[]{:T(128)}, bf16[4,2,2,128,128]{4,3,2,1,0:T(8,128)(2,1)}, bf16[4,1024,2,128]{1,3,2,0:T(8,128)(2,1)}, bf16[4,1024,2,128]{1,3,2,0:T(8,128)(2,1)},...) while((s32[]{:T(128)}, ...), condition=%wide.region_13.14_spmd.clone.clone, body=%wide.region_11.13_spmd.clone.sunk.clone | while | flops 676265472 | bytes 60308888 | solution.py:250
  900.4 6.1 copy.173
  906.5 4.5 reshape.380
  911.1 6.2 copy.175
  917.2 4.6 reshape.382
  921.9 7.3 convolution_convert_fusion.3
  930.6 7.2 convolution_convert_fusion.2
  939.2 7.1 convolution_convert_fusion.1
  951.2 27.9 %reduce-scatter.37.cloned.1.call-done = bf16[128,1024]{1,0:T(8,128)(2,1)} async-done(((bf16[1024,1024]{1,0:T(8,128)(2,1)}), bf16[128,1024]{1,0:T(8,128)(2,1)}) %reduce-scatter.37.cloned.1.call-update) | async-done | bytes 262160
  986.4 4.6 fusion.73
  991.0 58.8 %reduce-scatter.39.cloned.1.call-done = bf16[128,1024]{1,0:T(8,128)(2,1)} async-done(((bf16[1024,1024]{1,0:T(8,128)(2,1)}), bf16[128,1024]{1,0:T(8,128)(2,1)}) %reduce-scatter.39.cloned.1.call-update) | async-done | bytes 262160
  1051.2 4.6 fusion.71
  1062.6 8.5 fusion.75
  1072.2 8.1 fusion.66
  1080.3 8.9 reduce-scatter.31.cloned.1.call-done
  1091.6 37.8 %reduce-scatter.33.cloned.1.call-done = bf16[192,2048]{1,0:T(8,128)(2,1)} async-done(((bf16[768,2048]{1,0:T(8,128)(2,1)}), bf16[192,2048]{1,0:T(8,128)(2,1)}) %reduce-scatter.33.cloned.1.call-update) | async-done | bytes 786448 | tf_op jit(solution)/shard_map/reduce_scatter | solution.py:191
  1132.0 37.9 %reduce-scatter.35.cloned.1.call-done = bf16[192,2048]{1,0:T(8,128)(2,1)} async-done(((bf16[768,2048]{1,0:T(8,128)(2,1)}), bf16[192,2048]{1,0:T(8,128)(2,1)}) %reduce-scatter.35.cloned.1.call-update) | async-done | bytes 786448 | tf_op jit(solution)/shard_map/reduce_scatter | solution.py:197
  1172.3 5.6 fusion.89
  1177.9 131.0 %reduce-scatter.41.cloned.1.call-done = f32[64,16]{1,0:T(8,128)} async-done(((f32[2048,16]{1,0:T(8,128)}), f32[64,16]{1,0:T(8,128)}) %reduce-scatter.41.cloned.1.call-update) | async-done | bytes 4112
  1315.5 43.1 %all-reduce.8 = (f32[2048]{0:T(1024)S(1)}, f32[128]{0:T(128)S(1)}, f32[128]{0:T(128)S(1)}, f32[2048]{0:T(1024)S(1)}) all-reduce(f32[2048]{0:T(1024)S(1)} %get-tuple-element.417, f32[128]{0:T(128)S(1)} %bitcast_reduce_fusion, f32[128]{0:T(128)S(1)} %bitcast_reduce_fusion.1, ...), channel_id=11, replica_groups=mesh['seq'=4,'ctx'=8] {'seq','ctx'}, use_global_device_ids=true, to_apply=%region_26.27.clone | all-reduce | flops 4352 | bytes 34816
  1362.4 131.2 %reduce-scatter.25.cloned.1.call-done = f32[32,2048]{1,0:T(8,128)} async-done(((f32[1024,2048]{1,0:T(8,128)}), f32[32,2048]{1,0:T(8,128)}) %reduce-scatter.25.cloned.1.call-update) | async-done | bytes 262160 | tf_op jit(solution)/shard_map/reduce_scatter | solution.py:303
  1493.6 187.6 %reduce-scatter.27.cloned.1.call-done = f32[32,2048]{1,0:T(8,128)} async-done(((f32[1024,2048]{1,0:T(8,128)}), f32[32,2048]{1,0:T(8,128)}) %reduce-scatter.27.cloned.1.call-update) | async-done | bytes 262160 | tf_op jit(solution)/shard_map/reduce_scatter | solution.py:304
  1681.2 360.5 %reduce-scatter.23.cloned.1.call-done = f32[64,2048]{1,0:T(8,128)} async-done(((f32[2048,2048]{1,0:T(8,128)}), f32[64,2048]{1,0:T(8,128)}) %reduce-scatter.23.cloned.1.call-update) | async-done | bytes 524304 | tf_op jit(solution)/shard_map/reduce_scatter | solution.py:302
  2041.7 360.3 %reduce-scatter.29.cloned.1.call-done = f32[64,2048]{1,0:T(8,128)} async-done(((f32[2048,2048]{1,0:T(8,128)}), f32[64,2048]{1,0:T(8,128)}) %reduce-scatter.29.cloned.1.call-update) | async-done | bytes 524304 | tf_op jit(solution)/shard_map/reduce_scatter | solution.py:305
  (341 shorter events, 141.0 us)
Async XLA Ops:
  7.2 68.3 %all-gather.19.cloned.1.call-start = ((), (), s32[]{:S(2)}) async-start(), calls=%async_computation.15 | async-start | bytes 4325376 | tf_op jit(solution)/shard_map/all_gather | solution.py:99
  7.9 72.9 %copy-start.31 = (s32[1,16]{1,0:T(1,128)S(1)}, s32[1,16]{1,0:T(1,128)}, u32[]{:S(2)}) copy-start(s32[1,16]{1,0:T(1,128)} %param.22) | copy-start | bytes 196
  7.9 131.2 %all-gather.15.cloned.1.call-start = ((), (), s32[]{:S(2)}) async-start(), calls=%async_computation.13 | async-start | bytes 4325376 | tf_op jit(solution)/shard_map/all_gather | solution.py:98
  8.7 207.3 %all-gather.21.cloned.1.call-start = ((), (), s32[]{:S(2)}) async-start(), calls=%async_computation.16 | async-start | bytes 2359296 | tf_op jit(solution)/shard_map/all_gather | solution.py:120
  54.4 84.7 %copy-start = (bf16[128,2048]{1,0:T(8,128)(2,1)S(1)}, bf16[128,2048]{1,0:T(8,128)(2,1)}, u32[]{:S(2)}) copy-start(bf16[128,2048]{1,0:T(8,128)(2,1)} %param.20) | copy-start | bytes 1572868
  80.1 188.9 %all-gather.13.cloned.1.call-start = ((), (), s32[]{:S(2)}) async-start(), calls=%async_computation.12 | async-start | bytes 8650752 | tf_op jit(solution)/shard_map/all_gather | solution.py:97
  80.7 239.8 %all-gather.17.cloned.1.call-start = ((), (), s32[]{:S(2)}) async-start(), calls=%async_computation.14 | async-start | bytes 2359296 | tf_op jit(solution)/shard_map/all_gather | solution.py:119
  143.8 71.6 %copy-start.8 = (f32[16,8,8,128]{3,2,1,0:T(8,128)}, f32[16,8,8,128]{3,2,1,0:T(8,128)S(1)}, u32[]{:S(2)}) copy-start(f32[16,8,8,128]{3,2,1,0:T(8,128)S(1)} %copy.184) | copy-start | bytes 1572868
  143.8 3.4 copy-start.27
  145.8 252.9 %all-gather.23.cloned.1.call-start = ((), (), s32[]{:S(2)}) async-start(), calls=%async_computation.17 | async-start | bytes 8650752 | tf_op jit(solution)/shard_map/all_gather | solution.py:100
  146.4 281.0 %all-gather.27.cloned.1.call-start = ((), (), s32[]{:S(2)}) async-start(), calls=%async_computation.19 | async-start | bytes 3932160 | tf_op jit(solution)/shard_map/all_gather | solution.py:147
  147.1 355.8 %all-gather.25.cloned.1.call-start = ((), (), s32[]{:S(2)}) async-start(), calls=%async_computation.18 | async-start | bytes 4718592 | tf_op jit(solution)/shard_map/all_gather | solution.py:152
  215.6 59.7 %copy-start.24 = (bf16[2048,16]{0,1:T(8,128)(2,1)}, bf16[2048,16]{0,1:T(8,128)(2,1)S(1)}, u32[]{:S(2)}) copy-start(bf16[2048,16]{0,1:T(8,128)(2,1)S(1)} %reshape.368) | copy-start | bytes 196612
  345.8 2.9 copy-start.14
  348.7 54.7 %copy-start.10 = (bf16[128,2048]{0,1:T(8,128)(2,1)}, bf16[128,2048]{0,1:T(8,128)(2,1)S(1)}, u32[]{:S(2)}) copy-start(bf16[128,2048]{0,1:T(8,128)(2,1)S(1)} %fusion.57) | copy-start | bytes 1572868
  404.4 127.1 %all-gather.29.cloned.1.call-start = ((), (), s32[]{:S(2)}) async-start(), calls=%async_computation.20 | async-start | bytes 3932160 | tf_op jit(solution)/shard_map/all_gather | solution.py:148
  405.1 156.4 %all-gather.31.cloned.1.call-start = ((), (), s32[]{:S(2)}) async-start(), calls=%async_computation.21 | async-start | bytes 3932160 | tf_op jit(solution)/shard_map/all_gather | solution.py:149
  405.7 230.7 %all-gather.33.cloned.1.call-start = ((), (), s32[]{:S(2)}) async-start(), calls=%async_computation.23 | async-start | bytes 4718592 | tf_op jit(solution)/shard_map/all_gather | solution.py:153
  406.5 336.3 %reduce-scatter.21.cloned.1.call-start = ((), (), s32[]{:S(2)}) async-start(), calls=%async_computation.24 | async-start | bytes 4718592 | tf_op jit(solution)/shard_map/reduce_scatter | solution.py:175
  636.5 10.6 copy-start.29
  647.1 3.4 copy-start.35
  647.1 3.5 copy-start.33
  647.1 3.5 copy-start.30
  655.8 178.6 %reduce-scatter.19.cloned.1.call-start = ((), (), s32[]{:S(2)}) async-start(), calls=%async_computation.22 | async-start | bytes 4718592 | tf_op jit(solution)/shard_map/reduce_scatter | solution.py:158
  663.7 315.4 %reduce-scatter.37.cloned.1.call-start = ((), (), s32[]{:S(2)}) async-start(), calls=%async_computation.32 | async-start | bytes 2359296
  843.2 4.3 copy-start.4
  854.4 2.2 copy-start.20
  854.6 4.8 copy-start.15
  867.6 2.2 copy-start.20
  867.9 4.8 copy-start.15
  880.8 2.2 copy-start.20
  881.1 4.8 copy-start.15
  894.1 2.2 copy-start.20
  894.3 4.8 copy-start.15
  911.0 138.9 %reduce-scatter.39.cloned.1.call-start = ((), (), s32[]{:S(2)}) async-start(), calls=%async_computation.33 | async-start | bytes 2359296
  917.2 4.7 copy-start.36
  921.8 167.4 %reduce-scatter.31.cloned.1.call-start = ((), (), s32[]{:S(2)}) async-start(), calls=%async_computation.29 | async-start | bytes 3932160 | tf_op jit(solution)/shard_map/reduce_scatter | solution.py:185
  929.2 200.3 %reduce-scatter.33.cloned.1.call-start = ((), (), s32[]{:S(2)}) async-start(), calls=%async_computation.30 | async-start | bytes 3932160 | tf_op jit(solution)/shard_map/reduce_scatter | solution.py:191
  937.8 232.0 %reduce-scatter.35.cloned.1.call-start = ((), (), s32[]{:S(2)}) async-start(), calls=%async_computation.31 | async-start | bytes 3932160 | tf_op jit(solution)/shard_map/reduce_scatter | solution.py:197
  946.3 362.6 %reduce-scatter.41.cloned.1.call-start = ((), (), s32[]{:S(2)}) async-start(), calls=%async_computation.34 | async-start | bytes 1081344
  951.2 542.5 %reduce-scatter.25.cloned.1.call-start = ((), (), s32[]{:S(2)}) async-start(), calls=%async_computation.26 | async-start | bytes 8650752 | tf_op jit(solution)/shard_map/reduce_scatter | solution.py:303
  980.3 2.8 copy-start.9
  981.8 3.0 copy-start.13
  991.0 690.2 %reduce-scatter.27.cloned.1.call-start = ((), (), s32[]{:S(2)}) async-start(), calls=%async_computation.27 | async-start | bytes 8650752 | tf_op jit(solution)/shard_map/reduce_scatter | solution.py:304
  1055.9 985.8 %reduce-scatter.23.cloned.1.call-start = ((), (), s32[]{:S(2)}) async-start(), calls=%async_computation.25 | async-start | bytes 17301504 | tf_op jit(solution)/shard_map/reduce_scatter | solution.py:302
  1071.2 1330.8 %reduce-scatter.29.cloned.1.call-start = ((), (), s32[]{:S(2)}) async-start(), calls=%async_computation.28 | async-start | bytes 17301504 | tf_op jit(solution)/shard_map/reduce_scatter | solution.py:305
  1310.3 3.8 copy-start.3
  1314.1 46.9 %copy-start.28 = (f32[128]{0:T(128)S(1)}, f32[128]{0:T(128)}, u32[]{:S(2)}) copy-start(f32[128]{0:T(128)} %get-tuple-element.511) | copy-start | bytes 1540
  (30 other events, 39.5 us)
Sparse Core Ops, SparseCore 0:
  11.1 64.4 all-gather.18
  78.6 60.4 all-gather.14
  141.8 48.3 all-gather.20
  193.0 75.9 all-gather.12
  271.5 48.9 all-gather.16
  323.3 75.2 all-gather.22
  400.2 27.1 all-gather.26
  430.1 72.7 all-gather.24
  504.5 27.0 all-gather.28
  532.9 28.4 all-gather.30
  563.6 72.7 all-gather.32
  655.9 86.8 reduce-scatter.20
  746.4 87.9 reduce-scatter.18
  911.1 67.9 reduce-scatter.36
  982.5 67.3 reduce-scatter.38
  1052.3 36.8 reduce-scatter.30
  1091.6 37.8 reduce-scatter.32
  1131.9 37.8 reduce-scatter.34
  1172.0 136.7 reduce-scatter.40
  1311.6 181.9 reduce-scatter.24
  1496.5 184.6 reduce-scatter.26
  1684.1 357.5 reduce-scatter.22
  2044.6 357.3 reduce-scatter.28
where the time goes:
time: 2420 us; the launch traced here: 2410 us
  waiting for transfers between devices  1950 us (81%)
  blocking collectives  154 us (6%)
  matrix products  151 us (6%)
  local copies, waits for them, and re-layouts  80.5 us (3%)
  other arithmetic  38.1 us (2%)
    reduce_scatter x1, waiting for transfers between devices, per_device(): lax.psum_scatter(grad_w_query, ('seq', 'ctx'), scatter_dimension=0, tiled...  360 us
    reduce_scatter x1, waiting for transfers between devices, per_device(): lax.psum_scatter(grad_w_out, ('seq', 'ctx'), scatter_dimension=0, tiled=T...  360 us
    unnamed x26, waiting for transfers between devices  223 us
    reduce_scatter x1, waiting for transfers between devices, per_device(): lax.psum_scatter(grad_w_value, ('seq', 'ctx'), scatter_dimension=0, tiled...  188 us
    reduce_scatter x1, waiting for transfers between devices, per_device(): lax.psum_scatter(grad_w_key, ('seq', 'ctx'), scatter_dimension=0, tiled=T...  131 us
    reduce_scatter x1, waiting for transfers between devices, per_device(): lax.psum_scatter(jnp.dot(act_part, down_local, preferred_element_type=jnp...  90.2 us
    unnamed x2, blocking collectives  85.4 us
    reduce_scatter x1, waiting for transfers between devices, per_device(): lax.psum_scatter((jnp.dot(grad_gate_local, gate_local, preferred_element_...  78.1 us
  transfers between devices with their start and end apart: 23, of which 22 were waited for; matrix products, arithmetic and copies ran while one was open for 7% of the time, Pallas kernels for 0%

commit v1 on v0

--- a/solution.py
+++ b/solution.py
@@ -1,6 +1,9 @@
 import jax
 import jax.numpy as jnp
 from jax import lax
+from jax.experimental import pallas as pl
+from jax.experimental.pallas import tpu as pltpu
+
 from jax.sharding import PartitionSpec as P
 
 H = 16
@@ -328,6 +331,655 @@
     )
 
 
+BF16 = jnp.bfloat16
+F32 = jnp.float32
+BOTH = ("seq", "ctx")
+ROWS = ((0,), (0,))
+LAST = ((1,), (1,))
+
+
+def swap(v, d):
+    return lax.ppermute(v, "ctx", [(c, c ^ d) for c in range(8)])
+
+
+def hop(v, d):
+    return lax.ppermute(v, BOTH, [(i, i ^ d) for i in range(32)])
+
+
+def turn(v):
+    pairs = [
+        (8 * r + 4 * q + j, 8 * j + 4 * q + r) for r in range(4) for q in range(2) for j in range(4)
+    ]
+    return lax.ppermute(v, BOTH, pairs)
+
+
+def after(v, *others):
+    return lax.optimization_barrier((v, *others))[0]
+
+
+def gather_ctx(own):
+    inner = [(c, c ^ 6) for c in range(8) if (c >> 1) in (1, 2)]
+    outward = [(c, c ^ 2) for c in range(8) if (c >> 1) in (1, 2)]
+    z = lax.axis_index("ctx") >> 1
+    inside = (z == 1) | (z == 2)
+    z1 = swap(own, 2)
+    across = lax.ppermute(own, "ctx", inner)
+    y0 = swap(own, 1)
+    relayed = lax.ppermute(z1, "ctx", inner)
+    outer_near = lax.ppermute(across, "ctx", outward)
+    y1 = swap(z1, 1)
+    outer_far = lax.ppermute(relayed, "ctx", outward)
+    z2 = jnp.where(inside, relayed, outer_near)
+    y2 = swap(z2, 1)
+    z3 = jnp.where(inside, across, outer_far)
+    y3 = swap(z3, 1)
+    return [own, y0, z1, y1, z2, y2, z3, y3]
+
+
+def scatter_ctx(blocks):
+    other = [swap(blocks[2 * dz + 1], 1) for dz in range(4)]
+    kept3 = (blocks[6].astype(F32) + other[3].astype(F32)).astype(BF16)
+    far3 = swap(kept3, 4)
+    kept2 = (blocks[4].astype(F32) + after(other[2], kept3).astype(F32)).astype(BF16)
+    far2 = swap(kept2, 4)
+    kept1 = blocks[2].astype(F32) + other[1].astype(F32)
+    near = swap((kept1 + after(far3, kept2).astype(F32)).astype(BF16), 2)
+    kept0 = blocks[0].astype(F32) + other[0].astype(F32)
+    return kept0 + far2.astype(F32) + near.astype(F32)
+
+
+def picked(v, c):
+    v = v.reshape(8, v.shape[0] // 8, v.shape[1])
+    return [lax.dynamic_index_in_dim(v, c ^ d, 0, keepdims=False) for d in range(8)]
+
+
+def gather_small(v, flat):
+    blocks = v
+    for b in (2, 1, 0, 3, 4):
+        other = hop(blocks, 1 << b)
+        high = ((flat >> b) & 1) == 1
+        blocks = jnp.where(high, jnp.stack([other, blocks]), jnp.stack([blocks, other]))
+    return blocks.transpose((0, 1, 4, 3, 2, 5, 6)).reshape((32,) + v.shape)
+
+
+def sum_small(v):
+    for b in (0, 1, 2, 3, 4):
+        v = v + hop(v, 1 << b)
+    return v
+
+
+def dot(left, right, dims):
+    return lax.dot_general(left, right, (dims, ((), ())), preferred_element_type=F32)
+
+
+def full(shape, **kw):
+    return pl.BlockSpec(shape, lambda *_: (0,) * len(shape), **kw)
+
+
+def call(kernel, *rest, **kw):
+    inner = kernel_call(kernel, *rest, **kw)
+
+    return inner
+
+
+def kernel_call(kernel, grid, in_specs, out_specs, out_shape, flops, moved, exps=0, scratch=()):
+    return pl.pallas_call(
+        kernel,
+        grid_spec=pltpu.PrefetchScalarGridSpec(
+            num_scalar_prefetch=1,
+            grid=grid,
+            in_specs=in_specs,
+            out_specs=out_specs,
+            scratch_shapes=list(scratch),
+        ),
+        out_shape=out_shape,
+        cost_estimate=pl.CostEstimate(flops=flops, bytes_accessed=moved, transcendentals=exps),
+    )
+
+
+def struct(shape, dtype):
+    return jax.ShapeDtypeStruct(shape, dtype)
+
+
+def projection_kernel(c_ref, *refs):
+    chunks = refs[:8]
+    packed = refs[8:12]
+    wgt, g1, gq, gk, cosine, sine = refs[12:18]
+    x_out, xn_out, q_out, k_out, v_out, qr_out, kr_out, gate_out, weights = refs[18:27]
+    block = refs[27]
+    d = pl.program_id(0)
+
+    @pl.when(d == 0)
+    def _():
+        for e in range(4):
+            j = c_ref[1] ^ e
+            for start, size, first in ((0, 64, 0), (256, 32, 64), (384, 32, 96)):
+                at = pl.multiple_of(start + size * j, size)
+                weights[pl.ds(at, size)] = packed[e][first : first + size]
+
+    for i in range(8):
+
+        @pl.when(d == i)
+        def _():
+            block[...] = chunks[i][...]
+
+    x_out[...] = block[...]
+    x = block[...].astype(F32)
+    xn = (x * lax.rsqrt(jnp.mean(x * x, axis=-1, keepdims=True) + EPS) * g1[...]).astype(BF16)
+    xn_out[...] = xn
+    made = dot(xn, weights[...], LAST)
+    gate_out[...] = jax.nn.sigmoid(dot(xn, wgt[...], LAST))
+    q_out[...] = made[:, :256]
+    k_out[...] = made[:, 256:384]
+    v_out[...] = made[:, 384:].astype(BF16)
+
+    def turned(v, gain):
+        v = v * lax.rsqrt(jnp.mean(v * v, axis=-1, keepdims=True) + EPS) * gain
+        return (v * cosine[...] + pltpu.roll(v, HD // 2, 1) * sine[...]).astype(BF16)
+
+    qr_out[:, :HD] = turned(made[:, :HD], gq[...])
+    qr_out[:, HD:] = turned(made[:, HD : 2 * HD], gq[...])
+    kr_out[...] = turned(made[:, 2 * HD : 3 * HD], gk[...])
+
+
+def projection(c, chunks, packed, wgt, g1, gq, gk, cosine, sine):
+    rows, width = chunks[0].shape
+    length = 8 * rows
+    at = lambda d, c: (c[0] ^ d, 0)
+    return call(
+        projection_kernel,
+        (8,),
+        [full((rows, width), pipeline_mode=pl.Buffered(1))] * 8
+        + [
+            *[full((128, width), pipeline_mode=pl.Buffered(1))] * 4,
+            full(wgt.shape),
+            full((1, width)),
+            full((1, HD)),
+            full((1, HD)),
+            pl.BlockSpec((rows, HD), at),
+            pl.BlockSpec((rows, HD), at),
+        ],
+        [
+            *(pl.BlockSpec((rows, n), at) for n in (width, width, 2 * HD, HD, HD, 2 * HD, HD, 16)),
+            full((512, width)),
+        ],
+        [
+            struct((length, width), BF16),
+            struct((length, width), BF16),
+            struct((length, 2 * HD), F32),
+            struct((length, HD), F32),
+            struct((length, HD), BF16),
+            struct((length, 2 * HD), BF16),
+            struct((length, HD), BF16),
+            struct((length, 16), F32),
+            struct((512, width), BF16),
+        ],
+        2 * length * width * 528,
+        20 * length * width,
+        scratch=[pltpu.VMEM((rows, width), BF16)],
+    )(c, *chunks, *packed, wgt, g1, gq, gk, cosine, sine)
+
+
+def head_column(ref):
+    value = ref[...]
+    return jnp.where(pl.program_id(0) == 0, value[:, 0:1], value[:, 1:2])
+
+
+def attention_kernel(
+    c_ref, limit_ref, pos_ref, q_ref, k_ref, v_ref, gate_ref, out_ref, mixed_ref, lse_ref
+):
+    scores = dot(q_ref[...], k_ref[...], LAST) * (HD**-0.5)
+    scores = jnp.where(pos_ref[...] <= limit_ref[...], scores, NEG)
+    top = jnp.max(scores, axis=-1, keepdims=True)
+    weights = jnp.exp(scores - top)
+    total = jnp.sum(weights, axis=-1, keepdims=True)
+    probs = (weights * (1.0 / total)).astype(BF16)
+    attended = jnp.dot(probs, v_ref[...], preferred_element_type=F32)
+    out_ref[...] = attended
+    mixed_ref[...] = (attended * head_column(gate_ref)).astype(BF16)
+    lse_ref[0] = top + jnp.log(total)
+
+
+def attention(c, q, k, v, gates, limit, pos, tile=256):
+    length = q.shape[0]
+    return call(
+        attention_kernel,
+        (2, length // tile),
+        [
+            pl.BlockSpec((tile, 1), lambda h, i, c: (i, 0)),
+            full((1, length)),
+            pl.BlockSpec((tile, HD), lambda h, i, c: (i, h)),
+            full((length, HD)),
+            full((length, HD)),
+            pl.BlockSpec((tile, 16), lambda h, i, c: (i, 0)),
+        ],
+        [
+            pl.BlockSpec((tile, HD), lambda h, i, c: (i, h)),
+            pl.BlockSpec((tile, HD), lambda h, i, c: (i, h)),
+            pl.BlockSpec((1, tile, 1), lambda h, i, c: (h, i, 0)),
+        ],
+        [
+            struct((length, 2 * HD), F32),
+            struct((length, 2 * HD), BF16),
+            struct((2, length, 1), F32),
+        ],
+        8 * length * length * HD,
+        16 * length * HD,
+        2 * length * length,
+    )(c, limit, pos, q, k, v, gates)
+
+
+def hidden_kernel(c_ref, *refs):
+    mixed = refs[:8]
+    x, wo, g2 = refs[8:11]
+    xn_out, own_out = refs[11:13]
+    total = refs[13]
+    i = pl.program_id(0)
+    c = c_ref[0]
+    total[...] = x[...].astype(F32)
+    for d in range(8):
+        other = c ^ d
+        total[...] += jnp.dot(
+            mixed[d][...], wo[2 * (other & 3) + (other >> 2)], preferred_element_type=F32
+        )
+    h = total[...]
+    xn_out[...] = (
+        h * lax.rsqrt(jnp.mean(h * h, axis=-1, keepdims=True) + EPS) * g2[...]
+    ).astype(BF16)
+
+    @pl.when(i == c >> 1)
+    def _():
+        own_out[...] = total[pl.ds((c & 1) * 128, 128)]
+
+
+def hidden(c, mixed, x_all, wo, g2):
+    length, width = x_all.shape
+    return call(
+        hidden_kernel,
+        (4,),
+        [pl.BlockSpec((256, 256), lambda i, c: (i, 0))] * 8
+        + [
+            pl.BlockSpec((256, width), lambda i, c: (i, 0)),
+            full((8, 256, width), pipeline_mode=pl.Buffered(1)),
+            full((1, width)),
+        ],
+        [pl.BlockSpec((256, width), lambda i, c: (i, 0)), full((128, width))],
+        [struct((length, width), BF16), struct((128, width), F32)],
+        2 * length * width * width,
+        12 * length * width,
+        scratch=[pltpu.VMEM((256, width), F32)],
+    )(c, *mixed, x_all, wo.reshape(8, 256, width), g2)
+
+
+def join_kernel(c_ref, *refs):
+    for i in range(8):
+
+        @pl.when(pl.program_id(0) == i)
+        def _():
+            refs[8][...] = refs[i][...]
+
+
+def join(c, chunks):
+    rows, width = chunks[0].shape
+    return call(
+        join_kernel,
+        (8,),
+        [full((rows, width), pipeline_mode=pl.Buffered(1))] * 8,
+        pl.BlockSpec((rows, width), lambda d, c: (c[0] ^ d, 0)),
+        struct((8 * rows, width), chunks[0].dtype),
+        0,
+        32 * rows * width,
+    )(c, *chunks)
+
+
+def mixed_back_kernel(c_ref, *refs):
+    chunks = refs[:8]
+    wo, attended, gate_ref = refs[8:11]
+    all_out, att_out, logit_out = refs[11:]
+    for i in range(8):
+
+        @pl.when(pl.program_id(0) == i)
+        def _():
+            all_out[...] = chunks[i][...]
+
+    grad = dot(all_out[...], wo[0], LAST)
+    gates = gate_ref[...]
+    lane = lax.broadcasted_iota(jnp.int32, gates.shape, 1)
+    logits = jnp.zeros_like(gates)
+    for h in range(2):
+        part = grad[:, h * HD : (h + 1) * HD]
+        gate = gates[:, h : h + 1]
+        att_out[:, h * HD : (h + 1) * HD] = (part * gate).astype(BF16)
+        along = jnp.sum(part * attended[:, h * HD : (h + 1) * HD], axis=-1, keepdims=True)
+        logits = jnp.where(lane == h, along * gate * (1.0 - gate), logits)
+    logit_out[...] = logits.astype(BF16)
+
+
+def mixed_back(c, chunks, wo, attended, gates):
+    rows, width = chunks[0].shape
+    length = 8 * rows
+    at = lambda d, c: (c[0] ^ d, 0)
+    return call(
+        mixed_back_kernel,
+        (8,),
+        [full((rows, width), pipeline_mode=pl.Buffered(1))] * 8
+        + [
+            pl.BlockSpec((1, 256, width), lambda d, c: (2 * (c[0] & 3) + (c[0] >> 2), 0, 0)),
+            pl.BlockSpec((rows, 256), at),
+            pl.BlockSpec((rows, 16), at),
+        ],
+        [pl.BlockSpec((rows, n), at) for n in (width, 256, 16)],
+        [struct((length, n), BF16) for n in (width, 256, 16)],
+        512 * length * width,
+        6 * length * width,
+    )(c, *chunks, wo.reshape(8, 256, width), attended, gates)
+
+
+def attention_back_kernel(c_ref, *refs):
+    limit_ref, pos_ref, qr, kr, v, lse_ref, g, q_pre, k_pre, cosine, sine, cosine_all, sine_all = refs[:13]
+    gq, gk = refs[13:15]
+    gq_out, gk_out, gv_out, gains_out = refs[15:19]
+    gk_sum, gv_sum = refs[19:]
+    first = (pl.program_id(0) == 0) & (pl.program_id(1) == 0)
+    last = (pl.program_id(0) == 1) & (pl.program_id(1) == pl.num_programs(1) - 1)
+
+    def back(rotated, pre, gain, cos_ref, sin_ref):
+        grad = rotated.astype(BF16).astype(F32)
+        grad = grad * cos_ref[...] - pltpu.roll(grad, HD // 2, 1) * sin_ref[...]
+        scale = lax.rsqrt(jnp.mean(pre * pre, axis=-1, keepdims=True) + EPS)
+        weighted = grad * gain
+        out = scale * weighted - pre * (scale * scale * scale) * jnp.mean(
+            weighted * pre, axis=-1, keepdims=True
+        )
+        return out.astype(BF16), jnp.sum(grad * pre * scale, axis=0, keepdims=True)
+
+    @pl.when(first)
+    def _():
+        gk_sum[...] = jnp.zeros_like(gk_sum)
+        gv_sum[...] = jnp.zeros_like(gv_sum)
+        gains_out[...] = jnp.zeros_like(gains_out)
+
+    scores = dot(qr[...], kr[...], LAST) * (HD**-0.5)
+    scores = jnp.where(pos_ref[...] <= limit_ref[...], scores, NEG)
+    probs = jnp.exp(scores - lse_ref[0])
+    grad_probs = dot(g[...], v[...], LAST)
+    delta = jnp.sum(probs * grad_probs, axis=-1, keepdims=True)
+    grad_scores = (probs * (grad_probs - delta)).astype(BF16)
+    rotated = jnp.dot(grad_scores, kr[...], preferred_element_type=F32) * (HD**-0.5)
+    gk_sum[...] += dot(grad_scores, qr[...], ROWS)
+    gv_sum[...] += dot(probs.astype(BF16), g[...], ROWS)
+    gq_out[...], terms = back(rotated, q_pre[...], gq[...], cosine, sine)
+    gains_out[0:1] += terms
+
+    @pl.when(last)
+    def _():
+        gk_out[...], key_terms = back(
+            gk_sum[...] * (HD**-0.5), k_pre[...], gk[...], cosine_all, sine_all
+        )
+        gains_out[1:2] += key_terms
+        gv_out[...] = gv_sum[...].astype(BF16)
+
+
+def attention_back(c, qr, kr, v, lse, grad, q_pre, k_pre, cosine, sine, gq, gk, limit, pos, tile=256):
+    length = qr.shape[0]
+    mine = pl.BlockSpec((tile, HD), lambda h, i, c: (i, h))
+    rows = pl.BlockSpec((tile, HD), lambda h, i, c: (i, 0))
+    whole = full((length, HD))
+    return call(
+        attention_back_kernel,
+        (2, length // tile),
+        [
+            pl.BlockSpec((tile, 1), lambda h, i, c: (i, 0)),
+            full((1, length)),
+            mine,
+            whole,
+            whole,
+            pl.BlockSpec((1, tile, 1), lambda h, i, c: (h, i, 0)),
+            mine,
+            mine,
+            whole,
+            rows,
+            rows,
+            whole,
+            whole,
+            full((1, HD)),
+            full((1, HD)),
+        ],
+        [mine, whole, whole, full((8, HD))],
+        [
+            struct((length, 2 * HD), BF16),
+            struct((length, HD), BF16),
+            struct((length, HD), BF16),
+            struct((8, HD), F32),
+        ],
+        20 * length * length * HD,
+        40 * length * HD,
+        2 * length * length,
+        scratch=[pltpu.VMEM((length, HD), F32), pltpu.VMEM((length, HD), F32)],
+    )(c, limit, pos, qr, kr, v, lse, grad, q_pre, k_pre, cosine, sine, cosine, sine, gq, gk)
+
+
+def input_back_kernel(c_ref, *refs):
+    gq, gk, gv, logits, weights, wgt, xn, g1, gain2, heads = refs[:10]
+    outs = refs[10:18]
+    bundle, gate_sum = refs[18:]
+    d = pl.program_id(0)
+    mine = 2 * (c_ref[0] & 3) + (c_ref[0] >> 2)
+
+    @pl.when(d == 0)
+    def _():
+        bundle[...] = jnp.zeros_like(bundle)
+        gate_sum[...] = jnp.zeros_like(gate_sum)
+
+    part = jnp.dot(gq[...], weights[:256], preferred_element_type=F32)
+    part += jnp.dot(
+        jnp.concatenate([gk[...], gv[...]], axis=1), weights[256:], preferred_element_type=F32
+    )
+    part += jnp.dot(logits[...], wgt[...], preferred_element_type=F32)
+    bundle[16:17] += jnp.sum(part * xn[...].astype(F32), axis=0, keepdims=True)
+    gate_sum[...] += dot(logits[...], xn[...], ROWS)
+    for i in range(8):
+
+        @pl.when(d == i)
+        def _():
+            outs[i][...] = part.astype(BF16)
+
+    @pl.when(d == 7)
+    def _():
+        bundle[16:17] = bundle[16:17] / g1[...]
+        bundle[17:18] = gain2[...]
+        bundle[18:19, :HD] = heads[0:1]
+        bundle[18:19, HD : 2 * HD] = heads[1:2]
+        for g in range(8):
+
+            @pl.when(mine == g)
+            def _():
+                bundle[2 * g : 2 * g + 2] = gate_sum[0:2]
+
+
+def input_back(c, gq, gk, gv, logits, weights, wgt, xn, g1, gain2, heads):
+    length, width = xn.shape
+    rows = length // 8
+    at = lambda d, c: (c[0] ^ d, 0)
+    return call(
+        input_back_kernel,
+        (8,),
+        [pl.BlockSpec((rows, n), at) for n in (256, HD, HD, 16)]
+        + [
+            full(weights.shape, pipeline_mode=pl.Buffered(1)),
+            full(wgt.shape),
+            pl.BlockSpec((rows, width), at),
+            full((1, width)),
+            full((1, width)),
+            full((8, HD)),
+        ],
+        [full((rows, width))] * 8 + [full((24, width))],
+        [struct((rows, width), BF16)] * 8 + [struct((24, width), F32)],
+        1056 * length * width,
+        8 * length * width,
+        scratch=[pltpu.VMEM((16, width), F32)],
+    )(c, gq, gk, gv, logits, weights, wgt, xn, g1, gain2, heads)
+
+
+def per_device_small(*args):
+    return layer_small(*args)
+
+
+def layer_small(
+    tokens,
+    prefix,
+    span_order,
+    w_query,
+    w_key,
+    w_value,
+    w_out,
+    w_headgate,
+    attn_gain,
+    query_gain,
+    key_gain,
+    mlp_gain,
+    w_gate,
+    w_up,
+    w_down,
+    cotangent,
+):
+    rows, width = tokens.shape
+    length = 8 * rows
+    span = rows // 2
+    s = lax.axis_index("seq")
+    c = lax.axis_index("ctx")
+    flat = 8 * s + c
+    mine = 2 * (c & 3) + (c >> 2)
+    cs = jnp.stack([c, s]).astype(jnp.int32)
+
+    small = jnp.concatenate(
+        [
+            w_headgate,
+            attn_gain[None],
+            mlp_gain[None],
+            jnp.pad(jnp.concatenate([query_gain, key_gain]), (0, 56))[None],
+            jnp.zeros((13, 64), BF16),
+        ],
+        axis=0,
+    )
+    smalls = gather_small(small, flat)
+    wgt = smalls[:, :16].transpose(1, 0, 2).reshape(H, width)
+    wgt = lax.dynamic_slice_in_dim(jnp.concatenate([wgt, wgt], 0), 2 * mine, 16, 0)
+    g1 = smalls[:, 16].reshape(1, width).astype(F32)
+    g2 = smalls[:, 17].reshape(1, width).astype(F32)
+    gq = smalls[:, 18, :4].reshape(1, HD).astype(F32)
+    gk = smalls[:, 18, 4:8].reshape(1, HD).astype(F32)
+
+    x_chunks = gather_ctx(tokens)
+    local = jnp.concatenate([w_query, w_key, w_value], axis=0)
+    packed = [turn(local)]
+    packed.append(hop(packed[0], 8))
+    packed.append(hop(packed[0], 16))
+    packed.append(hop(packed[2], 8))
+    wo = lax.all_gather(w_out, BOTH, axis=0, tiled=True)
+    wd = lax.all_gather(w_down, "seq", axis=0, tiled=True)
+    wg = lax.all_gather(w_gate, "seq", axis=0, tiled=True)
+    wu = lax.all_gather(w_up, "seq", axis=0, tiled=True)
+
+    pos = (span_order[0][:, None] * span + jnp.arange(span, dtype=jnp.int32)).reshape(length)
+    limit = jnp.maximum(pos, prefix[0] - 1)
+    half = HD // 2
+    inv_freq = 1.0 / ROPE_BASE ** (jnp.arange(half, dtype=F32) * 2.0 / HD)
+    angles = pos.astype(F32)[:, None] * inv_freq[None, :]
+    cosine = jnp.cos(angles)
+    sine = jnp.sin(angles)
+    cosine = jnp.concatenate([cosine, cosine], axis=1)
+    sine = jnp.concatenate([-sine, sine], axis=1)
+    limit = limit[:, None]
+    pos = pos[None, :]
+
+    x_all, xn1, q_pre, k_pre, value, qr, kr, gates, w_qkv = projection(
+        cs, x_chunks, packed, wgt, g1, gq, gk, cosine, sine
+    )
+    cot_chunks = gather_ctx(after(cotangent, *x_chunks))
+    attended, mixed, lse = attention(cs, qr, kr, value, gates, limit, pos)
+    mixed_chunks = gather_ctx(mixed)
+    xn2_all, hidden1 = hidden(cs, mixed_chunks, x_all, wo, g2)
+    cot_all = join(cs, cot_chunks)
+
+    gate = project(xn2_all, wg)
+    up = project(xn2_all, wu)
+    grad_act = project(cot_all, wd)
+    sig = jax.nn.sigmoid(gate)
+    silu = gate * sig
+    act = (silu * up).astype(BF16)
+    grad_gate = (grad_act * up * sig * (1.0 + gate * (1.0 - sig))).astype(BF16)
+    grad_up = (grad_act * silu).astype(BF16)
+    grad_xn2_part = (
+        jnp.dot(grad_gate, wg, preferred_element_type=F32)
+        + jnp.dot(grad_up, wu, preferred_element_type=F32)
+    ).astype(BF16)
+    grad_xn2 = scatter_ctx(picked(grad_xn2_part, c))
+    ff_grads = [
+        outer(left, right).astype(BF16)
+        for left, right in ((grad_gate, xn2_all), (grad_up, xn2_all), (act, cot_all))
+    ]
+    grad_w_gate, grad_w_up, grad_w_down = (
+        lax.psum_scatter(v, "seq", scatter_dimension=0, tiled=True).astype(F32)
+        for v in ff_grads
+    )
+    branch_part = jnp.dot(act, wd, preferred_element_type=F32).astype(BF16)
+
+    _, scale2 = norm_apply(hidden1, g2)
+    grad_h1_norm, gain2_terms = norm_back(hidden1, scale2, g2, grad_xn2)
+    grad_hidden1 = cotangent.astype(F32) + grad_h1_norm
+    grad_gain2 = jnp.sum(gain2_terms, axis=0)
+    branch_chunks = gather_ctx(after(grad_hidden1.astype(BF16), *ff_grads, branch_part))
+    grad_branch_all, grad_att, grad_logits = mixed_back(cs, branch_chunks, wo, attended, gates)
+    branch = scatter_ctx(picked(after(branch_part, *branch_chunks), c))
+    output = (hidden1 + branch).astype(BF16)
+
+    gq_rows, gk_rows, gv_rows, head_gains = attention_back(
+        cs, qr, kr, value, lse, grad_att, q_pre, k_pre, cosine, sine, gq, gk, limit, pos
+    )
+    *parts, bundle = input_back(
+        cs, gq_rows, gk_rows, gv_rows, grad_logits, w_qkv, wgt, xn1, g1, grad_gain2[None], head_gains
+    )
+    grad_xn1 = scatter_ctx(parts)
+    x = tokens.astype(F32)
+    scale1 = lax.rsqrt(jnp.mean(x * x, axis=-1, keepdims=True) + EPS)
+    grad_x, _ = norm_back(x, scale1, g1, grad_xn1)
+    grad_tokens = grad_hidden1 + grad_x
+
+    pieces = jnp.concatenate(
+        [
+            outer(gq_rows, xn1).astype(BF16).reshape(4, 64, width),
+            outer(gk_rows, xn1).astype(BF16).reshape(4, 32, width),
+            outer(gv_rows, xn1).astype(BF16).reshape(4, 32, width),
+            outer(mixed, grad_branch_all).astype(BF16).reshape(4, 64, width),
+        ],
+        axis=1,
+    ).reshape(4 * 192, width)
+    home = lax.psum_scatter(pieces, "seq", scatter_dimension=0, tiled=True)
+    home = turn(home).astype(F32)
+    g_wq, g_wk, g_wv, g_wo = home[:64], home[64:96], home[96:128], home[128:]
+
+    bundle = sum_small(bundle)
+    blocks = lax.dynamic_slice_in_dim(bundle[:18], 64 * flat, 64, 1)
+    heads = lax.dynamic_slice_in_dim(bundle[18, : 2 * HD].reshape(2, HD), 4 * flat, 4, 1)
+    return (
+        output,
+        grad_tokens,
+        g_wq,
+        g_wk,
+        g_wv,
+        g_wo,
+        blocks[:16],
+        blocks[16],
+        heads[0],
+        heads[1],
+        blocks[17],
+        grad_w_gate,
+        grad_w_up,
+        grad_w_down,
+    )
+
+
 def solution(mesh):
     in_specs = (
         P(("seq", "ctx"), None),
@@ -363,6 +1015,8 @@
         P(("seq", "ctx"), None),
         P(("seq", "ctx"), None),
     )
+    sizes = dict(mesh.shape)
+    small = sizes == {"seq": 4, "ctx": 8}
     return jax.shard_map(
-        per_device, mesh=mesh, in_specs=in_specs, out_specs=out_specs, check_vma=False
-    )
+        per_device_small if small else per_device, mesh=mesh, in_specs=in_specs, out_specs=out_specs, check_vma=False
+    )

time: 2420 us -> 743 us (0.31)
  the two profiles are of different devices: /device:TPU:0 before, /device:TPU:22 now
where the time goes in v1:
time: 743 us; the launch traced here: 734 us
  waiting for transfers between devices  409 us (55%)
  starting transfers between devices  104 us (14%)
  Pallas kernels  88 us (12%)
  matrix products  62.8 us (8%)
  other arithmetic  34.1 us (5%)
  local copies, waits for them, and re-layouts  20.1 us (3%)
  between operations  16.1 us (2%)
    ppermute x41, waiting for transfers between devices, swap(): return lax.ppermute(v, 'ctx', [(c, c ^ d) for c in range(8)])  267 us
    ppermute x41, starting transfers between devices, swap(): return lax.ppermute(v, 'ctx', [(c, c ^ d) for c in range(8)])  55 us
    ppermute x4, waiting for transfers between devices, gather_ctx(): outer_far = lax.ppermute(relayed, 'ctx', outward)  46.4 us
    ppermute x4, waiting for transfers between devices, gather_ctx(): relayed = lax.ppermute(z1, 'ctx', inner)  40.8 us
    ppermute x13, waiting for transfers between devices, hop(): return lax.ppermute(v, BOTH, [(i, i ^ d) for i in range(32)])  38 us
    dot_general x3, matrix products, project(): lax.dot_general(left, right, (((1,), (1,)), ((), ())), preferred_element_...  24.8 us
    dot_general x7, matrix products, outer(): lax.dot_general(left, right, (((0,), (0,)), ((), ())), preferred_element_...  24.4 us
    pallas_call x1, Pallas kernels, hidden(): call(hidden_kernel, (4,), [pl.BlockSpec((256, 256), lambda i, c: (i, 0))]...  16.9 us
  transfers between devices with their start and end apart: 80, of which 44 were waited for; matrix products, arithmetic and copies ran while one was open for 9% of the time, Pallas kernels for 9%

profile of v1, /device:TPU:22, one launch (start us, length us, event | category | flops | bytes accessed | tf_op | source)
XLA Modules:
  0.0 734.2 jit_solution(2689196043287959550)
XLA Ops:
  31.8 7.3 collective-permute-done.14
  48.7 15.0 %collective-permute-done.3 = bf16[128,2048]{1,0:T(8,128)(2,1)S(1)} collective-permute-done((bf16[128,2048]{1,0:T(8,128)(2,1)}, bf16[128,2048]{1,0:T(8,128)(2,1)S(1)}, u32[]{:S(2)}, u32[]{:S(2)}) %collective-permute-start.3) | collective-permute-done | bytes 524320 | tf_op jit(solution)/shard_map/ppermute | solution.py:368
  66.2 24.9 %collective-permute-done.7 = bf16[128,2048]{1,0:T(8,128)(2,1)S(1)} collective-permute-done((bf16[128,2048]{1,0:T(8,128)(2,1)S(1)}, bf16[128,2048]{1,0:T(8,128)(2,1)S(1)}, u32[]{:S(2)}, u32[]{:S(2)}) %collective-permute-start.7) | collective-permute-done | bytes 524320 | tf_op jit(solution)/shard_map/ppermute | solution.py:371
  96.3 9.7 %collective-permute-done.6.refs_5_ = bf16[128,2048]{1,0:T(8,128)(2,1)} collective-permute-done((bf16[128,2048]{1,0:T(8,128)(2,1)S(1)}, bf16[128,2048]{1,0:T(8,128)(2,1)}, u32[]{:S(2)}, u32[]{:S(2)}) %collective-permute-start.6) | collective-permute-done | bytes 524320 | tf_op jit(solution)/shard_map/ppermute | solution.py:342
  106.0 9.9 %collective-permute-done.8.refs_7_ = bf16[128,2048]{1,0:T(8,128)(2,1)} collective-permute-done((bf16[128,2048]{1,0:T(8,128)(2,1)S(1)}, bf16[128,2048]{1,0:T(8,128)(2,1)}, u32[]{:S(2)}, u32[]{:S(2)}) %collective-permute-start.8) | collective-permute-done | bytes 524320 | tf_op jit(solution)/shard_map/ppermute | solution.py:342
  121.3 16.7 %shard_map.263 = (bf16[1024,2048]{1,0:T(8,128)(2,1)}, bf16[1024,2048]{1,0:T(8,128)(2,1)}, f32[1024,256]{1,0:T(8,128)}, f32[1024,128]{1,0:T(8,128)}, bf16[1024,12...) custom-call(s32[2]{0:T(128)} %pad_add_fusion.c_ref, ...), custom_call_target="tpu_custom_call" | custom-call | flops 2214592512 | bytes 41943040 | tf_op jit(solution)/shard_map/pallas_call | solution.py:489
  138.0 10.4 %shard_map.264 = (f32[1024,256]{1,0:T(8,128)}, bf16[1024,256]{1,0:T(8,128)(2,1)}, f32[2,1024,1]{2,1,0:T(8,128)}) custom-call(s32[2]{0:T(128)} %pad_add_fusion.c_ref, s32[1024,1]{1,0:T(8,128)} %max.19.limit_ref.refs_0_, s32[1,1024]{1,0:T(1,128)} %add.217.pos_ref.refs_1_, bf16[1024,256]{1,0:T(8,128)(2,1)} %get-tuple-element.53.q_ref.refs_2_, ...), custom_call_target="tpu_custom_call" | custom-call | flops 1073741824 | bytes 2097152 | tf_op jit(solution)/shard_map/pallas_call | solution.py:545
  167.1 9.5 %collective-permute-done.30 = bf16[128,2048]{1,0:T(8,128)(2,1)} collective-permute-done((bf16[128,2048]{1,0:T(8,128)(2,1)S(1)}, bf16[128,2048]{1,0:T(8,128)(2,1)}, u32[]{:S(2)}, u32[]{:S(2)}) %collective-permute-start.30) | collective-permute-done | bytes 524320 | tf_op jit(solution)/shard_map/ppermute | solution.py:368
  179.6 5.8 collective-permute-done.21
  188.6 6.1 collective-permute-done.34
  195.2 8.5 %collective-permute-done.25 = bf16[1024,256]{1,0:T(8,128)(2,1)S(1)} collective-permute-done((bf16[1024,256]{1,0:T(8,128)(2,1)S(1)}, bf16[1024,256]{1,0:T(8,128)(2,1)S(1)}, u32[]{:S(2)}, u32[]{:S(2)}) %collective-permute-start.25) | collective-permute-done | bytes 524320 | tf_op jit(solution)/shard_map/ppermute | solution.py:371
  208.4 5.2 collective-permute-done.33.refs_5_
  216.1 8.8 %collective-permute-done.35.refs_7_ = bf16[128,2048]{1,0:T(8,128)(2,1)} collective-permute-done((bf16[128,2048]{1,0:T(8,128)(2,1)S(1)}, bf16[128,2048]{1,0:T(8,128)(2,1)}, u32[]{:S(2)}, u32[]{:S(2)}) %collective-permute-start.35) | collective-permute-done | bytes 524320 | tf_op jit(solution)/shard_map/ppermute | solution.py:342
  225.0 7.0 shard_map.266
  236.1 11.2 %collective-permute-done.24.refs_5_ = bf16[1024,256]{1,0:T(8,128)(2,1)S(1)} collective-permute-done((bf16[1024,256]{1,0:T(8,128)(2,1)}, bf16[1024,256]{1,0:T(8,128)(2,1)S(1)}, u32[]{:S(2)}, u32[]{:S(2)}) %collective-permute-start.24) | collective-permute-done | bytes 524320 | tf_op jit(solution)/shard_map/ppermute | solution.py:342
  247.3 8.7 %collective-permute-done.26.refs_7_ = bf16[1024,256]{1,0:T(8,128)(2,1)} collective-permute-done((bf16[1024,256]{1,0:T(8,128)(2,1)}, bf16[1024,256]{1,0:T(8,128)(2,1)}, u32[]{:S(2)}, u32[]{:S(2)}) %collective-permute-start.26) | collective-permute-done | bytes 524320 | tf_op jit(solution)/shard_map/ppermute | solution.py:342
  256.0 16.9 %shard_map.265 = (bf16[1024,2048]{1,0:T(8,128)(2,1)}, f32[128,2048]{1,0:T(8,128)}) custom-call(s32[2]{0:T(128)} %pad_add_fusion.c_ref, bf16[1024,256]{1,0:T(8,128)(2,1)} %get-tuple-element.57.refs_0_, bf16[1024,256]{1,0:T(8,128)(2,1)} %collective-permute-done.18.refs_1_, bf16[1024,256]{1,0:T(8,128)(2,1)} %collective-permute-done.19.refs_2_, ...), custom_call_target="tpu_custom_call" | custom-call | flops 8589934592 | bytes 25165824 | tf_op jit(solution)/shard_map/pallas_call | solution.py:597
  272.9 6.2 fusion.35
  279.2 8.3 %fusion.36 = f32[1024,768]{1,0:T(8,128)} fusion(bf16[1024,2048]{1,0:T(8,128)(2,1)} %get-tuple-element.60, bf16[768,2048]{1,0:T(8,128)(2,1)} %all-gather.9.cloned.1.call-done), kind=kOutput, calls=%fused_computation.128 | convolution fusion | flops 3221225472 | bytes 10485760 | tf_op jit(solution)/shard_map/dot_general | solution.py:46
  287.5 10.2 %multiply_convert_fusion = (bf16[1024,768]{1,0:T(8,128)(2,1)S(1)}, bf16[1024,768]{1,0:T(8,128)(2,1)}, bf16[1024,768]{1,0:T(8,128)(2,1)}) fusion(f32[1024,768]{1,0:T(8,128)S(1)} %fusion.35, f32[1024,768]{1,0:T(8,128)} %fusion.36, bf16[1024,2048]{1,0:T(8,128)(2,1)} %shard_map.266, bf16[768,2048]{1,0:T(8,128)(2,1)} %all-gather.11.cloned.1.call-done), kind=kOutput, calls=%fused_computation.6 | convolution fusion | flops 3233021952 | bytes 18350080 | tf_op jit(solution)/shard_map/dot_general | solution.py:46
  298.9 5.0 convolution_convert_fusion.2
  303.9 8.0 %convolution_convert_fusion.3 = bf16[768,2048]{1,0:T(8,128)(2,1)} fusion(bf16[1024,768]{1,0:T(8,128)(2,1)} %get-tuple-element.104, bf16[1024,2048]{1,0:T(8,128)(2,1)} %get-tuple-element.60), kind=kOutput, calls=%fused_computation.4 | convolution fusion | flops 3222798336 | bytes 8912896 | tf_op jit(solution)/shard_map/dot_general | solution.py:52
  311.9 5.0 fusion.37
  333.2 5.9 collective-permute-done.38
  340.3 10.0 %collective-permute-done.37 = bf16[128,2048]{1,0:T(8,128)(2,1)S(1)} collective-permute-done((bf16[128,2048]{1,0:T(8,128)(2,1)}, bf16[128,2048]{1,0:T(8,128)(2,1)S(1)}, u32[]{:S(2)}, u32[]{:S(2)}) %collective-permute-start.37) | collective-permute-done | bytes 524320 | tf_op jit(solution)/shard_map/ppermute | solution.py:342
  351.5 19.1 %collective-permute-done.41 = bf16[128,2048]{1,0:T(8,128)(2,1)S(1)} collective-permute-done((bf16[128,2048]{1,0:T(8,128)(2,1)S(1)}, bf16[128,2048]{1,0:T(8,128)(2,1)S(1)}, u32[]{:S(2)}, u32[]{:S(2)}) %collective-permute-start.41) | collective-permute-done | bytes 524320 | tf_op jit(solution)/shard_map/ppermute | solution.py:342
  373.4 5.0 convolution_convert_fusion
  378.7 13.2 %collective-permute-done.42 = bf16[128,2048]{1,0:T(8,128)(2,1)S(1)} collective-permute-done((bf16[128,2048]{1,0:T(8,128)(2,1)S(1)}, bf16[128,2048]{1,0:T(8,128)(2,1)S(1)}, u32[]{:S(2)}, u32[]{:S(2)}) %collective-permute-start.42) | collective-permute-done | bytes 524320 | tf_op jit(solution)/shard_map/ppermute | solution.py:342
  399.1 10.0 %collective-permute-done.44.refs_2_ = bf16[128,2048]{1,0:T(8,128)(2,1)S(1)} collective-permute-done((bf16[128,2048]{1,0:T(8,128)(2,1)S(1)}, bf16[128,2048]{1,0:T(8,128)(2,1)S(1)}, u32[]{:S(2)}, u32[]{:S(2)}) %collective-permute-start.44) | collective-permute-done | bytes 524320 | tf_op jit(solution)/shard_map/ppermute | solution.py:342
  413.7 10.5 %collective-permute-done.46 = bf16[128,2048]{1,0:T(8,128)(2,1)S(1)} collective-permute-done((bf16[128,2048]{1,0:T(8,128)(2,1)S(1)}, bf16[128,2048]{1,0:T(8,128)(2,1)S(1)}, u32[]{:S(2)}, u32[]{:S(2)}) %collective-permute-start.46) | collective-permute-done | bytes 524320 | tf_op jit(solution)/shard_map/ppermute | solution.py:368
  428.8 6.9 collective-permute-done.50
  440.4 11.2 %collective-permute-done.45.refs_3_ = bf16[128,2048]{1,0:T(8,128)(2,1)S(1)} collective-permute-done((bf16[128,2048]{1,0:T(8,128)(2,1)S(1)}, bf16[128,2048]{1,0:T(8,128)(2,1)S(1)}, u32[]{:S(2)}, u32[]{:S(2)}) %collective-permute-start.45) | collective-permute-done | bytes 524320 | tf_op jit(solution)/shard_map/ppermute | solution.py:342
  451.6 11.2 %collective-permute-done.49.refs_5_ = bf16[128,2048]{1,0:T(8,128)(2,1)S(1)} collective-permute-done((bf16[128,2048]{1,0:T(8,128)(2,1)S(1)}, bf16[128,2048]{1,0:T(8,128)(2,1)S(1)}, u32[]{:S(2)}, u32[]{:S(2)}) %collective-permute-start.49) | collective-permute-done | bytes 524320 | tf_op jit(solution)/shard_map/ppermute | solution.py:342
  462.9 8.8 %collective-permute-done.51.refs_7_ = bf16[128,2048]{1,0:T(8,128)(2,1)S(1)} collective-permute-done((bf16[128,2048]{1,0:T(8,128)(2,1)S(1)}, bf16[128,2048]{1,0:T(8,128)(2,1)S(1)}, u32[]{:S(2)}, u32[]{:S(2)}) %collective-permute-start.51) | collective-permute-done | bytes 524320 | tf_op jit(solution)/shard_map/ppermute | solution.py:342
  472.6 10.8 %shard_map.267 = (bf16[1024,2048]{1,0:T(8,128)(2,1)}, bf16[1024,256]{1,0:T(8,128)(2,1)}, bf16[1024,16]{1,0:T(8,128)(2,1)}) custom-call(s32[2]{0:T(128)} %pad_add_fusion.c_ref, bf16[128,2048]{1,0:T(8,128)(2,1)} %copy-done.7, bf16[128,2048]{1,0:T(8,128)(2,1)} %copy-done.24, bf16[128,2048]{1,0:T(8,128)(2,1)} %copy-done.23, bf16[128,2048]{1,0:T(8,128)(2,1)} %copy-done.25, ...), custom_call_target="tpu_custom_call" | custom-call | flops 1073741824 | bytes 12582912 | tf_op jit(solution)/shard_map/pallas_call | solution.py:662
  483.4 14.0 %shard_map.268 = (bf16[1024,256]{1,0:T(8,128)(2,1)}, bf16[1024,128]{1,0:T(8,128)(2,1)}, bf16[1024,128]{1,0:T(8,128)(2,1)}, f32[8,128]{1,0:T(8,128)}) custom-call(s32[2]{0:T(128)} %pad_add_fusion.c_ref, s32[1024,1]{1,0:T(8,128)} %max.19.limit_ref.refs_0_, s32[1,1024]{1,0:T(1,128)} %add.217.pos_ref.refs_1_, bf16[1024,256]{1,0:T(8,128)(2,1)} %get-tuple-element.53.q_ref.refs_2_, ...), custom_call_target="tpu_custom_call" | custom-call | flops 2684354560 | bytes 5242880 | tf_op jit(solution)/shard_map/pallas_call | solution.py:728
  509.5 12.3 %shard_map.269 = (bf16[128,2048]{1,0:T(8,128)(2,1)}, bf16[128,2048]{1,0:T(8,128)(2,1)}, bf16[128,2048]{1,0:T(8,128)(2,1)}, bf16[128,2048]{1,0:T(8,128)(2,1)}, bf...) custom-call(s32[2]{0:T(128)} %pad_add_fusion.c_ref, ...), custom_call_target="tpu_custom_call" | custom-call | flops 2214592512 | bytes 16777216 | tf_op jit(solution)/shard_map/pallas_call | solution.py:804
  527.0 14.1 %collective-permute-done.67 = f32[24,2048]{1,0:T(8,128)S(1)} collective-permute-done((f32[24,2048]{1,0:T(8,128)}, f32[24,2048]{1,0:T(8,128)S(1)}, u32[]{:S(2)}, u32[]{:S(2)}) %collective-permute-start.67) | collective-permute-done | bytes 196640 | tf_op jit(solution)/shard_map/ppermute | solution.py:346
  552.5 6.4 collective-permute-done.69
  559.9 26.1 %collective-permute-done.54 = bf16[128,2048]{1,0:T(8,128)(2,1)S(1)} collective-permute-done((bf16[128,2048]{1,0:T(8,128)(2,1)S(1)}, bf16[128,2048]{1,0:T(8,128)(2,1)S(1)}, u32[]{:S(2)}, u32[]{:S(2)}) %collective-permute-start.54) | collective-permute-done | bytes 524320 | tf_op jit(solution)/shard_map/ppermute | solution.py:342
  586.2 11.1 %collective-permute-done.53 = bf16[128,2048]{1,0:T(8,128)(2,1)S(1)} collective-permute-done((bf16[128,2048]{1,0:T(8,128)(2,1)S(1)}, bf16[128,2048]{1,0:T(8,128)(2,1)S(1)}, u32[]{:S(2)}, u32[]{:S(2)}) %collective-permute-start.53) | collective-permute-done | bytes 524320 | tf_op jit(solution)/shard_map/ppermute | solution.py:342
  597.5 5.5 collective-permute-done.71
  607.3 19.5 %collective-permute-done.64 = bf16[128,2048]{1,0:T(8,128)(2,1)S(1)} collective-permute-done((bf16[128,2048]{1,0:T(8,128)(2,1)S(1)}, bf16[128,2048]{1,0:T(8,128)(2,1)S(1)}, u32[]{:S(2)}, u32[]{:S(2)}) %collective-permute-start.64) | collective-permute-done | bytes 524320 | tf_op jit(solution)/shard_map/ppermute | solution.py:342
  631.5 17.8 %collective-permute-done.57 = bf16[128,2048]{1,0:T(8,128)(2,1)S(1)} collective-permute-done((bf16[128,2048]{1,0:T(8,128)(2,1)S(1)}, bf16[128,2048]{1,0:T(8,128)(2,1)S(1)}, u32[]{:S(2)}, u32[]{:S(2)}) %collective-permute-start.57) | collective-permute-done | bytes 524320 | tf_op jit(solution)/shard_map/ppermute | solution.py:342
  652.6 10.9 %collective-permute-start.65 = (bf16[128,2048]{1,0:T(8,128)(2,1)S(1)}, bf16[128,2048]{1,0:T(8,128)(2,1)S(1)}, u32[]{:S(2)}, u32[]{:S(2)}) collective-permute-start(bf16[128,2048]{1,0:T(8,128)(2,1)S(1)} %add_convert_fusion.1), channel_id=1, source_target_pairs={{0,2},{1,3},{2,0},{3,1},{4,6},{5,7},{6,4},{7,5},{8,10},{9,11},{10,... | collective-permute-start | bytes 1572872 | tf_op jit(solution)/shard_map/ppermute | solution.py:342
  667.7 25.3 %collective-permute-done.65 = bf16[128,2048]{1,0:T(8,128)(2,1)S(1)} collective-permute-done((bf16[128,2048]{1,0:T(8,128)(2,1)S(1)}, bf16[128,2048]{1,0:T(8,128)(2,1)S(1)}, u32[]{:S(2)}, u32[]{:S(2)}) %collective-permute-start.65) | collective-permute-done | bytes 524320 | tf_op jit(solution)/shard_map/ppermute | solution.py:342
  693.8 6.6 collective-permute-done.58
  713.8 11.4 %collective-permute-done.66 = bf16[192,2048]{1,0:T(8,128)(2,1)S(1)} collective-permute-done((bf16[192,2048]{1,0:T(8,128)(2,1)}, bf16[192,2048]{1,0:T(8,128)(2,1)S(1)}, u32[]{:S(2)}, u32[]{:S(2)}) %collective-permute-start.66) | collective-permute-done | bytes 786464 | tf_op jit(solution)/shard_map/ppermute | solution.py:353
  (319 shorter events, 190.4 us)
Async XLA Ops:
  7.2 248.8 %all-gather.5.cloned.1.call-start = ((), (), s32[]{:S(2)}) async-start(), calls=%async_computation.4 | async-start | bytes 8650752 | tf_op jit(solution)/shard_map/all_gather | solution.py:879
  7.9 265.0 %all-gather.7.cloned.1.call-start = ((), (), s32[]{:S(2)}) async-start(), calls=%async_computation.5 | async-start | bytes 3932160 | tf_op jit(solution)/shard_map/all_gather | solution.py:881
  8.7 270.5 %all-gather.9.cloned.1.call-start = ((), (), s32[]{:S(2)}) async-start(), calls=%async_computation.6 | async-start | bytes 3932160 | tf_op jit(solution)/shard_map/all_gather | solution.py:882
  8.7 31.0 %collective-permute-start.1 = (bf16[128,2048]{1,0:T(8,128)(2,1)}, bf16[128,2048]{1,0:T(8,128)(2,1)}, u32[]{:S(2)}, u32[]{:S(2)}) collective-permute-start(bf16[128,2048]{1,0:T(8,128)(2,1)} %refs_0_.1), channel_id=1, source_target_pairs={{0,2},{1,3},{2,0},{3,1},{4,6},{5,7},{6,4},{7,5},{8,10},{9,11},{10,... | collective-permute-start | bytes 1572872 | tf_op jit(solution)/shard_map/ppermute | solution.py:342
  10.4 33.5 %collective-permute-start.4 = (bf16[128,2048]{1,0:T(8,128)(2,1)}, bf16[128,2048]{1,0:T(8,128)(2,1)S(1)}, u32[]{:S(2)}, u32[]{:S(2)}) collective-permute-start(bf16[128,2048]{1,0:T(8,128)(2,1)} %refs_0_.1), channel_id=1, source_target_pairs={{2,4},{3,5},{4,2},{5,3},{10,12},{11,13},{12,10},{13,11},{18,20},{1... | collective-permute-start | bytes 1572872 | tf_op jit(solution)/shard_map/ppermute | solution.py:366
  12.3 81.1 %collective-permute-start = (bf16[128,2048]{1,0:T(8,128)(2,1)}, bf16[128,2048]{1,0:T(8,128)(2,1)}, u32[]{:S(2)}, u32[]{:S(2)}) collective-permute-start(bf16[128,2048]{1,0:T(8,128)(2,1)} %refs_0_.1), channel_id=1, source_target_pairs={{0,1},{1,0},{2,3},{3,2},{4,5},{5,4},{6,7},{7,6},{8,9},{9,8},{10,11... | collective-permute-start | bytes 1572872 | tf_op jit(solution)/shard_map/ppermute | solution.py:342
  16.3 48.8 %collective-permute-start.9 = (bf16[128,2048]{1,0:T(8,128)(2,1)S(1)}, bf16[128,2048]{1,0:T(8,128)(2,1)}, u32[]{:S(2)}, u32[]{:S(2)}) collective-permute-start(bf16[128,2048]{1,0:T(8,128)(2,1)S(1)} %pad_maximum_fusion.1), channel_id=1, source_target_pairs={{0,0},{1,8},{2,16},{3,24},{4,4},{5,12},{6,20},{7,28},{8,1},{9,9},{... | collective-permute-start | bytes 1572872 | tf_op jit(solution)/shard_map/ppermute | solution.py:353
  20.9 266.5 %all-gather.11.cloned.1.call-start = ((), (), s32[]{:S(2)}) async-start(), calls=%async_computation.7 | async-start | bytes 3932160 | tf_op jit(solution)/shard_map/all_gather | solution.py:880
  48.6 43.0 %collective-permute-start.17 = (bf16[2,2,2,2,32,64]{5,4,1,2,3,0:T(8,128)(2,1)S(1)}, bf16[2,2,2,2,32,64]{5,4,1,2,3,0:T(8,128)(2,1)S(1)}, u32[]{:S(2)}, u32[]{:S(2)}) collective-permute-start(bf16[2,2,2,2,32,64]{5,4,1,2,3,0:T(8,128)(2,1)S(1)} %maximum_select_fusion.1), channel_id=1, source_target_pairs={{0,16},{1,17},{2,18},{3,19},{4,20},{5,21},{6,22},{7,23},{8,24},{9,... | collective-permute-start | bytes 196616 | tf_op jit(solution)/shard_map/ppermute | solution.py:346
  63.7 27.4 %collective-permute-start.7 = (bf16[128,2048]{1,0:T(8,128)(2,1)S(1)}, bf16[128,2048]{1,0:T(8,128)(2,1)S(1)}, u32[]{:S(2)}, u32[]{:S(2)}) collective-permute-start(bf16[128,2048]{1,0:T(8,128)(2,1)S(1)} %collective-permute-done.3), channel_id=1, source_target_pairs={{2,0},{3,1},{4,6},{5,7},{10,8},{11,9},{12,14},{13,15},{18,16},{19,... | collective-permute-start | bytes 1572872 | tf_op jit(solution)/shard_map/ppermute | solution.py:371
  65.1 31.2 %collective-permute-start.2 = (bf16[128,2048]{1,0:T(8,128)(2,1)}, bf16[128,2048]{1,0:T(8,128)(2,1)}, u32[]{:S(2)}, u32[]{:S(2)}) collective-permute-start(bf16[128,2048]{1,0:T(8,128)(2,1)} %collective-permute-done.1.refs_2_), channel_id=1, source_target_pairs={{0,1},{1,0},{2,3},{3,2},{4,5},{5,4},{6,7},{7,6},{8,9},{9,8},{10,11... | collective-permute-start | bytes 1572872 | tf_op jit(solution)/shard_map/ppermute | solution.py:342
  66.1 27.3 %collective-permute-start.11 = (bf16[128,2048]{1,0:T(8,128)(2,1)}, bf16[128,2048]{1,0:T(8,128)(2,1)}, u32[]{:S(2)}, u32[]{:S(2)}) collective-permute-start(bf16[128,2048]{1,0:T(8,128)(2,1)} %collective-permute-done.9.refs_8_), channel_id=1, source_target_pairs={{0,16},{1,17},{2,18},{3,19},{4,20},{5,21},{6,22},{7,23},{8,24},{9,... | collective-permute-start | bytes 1572872 | tf_op jit(solution)/shard_map/ppermute | solution.py:346
  93.4 27.9 %collective-permute-start.10 = (bf16[128,2048]{1,0:T(8,128)(2,1)}, bf16[128,2048]{1,0:T(8,128)(2,1)}, u32[]{:S(2)}, u32[]{:S(2)}) collective-permute-start(bf16[128,2048]{1,0:T(8,128)(2,1)} %collective-permute-done.9.refs_8_), channel_id=1, source_target_pairs={{0,8},{1,9},{2,10},{3,11},{4,12},{5,13},{6,14},{7,15},{8,0},{9,1},... | collective-permute-start | bytes 1572872 | tf_op jit(solution)/shard_map/ppermute | solution.py:346
  93.5 27.8 %collective-permute-start.12 = (bf16[128,2048]{1,0:T(8,128)(2,1)}, bf16[128,2048]{1,0:T(8,128)(2,1)}, u32[]{:S(2)}, u32[]{:S(2)}) collective-permute-start(bf16[128,2048]{1,0:T(8,128)(2,1)} %collective-permute-done.11.refs_10_), channel_id=1, source_target_pairs={{0,8},{1,9},{2,10},{3,11},{4,12},{5,13},{6,14},{7,15},{8,0},{9,1},... | collective-permute-start | bytes 1572872 | tf_op jit(solution)/shard_map/ppermute | solution.py:346
  115.9 36.3 %collective-permute-start.28 = (bf16[128,2048]{1,0:T(8,128)(2,1)S(1)}, bf16[128,2048]{1,0:T(8,128)(2,1)S(1)}, u32[]{:S(2)}, u32[]{:S(2)}) collective-permute-start(bf16[128,2048]{1,0:T(8,128)(2,1)S(1)} %copy-done.5), channel_id=1, source_target_pairs={{0,2},{1,3},{2,0},{3,1},{4,6},{5,7},{6,4},{7,5},{8,10},{9,11},{10,... | collective-permute-start | bytes 1572872 | tf_op jit(solution)/shard_map/ppermute | solution.py:342
  118.6 35.6 %collective-permute-start.31 = (bf16[128,2048]{1,0:T(8,128)(2,1)S(1)}, bf16[128,2048]{1,0:T(8,128)(2,1)S(1)}, u32[]{:S(2)}, u32[]{:S(2)}) collective-permute-start(bf16[128,2048]{1,0:T(8,128)(2,1)S(1)} %copy-done.5), channel_id=1, source_target_pairs={{2,4},{3,5},{4,2},{5,3},{10,12},{11,13},{12,10},{13,11},{18,20},{1... | collective-permute-start | bytes 1572872 | tf_op jit(solution)/shard_map/ppermute | solution.py:366
  152.2 24.4 %collective-permute-start.30 = (bf16[128,2048]{1,0:T(8,128)(2,1)S(1)}, bf16[128,2048]{1,0:T(8,128)(2,1)}, u32[]{:S(2)}, u32[]{:S(2)}) collective-permute-start(bf16[128,2048]{1,0:T(8,128)(2,1)S(1)} %collective-permute-done.28.refs_2_), channel_id=1, source_target_pairs={{2,4},{3,5},{4,2},{5,3},{10,12},{11,13},{12,10},{13,11},{18,20},{1... | collective-permute-start | bytes 1572872 | tf_op jit(solution)/shard_map/ppermute | solution.py:368
  156.4 545.2 %reduce-scatter.5.cloned.1.call-start = ((), (), s32[]{:S(2)}) async-start(), calls=%async_computation.8 | async-start | bytes 3932160 | tf_op jit(solution)/shard_map/reduce_scatter | solution.py:958
  166.6 39.8 %collective-permute-start.27 = (bf16[128,2048]{1,0:T(8,128)(2,1)S(1)}, bf16[128,2048]{1,0:T(8,128)(2,1)S(1)}, u32[]{:S(2)}, u32[]{:S(2)}) collective-permute-start(bf16[128,2048]{1,0:T(8,128)(2,1)S(1)} %copy-done.5), channel_id=1, source_target_pairs={{0,1},{1,0},{2,3},{3,2},{4,5},{5,4},{6,7},{7,6},{8,9},{9,8},{10,11... | collective-permute-start | bytes 1572872 | tf_op jit(solution)/shard_map/ppermute | solution.py:342
  176.6 55.4 %collective-permute-start.18 = (bf16[1024,256]{1,0:T(8,128)(2,1)}, bf16[1024,256]{1,0:T(8,128)(2,1)}, u32[]{:S(2)}, u32[]{:S(2)}) collective-permute-start(bf16[1024,256]{1,0:T(8,128)(2,1)} %get-tuple-element.57.refs_0_), channel_id=1, source_target_pairs={{0,1},{1,0},{2,3},{3,2},{4,5},{5,4},{6,7},{7,6},{8,9},{9,8},{10,11... | collective-permute-start | bytes 1572872 | tf_op jit(solution)/shard_map/ppermute | solution.py:342
  206.3 29.7 %collective-permute-start.20 = (bf16[1024,256]{1,0:T(8,128)(2,1)}, bf16[1024,256]{1,0:T(8,128)(2,1)S(1)}, u32[]{:S(2)}, u32[]{:S(2)}) collective-permute-start(bf16[1024,256]{1,0:T(8,128)(2,1)} %collective-permute-done.19.refs_2_), channel_id=1, source_target_pairs={{0,1},{1,0},{2,3},{3,2},{4,5},{5,4},{6,7},{7,6},{8,9},{9,8},{10,11... | collective-permute-start | bytes 1572872 | tf_op jit(solution)/shard_map/ppermute | solution.py:342
  207.7 39.6 %collective-permute-start.24 = (bf16[1024,256]{1,0:T(8,128)(2,1)}, bf16[1024,256]{1,0:T(8,128)(2,1)S(1)}, u32[]{:S(2)}, u32[]{:S(2)}) collective-permute-start(bf16[1024,256]{1,0:T(8,128)(2,1)} %broadcast_select_fusion.1.refs_4_), channel_id=1, source_target_pairs={{0,1},{1,0},{2,3},{3,2},{4,5},{5,4},{6,7},{7,6},{8,9},{9,8},{10,11... | collective-permute-start | bytes 1572872 | tf_op jit(solution)/shard_map/ppermute | solution.py:342
  214.4 41.6 %collective-permute-start.26 = (bf16[1024,256]{1,0:T(8,128)(2,1)}, bf16[1024,256]{1,0:T(8,128)(2,1)}, u32[]{:S(2)}, u32[]{:S(2)}) collective-permute-start(bf16[1024,256]{1,0:T(8,128)(2,1)} %broadcast_select_fusion.refs_6_), channel_id=1, source_target_pairs={{0,1},{1,0},{2,3},{3,2},{4,5},{5,4},{6,7},{7,6},{8,9},{9,8},{10,11... | collective-permute-start | bytes 1572872 | tf_op jit(solution)/shard_map/ppermute | solution.py:342
  325.0 25.3 %collective-permute-start.37 = (bf16[128,2048]{1,0:T(8,128)(2,1)}, bf16[128,2048]{1,0:T(8,128)(2,1)S(1)}, u32[]{:S(2)}, u32[]{:S(2)}) collective-permute-start(bf16[128,2048]{1,0:T(8,128)(2,1)} %get-tuple-element.113), channel_id=1, source_target_pairs={{0,1},{1,0},{2,3},{3,2},{4,5},{5,4},{6,7},{7,6},{8,9},{9,8},{10,11... | collective-permute-start | bytes 1572872 | tf_op jit(solution)/shard_map/ppermute | solution.py:342
  326.1 44.6 %collective-permute-start.40 = (bf16[128,2048]{1,0:T(8,128)(2,1)}, bf16[128,2048]{1,0:T(8,128)(2,1)S(1)}, u32[]{:S(2)}, u32[]{:S(2)}) collective-permute-start(bf16[128,2048]{1,0:T(8,128)(2,1)} %get-tuple-element.111), channel_id=1, source_target_pairs={{0,1},{1,0},{2,3},{3,2},{4,5},{5,4},{6,7},{7,6},{8,9},{9,8},{10,11... | collective-permute-start | bytes 1572872 | tf_op jit(solution)/shard_map/ppermute | solution.py:342
  327.0 51.4 %collective-permute-start.36 = (bf16[128,2048]{1,0:T(8,128)(2,1)}, bf16[128,2048]{1,0:T(8,128)(2,1)S(1)}, u32[]{:S(2)}, u32[]{:S(2)}) collective-permute-start(bf16[128,2048]{1,0:T(8,128)(2,1)} %get-tuple-element.110), channel_id=1, source_target_pairs={{0,1},{1,0},{2,3},{3,2},{4,5},{5,4},{6,7},{7,6},{8,9},{9,8},{10,11... | collective-permute-start | bytes 1572872 | tf_op jit(solution)/shard_map/ppermute | solution.py:342
  340.2 30.4 %collective-permute-start.41 = (bf16[128,2048]{1,0:T(8,128)(2,1)S(1)}, bf16[128,2048]{1,0:T(8,128)(2,1)S(1)}, u32[]{:S(2)}, u32[]{:S(2)}) collective-permute-start(bf16[128,2048]{1,0:T(8,128)(2,1)S(1)} %fusion.16), channel_id=1, source_target_pairs={{0,4},{1,5},{2,6},{3,7},{4,0},{5,1},{6,2},{7,3},{8,12},{9,13},{10,... | collective-permute-start | bytes 1572872 | tf_op jit(solution)/shard_map/ppermute | solution.py:342
  351.5 27.2 %collective-permute-start.39 = (bf16[128,2048]{1,0:T(8,128)(2,1)S(1)}, bf16[128,2048]{1,0:T(8,128)(2,1)S(1)}, u32[]{:S(2)}, u32[]{:S(2)}) collective-permute-start(bf16[128,2048]{1,0:T(8,128)(2,1)S(1)} %fusion.17), channel_id=1, source_target_pairs={{0,4},{1,5},{2,6},{3,7},{4,0},{5,1},{6,2},{7,3},{8,12},{9,13},{10,... | collective-permute-start | bytes 1572872 | tf_op jit(solution)/shard_map/ppermute | solution.py:342
  426.6 25.0 %collective-permute-start.45 = (bf16[128,2048]{1,0:T(8,128)(2,1)S(1)}, bf16[128,2048]{1,0:T(8,128)(2,1)S(1)}, u32[]{:S(2)}, u32[]{:S(2)}) collective-permute-start(bf16[128,2048]{1,0:T(8,128)(2,1)S(1)} %collective-permute-done.44.refs_2_), channel_id=1, source_target_pairs={{0,1},{1,0},{2,3},{3,2},{4,5},{5,4},{6,7},{7,6},{8,9},{9,8},{10,11... | collective-permute-start | bytes 1572872 | tf_op jit(solution)/shard_map/ppermute | solution.py:342
  427.7 35.2 %collective-permute-start.49 = (bf16[128,2048]{1,0:T(8,128)(2,1)S(1)}, bf16[128,2048]{1,0:T(8,128)(2,1)S(1)}, u32[]{:S(2)}, u32[]{:S(2)}) collective-permute-start(bf16[128,2048]{1,0:T(8,128)(2,1)S(1)} %broadcast_select_fusion.3.refs_4_), channel_id=1, source_target_pairs={{0,1},{1,0},{2,3},{3,2},{4,5},{5,4},{6,7},{7,6},{8,9},{9,8},{10,11... | collective-permute-start | bytes 1572872 | tf_op jit(solution)/shard_map/ppermute | solution.py:342
  435.8 36.0 %collective-permute-start.51 = (bf16[128,2048]{1,0:T(8,128)(2,1)S(1)}, bf16[128,2048]{1,0:T(8,128)(2,1)S(1)}, u32[]{:S(2)}, u32[]{:S(2)}) collective-permute-start(bf16[128,2048]{1,0:T(8,128)(2,1)S(1)} %broadcast_select_fusion.2.refs_6_), channel_id=1, source_target_pairs={{0,1},{1,0},{2,3},{3,2},{4,5},{5,4},{6,7},{7,6},{8,9},{9,8},{10,11... | collective-permute-start | bytes 1572872 | tf_op jit(solution)/shard_map/ppermute | solution.py:342
  507.4 199.0 %reduce-scatter.11.cloned.1.call-start = ((), (), s32[]{:S(2)}) async-start(), calls=%async_computation.11 | async-start | bytes 3932160 | tf_op jit(solution)/shard_map/reduce_scatter | solution.py:923
  508.0 200.9 %reduce-scatter.9.cloned.1.call-start = ((), (), s32[]{:S(2)}) async-start(), calls=%async_computation.10 | async-start | bytes 3932160 | tf_op jit(solution)/shard_map/reduce_scatter | solution.py:923
  508.8 202.6 %reduce-scatter.7.cloned.1.call-start = ((), (), s32[]{:S(2)}) async-start(), calls=%async_computation.9 | async-start | bytes 3932160 | tf_op jit(solution)/shard_map/reduce_scatter | solution.py:923
  521.8 27.0 %collective-permute-start.61 = (bf16[128,2048]{1,0:T(8,128)(2,1)}, bf16[128,2048]{1,0:T(8,128)(2,1)S(1)}, u32[]{:S(2)}, u32[]{:S(2)}) collective-permute-start(bf16[128,2048]{1,0:T(8,128)(2,1)} %get-tuple-element.85), channel_id=1, source_target_pairs={{0,1},{1,0},{2,3},{3,2},{4,5},{5,4},{6,7},{7,6},{8,9},{9,8},{10,11... | collective-permute-start | bytes 1572872 | tf_op jit(solution)/shard_map/ppermute | solution.py:342
  524.0 28.4 %collective-permute-start.60 = (bf16[128,2048]{1,0:T(8,128)(2,1)}, bf16[128,2048]{1,0:T(8,128)(2,1)S(1)}, u32[]{:S(2)}, u32[]{:S(2)}) collective-permute-start(bf16[128,2048]{1,0:T(8,128)(2,1)} %get-tuple-element.83), channel_id=1, source_target_pairs={{0,1},{1,0},{2,3},{3,2},{4,5},{5,4},{6,7},{7,6},{8,9},{9,8},{10,11... | collective-permute-start | bytes 1572872 | tf_op jit(solution)/shard_map/ppermute | solution.py:342
  525.0 103.0 %collective-permute-start.63 = (bf16[128,2048]{1,0:T(8,128)(2,1)}, bf16[128,2048]{1,0:T(8,128)(2,1)S(1)}, u32[]{:S(2)}, u32[]{:S(2)}) collective-permute-start(bf16[128,2048]{1,0:T(8,128)(2,1)} %get-tuple-element.88), channel_id=1, source_target_pairs={{0,1},{1,0},{2,3},{3,2},{4,5},{5,4},{6,7},{7,6},{8,9},{9,8},{10,11... | collective-permute-start | bytes 1572872 | tf_op jit(solution)/shard_map/ppermute | solution.py:342
  526.0 137.8 %collective-permute-start.59 = (bf16[128,2048]{1,0:T(8,128)(2,1)}, bf16[128,2048]{1,0:T(8,128)(2,1)S(1)}, u32[]{:S(2)}, u32[]{:S(2)}) collective-permute-start(bf16[128,2048]{1,0:T(8,128)(2,1)} %get-tuple-element.81), channel_id=1, source_target_pairs={{0,1},{1,0},{2,3},{3,2},{4,5},{5,4},{6,7},{7,6},{8,9},{9,8},{10,11... | collective-permute-start | bytes 1572872 | tf_op jit(solution)/shard_map/ppermute | solution.py:342
  547.8 38.3 %collective-permute-start.54 = (bf16[128,2048]{1,0:T(8,128)(2,1)S(1)}, bf16[128,2048]{1,0:T(8,128)(2,1)S(1)}, u32[]{:S(2)}, u32[]{:S(2)}) collective-permute-start(bf16[128,2048]{1,0:T(8,128)(2,1)S(1)} %get-tuple-element.108), channel_id=1, source_target_pairs={{0,1},{1,0},{2,3},{3,2},{4,5},{5,4},{6,7},{7,6},{8,9},{9,8},{10,11... | collective-permute-start | bytes 1572872 | tf_op jit(solution)/shard_map/ppermute | solution.py:342
  548.8 48.4 %collective-permute-start.53 = (bf16[128,2048]{1,0:T(8,128)(2,1)S(1)}, bf16[128,2048]{1,0:T(8,128)(2,1)S(1)}, u32[]{:S(2)}, u32[]{:S(2)}) collective-permute-start(bf16[128,2048]{1,0:T(8,128)(2,1)S(1)} %get-tuple-element.109), channel_id=1, source_target_pairs={{0,1},{1,0},{2,3},{3,2},{4,5},{5,4},{6,7},{7,6},{8,9},{9,8},{10,11... | collective-permute-start | bytes 1572872 | tf_op jit(solution)/shard_map/ppermute | solution.py:342
  558.9 93.8 %collective-permute-start.56 = (bf16[128,2048]{1,0:T(8,128)(2,1)S(1)}, bf16[128,2048]{1,0:T(8,128)(2,1)S(1)}, u32[]{:S(2)}, u32[]{:S(2)}) collective-permute-start(bf16[128,2048]{1,0:T(8,128)(2,1)S(1)} %get-tuple-element.107), channel_id=1, source_target_pairs={{0,1},{1,0},{2,3},{3,2},{4,5},{5,4},{6,7},{7,6},{8,9},{9,8},{10,11... | collective-permute-start | bytes 1572872 | tf_op jit(solution)/shard_map/ppermute | solution.py:342
  597.3 29.5 %collective-permute-start.64 = (bf16[128,2048]{1,0:T(8,128)(2,1)S(1)}, bf16[128,2048]{1,0:T(8,128)(2,1)S(1)}, u32[]{:S(2)}, u32[]{:S(2)}) collective-permute-start(bf16[128,2048]{1,0:T(8,128)(2,1)S(1)} %add_convert_fusion.3), channel_id=1, source_target_pairs={{0,4},{1,5},{2,6},{3,7},{4,0},{5,1},{6,2},{7,3},{8,12},{9,13},{10,... | collective-permute-start | bytes 1572872 | tf_op jit(solution)/shard_map/ppermute | solution.py:342
  603.1 46.2 %collective-permute-start.57 = (bf16[128,2048]{1,0:T(8,128)(2,1)S(1)}, bf16[128,2048]{1,0:T(8,128)(2,1)S(1)}, u32[]{:S(2)}, u32[]{:S(2)}) collective-permute-start(bf16[128,2048]{1,0:T(8,128)(2,1)S(1)} %fusion.8), channel_id=1, source_target_pairs={{0,4},{1,5},{2,6},{3,7},{4,0},{5,1},{6,2},{7,3},{8,12},{9,13},{10,... | collective-permute-start | bytes 1572872 | tf_op jit(solution)/shard_map/ppermute | solution.py:342
  626.8 67.0 %collective-permute-start.52 = (bf16[128,2048]{1,0:T(8,128)(2,1)S(1)}, bf16[128,2048]{1,0:T(8,128)(2,1)S(1)}, u32[]{:S(2)}, u32[]{:S(2)}) collective-permute-start(bf16[128,2048]{1,0:T(8,128)(2,1)S(1)} %get-tuple-element.106), channel_id=1, source_target_pairs={{0,1},{1,0},{2,3},{3,2},{4,5},{5,4},{6,7},{7,6},{8,9},{9,8},{10,11... | collective-permute-start | bytes 1572872 | tf_op jit(solution)/shard_map/ppermute | solution.py:342
  628.0 39.7 %collective-permute-start.62 = (bf16[128,2048]{1,0:T(8,128)(2,1)S(1)}, bf16[128,2048]{1,0:T(8,128)(2,1)S(1)}, u32[]{:S(2)}, u32[]{:S(2)}) collective-permute-start(bf16[128,2048]{1,0:T(8,128)(2,1)S(1)} %add_convert_fusion.2), channel_id=1, source_target_pairs={{0,4},{1,5},{2,6},{3,7},{4,0},{5,1},{6,2},{7,3},{8,12},{9,13},{10,... | collective-permute-start | bytes 1572872 | tf_op jit(solution)/shard_map/ppermute | solution.py:342
  649.3 44.6 %collective-permute-start.55 = (bf16[128,2048]{1,0:T(8,128)(2,1)S(1)}, bf16[128,2048]{1,0:T(8,128)(2,1)S(1)}, u32[]{:S(2)}, u32[]{:S(2)}) collective-permute-start(bf16[128,2048]{1,0:T(8,128)(2,1)S(1)} %fusion.9), channel_id=1, source_target_pairs={{0,4},{1,5},{2,6},{3,7},{4,0},{5,1},{6,2},{7,3},{8,12},{9,13},{10,... | collective-permute-start | bytes 1572872 | tf_op jit(solution)/shard_map/ppermute | solution.py:342
  652.6 40.4 %collective-permute-start.65 = (bf16[128,2048]{1,0:T(8,128)(2,1)S(1)}, bf16[128,2048]{1,0:T(8,128)(2,1)S(1)}, u32[]{:S(2)}, u32[]{:S(2)}) collective-permute-start(bf16[128,2048]{1,0:T(8,128)(2,1)S(1)} %add_convert_fusion.1), channel_id=1, source_target_pairs={{0,2},{1,3},{2,0},{3,1},{4,6},{5,7},{6,4},{7,5},{8,10},{9,11},{10,... | collective-permute-start | bytes 1572872 | tf_op jit(solution)/shard_map/ppermute | solution.py:342
  663.8 36.6 %collective-permute-start.58 = (bf16[128,2048]{1,0:T(8,128)(2,1)S(1)}, bf16[128,2048]{1,0:T(8,128)(2,1)S(1)}, u32[]{:S(2)}, u32[]{:S(2)}) collective-permute-start(bf16[128,2048]{1,0:T(8,128)(2,1)S(1)} %fusion.7), channel_id=1, source_target_pairs={{0,2},{1,3},{2,0},{3,1},{4,6},{5,7},{6,4},{7,5},{8,10},{9,11},{10,... | collective-permute-start | bytes 1572872 | tf_op jit(solution)/shard_map/ppermute | solution.py:342
  (80 other events, 1781.2 us)
Sparse Core Ops, SparseCore 0:
  11.0 89.1 all-gather.4
  101.7 30.2 all-gather.6
  133.6 28.5 all-gather.8
  163.6 28.4 all-gather.10
  507.5 36.9 reduce-scatter.4
  546.9 37.8 reduce-scatter.10
  587.4 37.9 reduce-scatter.8
  627.8 37.8 reduce-scatter.6

commit v2 on v1

--- a/solution.py
+++ b/solution.py
@@ -369,28 +369,22 @@
     outer_near = lax.ppermute(across, "ctx", outward)
     y1 = swap(z1, 1)
     outer_far = lax.ppermute(relayed, "ctx", outward)
-    z2 = jnp.where(inside, relayed, outer_near)
+    z2 = after(jnp.where(inside, relayed, outer_near))
     y2 = swap(z2, 1)
-    z3 = jnp.where(inside, across, outer_far)
+    z3 = after(jnp.where(inside, across, outer_far))
     y3 = swap(z3, 1)
     return [own, y0, z1, y1, z2, y2, z3, y3]
 
 
 def scatter_ctx(blocks):
     other = [swap(blocks[2 * dz + 1], 1) for dz in range(4)]
-    kept3 = (blocks[6].astype(F32) + other[3].astype(F32)).astype(BF16)
-    far3 = swap(kept3, 4)
-    kept2 = (blocks[4].astype(F32) + after(other[2], kept3).astype(F32)).astype(BF16)
-    far2 = swap(kept2, 4)
-    kept1 = blocks[2].astype(F32) + other[1].astype(F32)
-    near = swap((kept1 + after(far3, kept2).astype(F32)).astype(BF16), 2)
-    kept0 = blocks[0].astype(F32) + other[0].astype(F32)
-    return kept0 + far2.astype(F32) + near.astype(F32)
-
-
-def picked(v, c):
-    v = v.reshape(8, v.shape[0] // 8, v.shape[1])
-    return [lax.dynamic_index_in_dim(v, c ^ d, 0, keepdims=False) for d in range(8)]
+    far3 = (blocks[6].astype(F32) + other[3].astype(F32)).astype(BF16)
+    via = swap(far3, 2)
+    far2 = (blocks[4].astype(F32) + other[2].astype(F32) + via.astype(F32)).astype(BF16)
+    across = swap(far2, 4)
+    near = (blocks[2].astype(F32) + after(other[1], far2).astype(F32)).astype(BF16)
+    beside = swap(near, 2)
+    return blocks[0].astype(F32) + other[0].astype(F32) + across.astype(F32) + beside.astype(F32)
 
 
 def gather_small(v, flat):
@@ -403,7 +397,7 @@
 
 
 def sum_small(v):
-    for b in (0, 1, 2, 3, 4):
+    for b in (2, 1, 3, 4, 0):
         v = v + hop(v, 1 << b)
     return v
 
@@ -441,6 +435,20 @@
     return jax.ShapeDtypeStruct(shape, dtype)
 
 
+def take_pair(step, odd, chunks, block):
+    half = block.shape[0] // 2
+    for i in range(4):
+
+        @pl.when(step == i)
+        def _():
+            block[pl.ds(pl.multiple_of(odd * half, half), half)] = chunks[2 * i][...]
+            block[pl.ds(pl.multiple_of((1 - odd) * half, half), half)] = chunks[2 * i + 1][...]
+
+
+def pair_at(d, c):
+    return ((c[0] >> 1) ^ d, 0)
+
+
 def projection_kernel(c_ref, *refs):
     chunks = refs[:8]
     packed = refs[8:12]
@@ -448,6 +456,7 @@
     x_out, xn_out, q_out, k_out, v_out, qr_out, kr_out, gate_out, weights = refs[18:27]
     block = refs[27]
     d = pl.program_id(0)
+    odd = c_ref[0] & 1
 
     @pl.when(d == 0)
     def _():
@@ -457,12 +466,7 @@
                 at = pl.multiple_of(start + size * j, size)
                 weights[pl.ds(at, size)] = packed[e][first : first + size]
 
-    for i in range(8):
-
-        @pl.when(d == i)
-        def _():
-            block[...] = chunks[i][...]
-
+    take_pair(d, odd, chunks, block)
     x_out[...] = block[...]
     x = block[...].astype(F32)
     xn = (x * lax.rsqrt(jnp.mean(x * x, axis=-1, keepdims=True) + EPS) * g1[...]).astype(BF16)
@@ -485,10 +489,10 @@
 def projection(c, chunks, packed, wgt, g1, gq, gk, cosine, sine):
     rows, width = chunks[0].shape
     length = 8 * rows
-    at = lambda d, c: (c[0] ^ d, 0)
+    at = pair_at
     return call(
         projection_kernel,
-        (8,),
+        (4,),
         [full((rows, width), pipeline_mode=pl.Buffered(1))] * 8
         + [
             *[full((128, width), pipeline_mode=pl.Buffered(1))] * 4,
@@ -496,11 +500,11 @@
             full((1, width)),
             full((1, HD)),
             full((1, HD)),
-            pl.BlockSpec((rows, HD), at),
-            pl.BlockSpec((rows, HD), at),
+            pl.BlockSpec((2 * rows, HD), at),
+            pl.BlockSpec((2 * rows, HD), at),
         ],
         [
-            *(pl.BlockSpec((rows, n), at) for n in (width, width, 2 * HD, HD, HD, 2 * HD, HD, 16)),
+            *(pl.BlockSpec((2 * rows, n), at) for n in (width, width, 2 * HD, HD, HD, 2 * HD, HD, 16)),
             full((512, width)),
         ],
         [
@@ -516,7 +520,7 @@
         ],
         2 * length * width * 528,
         20 * length * width,
-        scratch=[pltpu.VMEM((rows, width), BF16)],
+        scratch=[pltpu.VMEM((2 * rows, width), BF16)],
     )(c, *chunks, *packed, wgt, g1, gq, gk, cosine, sine)
 
 
@@ -573,23 +577,26 @@
     mixed = refs[:8]
     x, wo, g2 = refs[8:11]
     xn_out, own_out = refs[11:13]
-    total = refs[13]
-    i = pl.program_id(0)
+    left, total = refs[13:]
     c = c_ref[0]
-    total[...] = x[...].astype(F32)
+    odd = c & 1
     for d in range(8):
         other = c ^ d
-        total[...] += jnp.dot(
-            mixed[d][...], wo[2 * (other & 3) + (other >> 2)], preferred_element_type=F32
+        at = pl.multiple_of(256 * (2 * (other & 3) + (other >> 2)), 256)
+        left[:, pl.ds(at, 256)] = mixed[d][...]
+    for n in range(0, total.shape[1], 512):
+        cols = slice(n, n + 512)
+        total[:, cols] = x[:, cols].astype(F32) + jnp.dot(
+            left[...], wo[:, cols], preferred_element_type=F32
         )
     h = total[...]
-    xn_out[...] = (
-        h * lax.rsqrt(jnp.mean(h * h, axis=-1, keepdims=True) + EPS) * g2[...]
-    ).astype(BF16)
-
-    @pl.when(i == c >> 1)
+    xn = (h * lax.rsqrt(jnp.mean(h * h, axis=-1, keepdims=True) + EPS) * g2[...]).astype(BF16)
+    xn_out[pl.ds(pl.multiple_of(odd * 128, 128), 128)] = xn[:128]
+    xn_out[pl.ds(pl.multiple_of((1 - odd) * 128, 128), 128)] = xn[128:]
+
+    @pl.when(pl.program_id(0) == c >> 1)
     def _():
-        own_out[...] = total[pl.ds((c & 1) * 128, 128)]
+        own_out[...] = total[pl.ds(pl.multiple_of(odd * 128, 128), 128)]
 
 
 def hidden(c, mixed, x_all, wo, g2):
@@ -600,48 +607,22 @@
         [pl.BlockSpec((256, 256), lambda i, c: (i, 0))] * 8
         + [
             pl.BlockSpec((256, width), lambda i, c: (i, 0)),
-            full((8, 256, width), pipeline_mode=pl.Buffered(1)),
+            full((width, width), pipeline_mode=pl.Buffered(1)),
             full((1, width)),
         ],
-        [pl.BlockSpec((256, width), lambda i, c: (i, 0)), full((128, width))],
+        [pl.BlockSpec((256, width), pair_at), full((128, width))],
         [struct((length, width), BF16), struct((128, width), F32)],
         2 * length * width * width,
         12 * length * width,
-        scratch=[pltpu.VMEM((256, width), F32)],
-    )(c, *mixed, x_all, wo.reshape(8, 256, width), g2)
-
-
-def join_kernel(c_ref, *refs):
-    for i in range(8):
-
-        @pl.when(pl.program_id(0) == i)
-        def _():
-            refs[8][...] = refs[i][...]
-
-
-def join(c, chunks):
-    rows, width = chunks[0].shape
-    return call(
-        join_kernel,
-        (8,),
-        [full((rows, width), pipeline_mode=pl.Buffered(1))] * 8,
-        pl.BlockSpec((rows, width), lambda d, c: (c[0] ^ d, 0)),
-        struct((8 * rows, width), chunks[0].dtype),
-        0,
-        32 * rows * width,
-    )(c, *chunks)
+        scratch=[pltpu.VMEM((256, width), BF16), pltpu.VMEM((256, width), F32)],
+    )(c, *mixed, x_all, wo, g2)
 
 
 def mixed_back_kernel(c_ref, *refs):
     chunks = refs[:8]
     wo, attended, gate_ref = refs[8:11]
     all_out, att_out, logit_out = refs[11:]
-    for i in range(8):
-
-        @pl.when(pl.program_id(0) == i)
-        def _():
-            all_out[...] = chunks[i][...]
-
+    take_pair(pl.program_id(0), c_ref[0] & 1, chunks, all_out)
     grad = dot(all_out[...], wo[0], LAST)
     gates = gate_ref[...]
     lane = lax.broadcasted_iota(jnp.int32, gates.shape, 1)
@@ -658,17 +639,17 @@
 def mixed_back(c, chunks, wo, attended, gates):
     rows, width = chunks[0].shape
     length = 8 * rows
-    at = lambda d, c: (c[0] ^ d, 0)
+    at = pair_at
     return call(
         mixed_back_kernel,
-        (8,),
+        (4,),
         [full((rows, width), pipeline_mode=pl.Buffered(1))] * 8
         + [
             pl.BlockSpec((1, 256, width), lambda d, c: (2 * (c[0] & 3) + (c[0] >> 2), 0, 0)),
-            pl.BlockSpec((rows, 256), at),
-            pl.BlockSpec((rows, 16), at),
-        ],
-        [pl.BlockSpec((rows, n), at) for n in (width, 256, 16)],
+            pl.BlockSpec((2 * rows, 256), at),
+            pl.BlockSpec((2 * rows, 16), at),
+        ],
+        [pl.BlockSpec((2 * rows, n), at) for n in (width, 256, 16)],
         [struct((length, n), BF16) for n in (width, 256, 16)],
         512 * length * width,
         6 * length * width,
@@ -760,15 +741,16 @@
 
 
 def input_back_kernel(c_ref, *refs):
-    gq, gk, gv, logits, weights, wgt, xn, g1, gain2, heads = refs[:10]
-    outs = refs[10:18]
-    bundle, gate_sum = refs[18:]
+    gq, gk, gv, logits, weights, wgt, xn, g1, start = refs[:9]
+    outs = refs[9:13]
+    bundle, gate_sum, held = refs[13:]
     d = pl.program_id(0)
     mine = 2 * (c_ref[0] & 3) + (c_ref[0] >> 2)
 
     @pl.when(d == 0)
     def _():
-        bundle[...] = jnp.zeros_like(bundle)
+        bundle[...] = start[...]
+        bundle[16:17] = start[16:17] * g1[...]
         gate_sum[...] = jnp.zeros_like(gate_sum)
 
     part = jnp.dot(gq[...], weights[:256], preferred_element_type=F32)
@@ -778,47 +760,46 @@
     part += jnp.dot(logits[...], wgt[...], preferred_element_type=F32)
     bundle[16:17] += jnp.sum(part * xn[...].astype(F32), axis=0, keepdims=True)
     gate_sum[...] += dot(logits[...], xn[...], ROWS)
-    for i in range(8):
+    held[...] = part.astype(BF16)
+    odd = c_ref[0] & 1
+    for i in range(2):
 
         @pl.when(d == i)
         def _():
-            outs[i][...] = part.astype(BF16)
-
-    @pl.when(d == 7)
+            outs[2 * i][...] = held[pl.ds(pl.multiple_of(odd * 128, 128), 128)]
+            outs[2 * i + 1][...] = held[pl.ds(pl.multiple_of((1 - odd) * 128, 128), 128)]
+
+    @pl.when(d == 1)
     def _():
         bundle[16:17] = bundle[16:17] / g1[...]
-        bundle[17:18] = gain2[...]
-        bundle[18:19, :HD] = heads[0:1]
-        bundle[18:19, HD : 2 * HD] = heads[1:2]
         for g in range(8):
 
             @pl.when(mine == g)
             def _():
-                bundle[2 * g : 2 * g + 2] = gate_sum[0:2]
-
-
-def input_back(c, gq, gk, gv, logits, weights, wgt, xn, g1, gain2, heads):
+                bundle[2 * g : 2 * g + 2] += gate_sum[0:2]
+
+
+def input_back(c, base, gq, gk, gv, logits, weights, wgt, xn, g1, start):
     length, width = xn.shape
     rows = length // 8
-    at = lambda d, c: (c[0] ^ d, 0)
+    at = lambda d, c: ((c[0] >> 1) ^ (d + base), 0)
     return call(
         input_back_kernel,
-        (8,),
-        [pl.BlockSpec((rows, n), at) for n in (256, HD, HD, 16)]
+        (2,),
+        [pl.BlockSpec((2 * rows, n), at) for n in (256, HD, HD, 16)]
         + [
             full(weights.shape, pipeline_mode=pl.Buffered(1)),
             full(wgt.shape),
-            pl.BlockSpec((rows, width), at),
+            pl.BlockSpec((2 * rows, width), at),
             full((1, width)),
-            full((1, width)),
-            full((8, HD)),
-        ],
-        [full((rows, width))] * 8 + [full((24, width))],
-        [struct((rows, width), BF16)] * 8 + [struct((24, width), F32)],
-        1056 * length * width,
-        8 * length * width,
-        scratch=[pltpu.VMEM((16, width), F32)],
-    )(c, gq, gk, gv, logits, weights, wgt, xn, g1, gain2, heads)
+            full((24, width)),
+        ],
+        [full((rows, width))] * 4 + [full((24, width))],
+        [struct((rows, width), BF16)] * 4 + [struct((24, width), F32)],
+        528 * length * width,
+        4 * length * width,
+        scratch=[pltpu.VMEM((16, width), F32), pltpu.VMEM((2 * rows, width), BF16)],
+    )(c, gq, gk, gv, logits, weights, wgt, xn, g1, start)
 
 
 def per_device_small(*args):
@@ -876,10 +857,9 @@
     packed.append(hop(packed[0], 8))
     packed.append(hop(packed[0], 16))
     packed.append(hop(packed[2], 8))
+    ff = lax.all_gather(jnp.concatenate([w_gate, w_up, w_down], axis=0), "seq", axis=0)
+    wg, wu, wd = (v.reshape(768, width) for v in jnp.split(ff, 3, axis=1))
     wo = lax.all_gather(w_out, BOTH, axis=0, tiled=True)
-    wd = lax.all_gather(w_down, "seq", axis=0, tiled=True)
-    wg = lax.all_gather(w_gate, "seq", axis=0, tiled=True)
-    wu = lax.all_gather(w_up, "seq", axis=0, tiled=True)
 
     pos = (span_order[0][:, None] * span + jnp.arange(span, dtype=jnp.int32)).reshape(length)
     limit = jnp.maximum(pos, prefix[0] - 1)
@@ -896,11 +876,11 @@
     x_all, xn1, q_pre, k_pre, value, qr, kr, gates, w_qkv = projection(
         cs, x_chunks, packed, wgt, g1, gq, gk, cosine, sine
     )
-    cot_chunks = gather_ctx(after(cotangent, *x_chunks))
+    cot_chunks = gather_ctx(cotangent)
     attended, mixed, lse = attention(cs, qr, kr, value, gates, limit, pos)
     mixed_chunks = gather_ctx(mixed)
     xn2_all, hidden1 = hidden(cs, mixed_chunks, x_all, wo, g2)
-    cot_all = join(cs, cot_chunks)
+    cot_all = jnp.concatenate(cot_chunks, axis=0)
 
     gate = project(xn2_all, wg)
     up = project(xn2_all, wu)
@@ -910,19 +890,18 @@
     act = (silu * up).astype(BF16)
     grad_gate = (grad_act * up * sig * (1.0 + gate * (1.0 - sig))).astype(BF16)
     grad_up = (grad_act * silu).astype(BF16)
+
     grad_xn2_part = (
         jnp.dot(grad_gate, wg, preferred_element_type=F32)
         + jnp.dot(grad_up, wu, preferred_element_type=F32)
     ).astype(BF16)
-    grad_xn2 = scatter_ctx(picked(grad_xn2_part, c))
-    ff_grads = [
-        outer(left, right).astype(BF16)
-        for left, right in ((grad_gate, xn2_all), (grad_up, xn2_all), (act, cot_all))
-    ]
-    grad_w_gate, grad_w_up, grad_w_down = (
-        lax.psum_scatter(v, "seq", scatter_dimension=0, tiled=True).astype(F32)
-        for v in ff_grads
-    )
+    grad_xn2 = scatter_ctx(jnp.split(grad_xn2_part, 8, axis=0))
+    ff_grads = []
+    for left, right in ((grad_gate, xn2_all), (grad_up, xn2_all), (act, cot_all)):
+        ff_grads.append(outer(left, right).astype(BF16))
+    joined = jnp.concatenate([v.reshape(4, 192, width) for v in ff_grads], axis=1)
+    summed = lax.psum_scatter(joined.reshape(2304, width), "seq", scatter_dimension=0, tiled=True)
+    grad_w_gate, grad_w_up, grad_w_down = jnp.split(summed.astype(F32), 3, axis=0)
     branch_part = jnp.dot(act, wd, preferred_element_type=F32).astype(BF16)
 
     _, scale2 = norm_apply(hidden1, g2)
@@ -931,33 +910,44 @@
     grad_gain2 = jnp.sum(gain2_terms, axis=0)
     branch_chunks = gather_ctx(after(grad_hidden1.astype(BF16), *ff_grads, branch_part))
     grad_branch_all, grad_att, grad_logits = mixed_back(cs, branch_chunks, wo, attended, gates)
-    branch = scatter_ctx(picked(after(branch_part, *branch_chunks), c))
+    grad_wo = outer(mixed, grad_branch_all).astype(BF16)
+    branch_part = after(branch_part, *branch_chunks)
+    branch = scatter_ctx(jnp.split(branch_part, 8, axis=0))
     output = (hidden1 + branch).astype(BF16)
 
     gq_rows, gk_rows, gv_rows, head_gains = attention_back(
         cs, qr, kr, value, lse, grad_att, q_pre, k_pre, cosine, sine, gq, gk, limit, pos
     )
-    *parts, bundle = input_back(
-        cs, gq_rows, gk_rows, gv_rows, grad_logits, w_qkv, wgt, xn1, g1, grad_gain2[None], head_gains
-    )
-    grad_xn1 = scatter_ctx(parts)
+    heads = jnp.pad(head_gains[:2].reshape(1, 2 * HD), ((0, 0), (0, width - 2 * HD)))
+    bundle = jnp.concatenate(
+        [jnp.zeros((17, width), F32), grad_gain2[None], heads, jnp.zeros((5, width), F32)], axis=0
+    )
+    shared = (gq_rows, gk_rows, gv_rows, grad_logits, w_qkv, wgt, xn1, g1)
+    *far, bundle = input_back(cs, 2, *shared, bundle)
+    *close, bundle = input_back(cs, 0, *shared, bundle)
+    grad_xn1 = scatter_ctx(close + far)
     x = tokens.astype(F32)
     scale1 = lax.rsqrt(jnp.mean(x * x, axis=-1, keepdims=True) + EPS)
     grad_x, _ = norm_back(x, scale1, g1, grad_xn1)
     grad_tokens = grad_hidden1 + grad_x
 
+    g_wo = lax.psum_scatter(grad_wo, "seq", scatter_dimension=0, tiled=True)
+    g_wo = turn(g_wo).astype(F32)
     pieces = jnp.concatenate(
         [
-            outer(gq_rows, xn1).astype(BF16).reshape(4, 64, width),
-            outer(gk_rows, xn1).astype(BF16).reshape(4, 32, width),
-            outer(gv_rows, xn1).astype(BF16).reshape(4, 32, width),
-            outer(mixed, grad_branch_all).astype(BF16).reshape(4, 64, width),
-        ],
-        axis=1,
-    ).reshape(4 * 192, width)
-    home = lax.psum_scatter(pieces, "seq", scatter_dimension=0, tiled=True)
-    home = turn(home).astype(F32)
-    g_wq, g_wk, g_wv, g_wo = home[:64], home[64:96], home[96:128], home[128:]
+            outer(gq_rows, xn1).astype(BF16).reshape(2, 2, 64, width),
+            outer(gk_rows, xn1).astype(BF16).reshape(2, 2, 32, width),
+            outer(gv_rows, xn1).astype(BF16).reshape(2, 2, 32, width),
+        ],
+        axis=2,
+    )
+    for axis, bit in ((1, s & 1), (0, s >> 1)):
+        sent = lax.dynamic_index_in_dim(pieces, 1 - bit, axis, keepdims=False)
+        kept = lax.dynamic_index_in_dim(pieces, bit, axis, keepdims=False)
+        got = hop(sent, 8 if axis else 16)
+        pieces = (kept.astype(F32) + got.astype(F32)).astype(BF16)
+    home = turn(pieces)
+    g_wq, g_wk, g_wv = (v.astype(F32) for v in jnp.split(home, (64, 96), axis=0))
 
     bundle = sum_small(bundle)
     blocks = lax.dynamic_slice_in_dim(bundle[:18], 64 * flat, 64, 1)

time: 743 us -> 657 us (0.88)
  the two profiles are of different devices: /device:TPU:22 before, /device:TPU:24 now
where the time goes in v2:
time: 657 us; the launch traced here: 649 us
  waiting for transfers between devices  286 us (44%)
  starting transfers between devices  149 us (23%)
  Pallas kernels  76 us (12%)
  matrix products  60.7 us (9%)
  local copies, waits for them, and re-layouts  32.3 us (5%)
  other arithmetic  28.7 us (4%)
  between operations  16 us (2%)
    ppermute x41, waiting for transfers between devices, swap(): return lax.ppermute(v, 'ctx', [(c, c ^ d) for c in range(8)])  164 us
    ppermute x41, starting transfers between devices, swap(): return lax.ppermute(v, 'ctx', [(c, c ^ d) for c in range(8)])  70.9 us
    ppermute x15, waiting for transfers between devices, hop(): return lax.ppermute(v, BOTH, [(i, i ^ d) for i in range(32)])  58.9 us
    ppermute x15, starting transfers between devices, hop(): return lax.ppermute(v, BOTH, [(i, i ^ d) for i in range(32)])  40.8 us
    dot_general x7, matrix products, outer(): lax.dot_general(left, right, (((0,), (0,)), ((), ())), preferred_element_...  32.4 us
    ppermute x4, waiting for transfers between devices, gather_ctx(): outer_far = lax.ppermute(relayed, 'ctx', outward)  32.4 us
    ppermute x3, starting transfers between devices, turn(): return lax.ppermute(v, BOTH, pairs)  19.2 us
    ppermute x3, waiting for transfers between devices, turn(): return lax.ppermute(v, BOTH, pairs)  18.1 us
  transfers between devices with their start and end apart: 79, of which 38 were waited for; matrix products, arithmetic and copies ran while one was open for 11% of the time, Pallas kernels for 8%

profile of v2, /device:TPU:24, one launch (start us, length us, event | category | flops | bytes accessed | tf_op | source)
XLA Modules:
  0.0 648.5 jit_solution(6766501058648954603)
XLA Ops:
  26.4 8.2 %collective-permute-done.13 = bf16[32,64]{1,0:T(8,128)(2,1)S(1)} collective-permute-done((bf16[32,64]{1,0:T(8,128)(2,1)S(1)}, bf16[32,64]{1,0:T(8,128)(2,1)S(1)}, u32[]{:S(2)}, u32[]{:S(2)}) %collective-permute-start.13) | collective-permute-done | bytes 4128 | tf_op jit(solution)/shard_map/ppermute | solution.py:346
  45.8 7.4 %collective-permute-done.17 = bf16[2,2,2,2,32,64]{5,4,1,2,3,0:T(8,128)(2,1)S(1)} collective-permute-done((bf16[2,2,2,2,32,64]{5,4,1,2,3,0:T(8,128)(2,1)S(1)}, bf16[2,2,2,2,32,64]{5,4,1,2,3,0:T(8,128)(2,1)S(1)}, u32[]{:S(2)}, u32[]{:S(2)}) %collective-permute-start.17) | collective-permute-done | bytes 65568 | tf_op jit(solution)/shard_map/ppermute | solution.py:346
  63.3 7.3 %collective-permute-done.9.refs_8_ = bf16[128,2048]{1,0:T(8,128)(2,1)} collective-permute-done((bf16[128,2048]{1,0:T(8,128)(2,1)S(1)}, bf16[128,2048]{1,0:T(8,128)(2,1)}, u32[]{:S(2)}, u32[]{:S(2)}) %collective-permute-start.9) | collective-permute-done | bytes 524320 | tf_op jit(solution)/shard_map/ppermute | solution.py:353
  77.1 11.3 %collective-permute-done.7 = bf16[128,2048]{1,0:T(8,128)(2,1)S(1)} collective-permute-done((bf16[128,2048]{1,0:T(8,128)(2,1)}, bf16[128,2048]{1,0:T(8,128)(2,1)S(1)}, u32[]{:S(2)}, u32[]{:S(2)}) %collective-permute-start.7) | collective-permute-done | bytes 524320 | tf_op jit(solution)/shard_map/ppermute | solution.py:371
  92.0 7.3 %collective-permute-done.11.refs_10_ = bf16[128,2048]{1,0:T(8,128)(2,1)} collective-permute-done((bf16[128,2048]{1,0:T(8,128)(2,1)}, bf16[128,2048]{1,0:T(8,128)(2,1)}, u32[]{:S(2)}, u32[]{:S(2)}) %collective-permute-start.11) | collective-permute-done | bytes 524320 | tf_op jit(solution)/shard_map/ppermute | solution.py:346
  110.5 6.3 collective-permute-done.6.refs_5_
  116.8 12.6 %collective-permute-done.8.refs_7_ = bf16[128,2048]{1,0:T(8,128)(2,1)} collective-permute-done((bf16[128,2048]{1,0:T(8,128)(2,1)}, bf16[128,2048]{1,0:T(8,128)(2,1)}, u32[]{:S(2)}, u32[]{:S(2)}) %collective-permute-start.8) | collective-permute-done | bytes 524320 | tf_op jit(solution)/shard_map/ppermute | solution.py:342
  129.4 12.7 %shard_map.263 = (bf16[1024,2048]{1,0:T(8,128)(2,1)}, bf16[1024,2048]{1,0:T(8,128)(2,1)}, f32[1024,256]{1,0:T(8,128)}, f32[1024,128]{1,0:T(8,128)}, bf16[1024,12...) custom-call(s32[2]{0:T(128)} %pad_add_fusion.c_ref, ...), custom_call_target="tpu_custom_call" | custom-call | flops 2214592512 | bytes 41943040 | tf_op jit(solution)/shard_map/pallas_call | solution.py:493
  142.1 10.3 %shard_map.264 = (f32[1024,256]{1,0:T(8,128)}, bf16[1024,256]{1,0:T(8,128)(2,1)}, f32[2,1024,1]{2,1,0:T(8,128)}) custom-call(s32[2]{0:T(128)} %pad_add_fusion.c_ref, s32[1024,1]{1,0:T(8,128)} %max.19.limit_ref.refs_0_, s32[1,1024]{1,0:T(1,128)} %add.204.pos_ref.refs_1_, bf16[1024,256]{1,0:T(8,128)(2,1)} %get-tuple-element.50.q_ref.refs_2_, ...), custom_call_target="tpu_custom_call" | custom-call | flops 1073741824 | bytes 2097152 | tf_op jit(solution)/shard_map/pallas_call | solution.py:549
  152.4 10.3 %collective-permute-start.19 = (bf16[1024,256]{1,0:T(8,128)(2,1)}, bf16[1024,256]{1,0:T(8,128)(2,1)}, u32[]{:S(2)}, u32[]{:S(2)}) collective-permute-start(bf16[1024,256]{1,0:T(8,128)(2,1)} %get-tuple-element.54.refs_0_), channel_id=1, source_target_pairs={{0,2},{1,3},{2,0},{3,1},{4,6},{5,7},{6,4},{7,5},{8,10},{9,11},{10,... | collective-permute-start | bytes 1572872 | tf_op jit(solution)/shard_map/ppermute | solution.py:342
  165.7 18.4 %collective-permute-done.19.refs_2_ = bf16[1024,256]{1,0:T(8,128)(2,1)} collective-permute-done((bf16[1024,256]{1,0:T(8,128)(2,1)}, bf16[1024,256]{1,0:T(8,128)(2,1)}, u32[]{:S(2)}, u32[]{:S(2)}) %collective-permute-start.19) | collective-permute-done | bytes 524320 | tf_op jit(solution)/shard_map/ppermute | solution.py:342
  192.5 7.3 %collective-permute-done.35 = bf16[128,2048]{1,0:T(8,128)(2,1)S(1)} collective-permute-done((bf16[128,2048]{1,0:T(8,128)(2,1)S(1)}, bf16[128,2048]{1,0:T(8,128)(2,1)S(1)}, u32[]{:S(2)}, u32[]{:S(2)}) %collective-permute-start.35) | collective-permute-done | bytes 524320 | tf_op jit(solution)/shard_map/ppermute | solution.py:342
  203.1 10.7 %collective-permute-done.25 = bf16[1024,256]{1,0:T(8,128)(2,1)S(1)} collective-permute-done((bf16[1024,256]{1,0:T(8,128)(2,1)S(1)}, bf16[1024,256]{1,0:T(8,128)(2,1)S(1)}, u32[]{:S(2)}, u32[]{:S(2)}) %collective-permute-start.25) | collective-permute-done | bytes 524320 | tf_op jit(solution)/shard_map/ppermute | solution.py:371
  215.8 6.2 fusion.22
  222.8 5.2 fusion.27
  228.0 5.5 collective-permute-done.24.refs_5_
  233.5 8.6 %collective-permute-done.26.refs_7_ = bf16[1024,256]{1,0:T(8,128)(2,1)S(1)} collective-permute-done((bf16[1024,256]{1,0:T(8,128)(2,1)S(1)}, bf16[1024,256]{1,0:T(8,128)(2,1)S(1)}, u32[]{:S(2)}, u32[]{:S(2)}) %collective-permute-start.26) | collective-permute-done | bytes 524320 | tf_op jit(solution)/shard_map/ppermute | solution.py:342
  243.0 17.2 %shard_map.265 = (bf16[1024,2048]{1,0:T(8,128)(2,1)}, f32[128,2048]{1,0:T(8,128)}) custom-call(s32[2]{0:T(128)} %pad_add_fusion.c_ref, bf16[1024,256]{1,0:T(8,128)(2,1)} %get-tuple-element.54.refs_0_, bf16[1024,256]{1,0:T(8,128)(2,1)} %collective-permute-done.18.refs_1_, bf16[1024,256]{1,0:T(8,128)(2,1)} %collective-permute-done.19.refs_2_, ...), custom_call_target="tpu_custom_call" | custom-call | flops 8589934592 | bytes 25165824 | tf_op jit(solution)/shard_map/pallas_call | solution.py:604
  260.2 6.4 fusion.26
  271.3 15.3 %convolution_convert_fusion.2 = bf16[768,2048]{1,0:T(8,128)(2,1)} fusion(bf16[1024,768]{1,0:T(8,128)(2,1)S(1)} %get-tuple-element.99, bf16[1024,2048]{1,0:T(8,128)(2,1)S(1)} %copy-done.49), kind=kOutput, calls=%fused_computation.4 | convolution fusion | flops 3222798336 | bytes 8912896 | tf_op jit(solution)/shard_map/dot_general | solution.py:52
  300.9 7.9 %collective-permute-done.38 = bf16[128,2048]{1,0:T(8,128)(2,1)S(1)} collective-permute-done((bf16[128,2048]{1,0:T(8,128)(2,1)S(1)}, bf16[128,2048]{1,0:T(8,128)(2,1)S(1)}, u32[]{:S(2)}, u32[]{:S(2)}) %collective-permute-start.38) | collective-permute-done | bytes 524320 | tf_op jit(solution)/shard_map/ppermute | solution.py:342
  308.9 8.7 %collective-permute-start.39 = (bf16[128,2048]{1,0:T(8,128)(2,1)S(1)}, bf16[128,2048]{1,0:T(8,128)(2,1)S(1)}, u32[]{:S(2)}, u32[]{:S(2)}) collective-permute-start(bf16[128,2048]{1,0:T(8,128)(2,1)S(1)} %add_convert_fusion.10), channel_id=1, source_target_pairs={{0,2},{1,3},{2,0},{3,1},{4,6},{5,7},{6,4},{7,5},{8,10},{9,11},{10,... | collective-permute-start | bytes 1572872 | tf_op jit(solution)/shard_map/ppermute | solution.py:342
  325.0 5.8 collective-permute-start.40
  340.1 5.0 convolution_convert_fusion
  345.1 11.2 %collective-permute-done.42 = bf16[128,2048]{1,0:T(8,128)(2,1)S(1)} collective-permute-done((bf16[128,2048]{1,0:T(8,128)(2,1)S(1)}, bf16[128,2048]{1,0:T(8,128)(2,1)S(1)}, u32[]{:S(2)}, u32[]{:S(2)}) %collective-permute-start.42) | collective-permute-done | bytes 524320 | tf_op jit(solution)/shard_map/ppermute | solution.py:342
  358.2 8.7 %collective-permute-done.44.refs_2_ = bf16[128,2048]{1,0:T(8,128)(2,1)S(1)} collective-permute-done((bf16[128,2048]{1,0:T(8,128)(2,1)S(1)}, bf16[128,2048]{1,0:T(8,128)(2,1)S(1)}, u32[]{:S(2)}, u32[]{:S(2)}) %collective-permute-start.44) | collective-permute-done | bytes 524320 | tf_op jit(solution)/shard_map/ppermute | solution.py:342
  372.3 9.2 %collective-permute-done.48 = bf16[128,2048]{1,0:T(8,128)(2,1)S(1)} collective-permute-done((bf16[128,2048]{1,0:T(8,128)(2,1)S(1)}, bf16[128,2048]{1,0:T(8,128)(2,1)S(1)}, u32[]{:S(2)}, u32[]{:S(2)}) %collective-permute-start.48) | collective-permute-done | bytes 524320 | tf_op jit(solution)/shard_map/ppermute | solution.py:369
  383.5 10.3 %collective-permute-done.50 = bf16[128,2048]{1,0:T(8,128)(2,1)S(1)} collective-permute-done((bf16[128,2048]{1,0:T(8,128)(2,1)S(1)}, bf16[128,2048]{1,0:T(8,128)(2,1)S(1)}, u32[]{:S(2)}, u32[]{:S(2)}) %collective-permute-start.50) | collective-permute-done | bytes 524320 | tf_op jit(solution)/shard_map/ppermute | solution.py:371
  396.3 11.1 %collective-permute-done.49.refs_5_ = bf16[128,2048]{1,0:T(8,128)(2,1)S(1)} collective-permute-done((bf16[128,2048]{1,0:T(8,128)(2,1)S(1)}, bf16[128,2048]{1,0:T(8,128)(2,1)S(1)}, u32[]{:S(2)}, u32[]{:S(2)}) %collective-permute-start.49) | collective-permute-done | bytes 524320 | tf_op jit(solution)/shard_map/ppermute | solution.py:342
  407.4 5.6 collective-permute-done.51.refs_7_
  413.8 7.9 %shard_map.266 = (bf16[1024,2048]{1,0:T(8,128)(2,1)}, bf16[1024,256]{1,0:T(8,128)(2,1)}, bf16[1024,16]{1,0:T(8,128)(2,1)}) custom-call(s32[2]{0:T(128)} %pad_add_fusion.c_ref, bf16[128,2048]{1,0:T(8,128)(2,1)} %copy-done.9, bf16[128,2048]{1,0:T(8,128)(2,1)} %copy-done.20, bf16[128,2048]{1,0:T(8,128)(2,1)} %copy-done.19, bf16[128,2048]{1,0:T(8,128)(2,1)} %copy-done.21, ...), custom_call_target="tpu_custom_call" | custom-call | flops 1073741824 | bytes 12582912 | tf_op jit(solution)/shard_map/pallas_call | solution.py:643
  426.6 7.7 %pad_maximum_fusion = bf16[4,576,2048]{2,1,0:T(8,128)(2,1)} fusion(bf16[4,192,2048]{2,1,0:T(8,128)(2,1)} %bitcast.112, bf16[4,192,2048]{2,1,0:T(8,128)(2,1)} %bitcast.110, bf16[4,192,2048]{2,1,0:T(8,128)(2,1)} %bitcast.111), kind=kLoop, calls=%fused_computation | loop fusion | flops 28311552 | bytes 18874368 | tf_op jit(solution)/shard_map/concatenate | solution.py:902
  434.5 14.1 %shard_map.267 = (bf16[1024,256]{1,0:T(8,128)(2,1)}, bf16[1024,128]{1,0:T(8,128)(2,1)}, bf16[1024,128]{1,0:T(8,128)(2,1)}, f32[8,128]{1,0:T(8,128)}) custom-call(s32[2]{0:T(128)} %pad_add_fusion.c_ref, s32[1024,1]{1,0:T(8,128)} %max.19.limit_ref.refs_0_, s32[1,1024]{1,0:T(1,128)} %add.204.pos_ref.refs_1_, bf16[1024,256]{1,0:T(8,128)(2,1)} %get-tuple-element.50.q_ref.refs_2_, ...), custom_call_target="tpu_custom_call" | custom-call | flops 2684354560 | bytes 5242880 | tf_op jit(solution)/shard_map/pallas_call | solution.py:709
  450.1 6.9 %shard_map.268 = (bf16[128,2048]{1,0:T(8,128)(2,1)}, bf16[128,2048]{1,0:T(8,128)(2,1)}, bf16[128,2048]{1,0:T(8,128)(2,1)}, bf16[128,2048]{1,0:T(8,128)(2,1)}, f32[24,2048]{1,0:T(8,128)}) custom-call(s32[2]{0:T(128)} %pad_add_fusion.c_ref, bf16[1024,256]{1,0:T(8,128)(2,1)} %get-tuple-element.67.refs_0_, bf16[1024,128]{1,0:T(8,128)(2,1)} %get-tuple-element.68.refs_1_, ...), custom_call_target="tpu_custom_call" | custom-call | flops 1107296256 | bytes 8388608 | tf_op jit(solution)/shard_map/pallas_call | solution.py:786
  457.0 6.9 %shard_map.269 = (bf16[128,2048]{1,0:T(8,128)(2,1)}, bf16[128,2048]{1,0:T(8,128)(2,1)}, bf16[128,2048]{1,0:T(8,128)(2,1)}, bf16[128,2048]{1,0:T(8,128)(2,1)}, f32[24,2048]{1,0:T(8,128)}) custom-call(s32[2]{0:T(128)} %pad_add_fusion.c_ref, bf16[1024,256]{1,0:T(8,128)(2,1)} %get-tuple-element.67.refs_0_, bf16[1024,128]{1,0:T(8,128)(2,1)} %get-tuple-element.68.refs_1_, ...), custom_call_target="tpu_custom_call" | custom-call | flops 1107296256 | bytes 8388608 | tf_op jit(solution)/shard_map/pallas_call | solution.py:786
  463.9 17.6 %collective-permute-start.70 = (f32[24,2048]{1,0:T(8,128)}, f32[24,2048]{1,0:T(8,128)S(1)}, u32[]{:S(2)}, u32[]{:S(2)}) collective-permute-start(f32[24,2048]{1,0:T(8,128)} %get-tuple-element.85), channel_id=1, source_target_pairs={{0,4},{1,5},{2,6},{3,7},{4,0},{5,1},{6,2},{7,3},{8,12},{9,13},{10,... | collective-permute-start | bytes 589832 | tf_op jit(solution)/shard_map/ppermute | solution.py:346
  489.5 5.4 collective-permute-done.71
  498.1 9.5 %collective-permute-done.54 = bf16[128,2048]{1,0:T(8,128)(2,1)S(1)} collective-permute-done((bf16[128,2048]{1,0:T(8,128)(2,1)S(1)}, bf16[128,2048]{1,0:T(8,128)(2,1)S(1)}, u32[]{:S(2)}, u32[]{:S(2)}) %collective-permute-start.54) | collective-permute-done | bytes 524320 | tf_op jit(solution)/shard_map/ppermute | solution.py:342
  507.6 5.9 collective-permute-start.73
  513.7 7.8 %collective-permute-done.73 = f32[24,2048]{1,0:T(8,128)S(1)} collective-permute-done((f32[24,2048]{1,0:T(8,128)S(1)}, f32[24,2048]{1,0:T(8,128)S(1)}, u32[]{:S(2)}, u32[]{:S(2)}) %collective-permute-start.73) | collective-permute-done | bytes 196640 | tf_op jit(solution)/shard_map/ppermute | solution.py:346
  523.8 17.4 %collective-permute-done.74 = f32[24,2048]{1,0:T(8,128)S(1)} collective-permute-done((f32[24,2048]{1,0:T(8,128)S(1)}, f32[24,2048]{1,0:T(8,128)S(1)}, u32[]{:S(2)}, u32[]{:S(2)}) %collective-permute-start.74) | collective-permute-done | bytes 196640 | tf_op jit(solution)/shard_map/ppermute | solution.py:346
  545.7 7.5 %collective-permute-done.55 = bf16[128,2048]{1,0:T(8,128)(2,1)S(1)} collective-permute-done((bf16[128,2048]{1,0:T(8,128)(2,1)S(1)}, bf16[128,2048]{1,0:T(8,128)(2,1)S(1)}, u32[]{:S(2)}, u32[]{:S(2)}) %collective-permute-start.55) | collective-permute-done | bytes 524320 | tf_op jit(solution)/shard_map/ppermute | solution.py:342
  562.4 7.8 %collective-permute-start.67 = (bf16[128,2048]{1,0:T(8,128)(2,1)S(1)}, bf16[128,2048]{1,0:T(8,128)(2,1)S(1)}, u32[]{:S(2)}, u32[]{:S(2)}) collective-permute-start(bf16[128,2048]{1,0:T(8,128)(2,1)S(1)} %dynamic-slice_bitcast_fusion.1), channel_id=1, source_target_pairs={{0,16},{1,17},{2,18},{3,19},{4,20},{5,21},{6,22},{7,23},{8,24},{9,... | collective-permute-start | bytes 1572872 | tf_op jit(solution)/shard_map/ppermute | solution.py:346
  580.4 21.0 %collective-permute-done.65 = bf16[128,2048]{1,0:T(8,128)(2,1)S(1)} collective-permute-done((bf16[128,2048]{1,0:T(8,128)(2,1)S(1)}, bf16[128,2048]{1,0:T(8,128)(2,1)S(1)}, u32[]{:S(2)}, u32[]{:S(2)}) %collective-permute-start.65) | collective-permute-done | bytes 524320 | tf_op jit(solution)/shard_map/ppermute | solution.py:342
  601.4 7.3 %collective-permute-start.68 = (bf16[128,2048]{1,0:T(8,128)(2,1)S(1)}, bf16[128,2048]{1,0:T(8,128)(2,1)S(1)}, u32[]{:S(2)}, u32[]{:S(2)}) collective-permute-start(bf16[128,2048]{1,0:T(8,128)(2,1)S(1)} %fusion.7), channel_id=1, source_target_pairs={{0,0},{1,8},{2,16},{3,24},{4,4},{5,12},{6,20},{7,28},{8,1},{9,9},{... | collective-permute-start | bytes 1572872 | tf_op jit(solution)/shard_map/ppermute | solution.py:353
  610.8 5.5 collective-permute-done.58
  617.4 7.0 %collective-permute-start.69 = (bf16[64,2048]{1,0:T(8,128)(2,1)}, bf16[64,2048]{1,0:T(8,128)(2,1)S(1)}, u32[]{:S(2)}, u32[]{:S(2)}) collective-permute-start(bf16[64,2048]{1,0:T(8,128)(2,1)} %reduce-scatter.3.cloned.1.call-done), channel_id=1, source_target_pairs={{0,0},{1,8},{2,16},{3,24},{4,4},{5,12},{6,20},{7,28},{8,1},{9,9},{... | collective-permute-start | bytes 786440 | tf_op jit(solution)/shard_map/ppermute | solution.py:353
  624.4 8.6 %collective-permute-done.68 = bf16[128,2048]{1,0:T(8,128)(2,1)S(1)} collective-permute-done((bf16[128,2048]{1,0:T(8,128)(2,1)S(1)}, bf16[128,2048]{1,0:T(8,128)(2,1)S(1)}, u32[]{:S(2)}, u32[]{:S(2)}) %collective-permute-start.68) | collective-permute-done | bytes 524320 | tf_op jit(solution)/shard_map/ppermute | solution.py:353
  (339 shorter events, 182.5 us)
Async XLA Ops:
  7.3 208.5 %all-gather.6.cloned.1.call-start = ((), (), s32[]{:S(2)}) async-start(), calls=%async_computation.5 | async-start | bytes 11796480 | tf_op jit(solution)/shard_map/all_gather | solution.py:860
  10.7 231.4 %all-gather.4.cloned.1.call-start = ((), (), s32[]{:S(2)}) async-start(), calls=%async_computation.2 | async-start | bytes 8650752 | tf_op jit(solution)/shard_map/all_gather | solution.py:862
  11.4 606.0 %reduce-scatter.3.cloned.1.call-start = ((), (), s32[]{:S(2)}) async-start(), calls=%async_computation.3 | async-start | bytes 1310720 | tf_op jit(solution)/shard_map/reduce_scatter | solution.py:934
  11.5 59.9 %collective-permute-start.28 = (bf16[128,2048]{1,0:T(8,128)(2,1)S(1)}, bf16[128,2048]{1,0:T(8,128)(2,1)}, u32[]{:S(2)}, u32[]{:S(2)}) collective-permute-start(bf16[128,2048]{1,0:T(8,128)(2,1)S(1)} %copy-done.11), channel_id=1, source_target_pairs={{0,2},{1,3},{2,0},{3,1},{4,6},{5,7},{6,4},{7,5},{8,10},{9,11},{10,... | collective-permute-start | bytes 1572872 | tf_op jit(solution)/shard_map/ppermute | solution.py:342
  12.0 61.5 %collective-permute-start.27 = (bf16[128,2048]{1,0:T(8,128)(2,1)S(1)}, bf16[128,2048]{1,0:T(8,128)(2,1)}, u32[]{:S(2)}, u32[]{:S(2)}) collective-permute-start(bf16[128,2048]{1,0:T(8,128)(2,1)S(1)} %copy-done.11), channel_id=1, source_target_pairs={{0,1},{1,0},{2,3},{3,2},{4,5},{5,4},{6,7},{7,6},{8,9},{9,8},{10,11... | collective-permute-start | bytes 1572872 | tf_op jit(solution)/shard_map/ppermute | solution.py:342
  13.5 46.3 %collective-permute-start.4 = (bf16[128,2048]{1,0:T(8,128)(2,1)S(1)}, bf16[128,2048]{1,0:T(8,128)(2,1)}, u32[]{:S(2)}, u32[]{:S(2)}) collective-permute-start(bf16[128,2048]{1,0:T(8,128)(2,1)S(1)} %copy-done.14), channel_id=1, source_target_pairs={{2,4},{3,5},{4,2},{5,3},{10,12},{11,13},{12,10},{13,11},{18,20},{1... | collective-permute-start | bytes 1572872 | tf_op jit(solution)/shard_map/ppermute | solution.py:366
  15.0 43.1 %collective-permute-start.1 = (bf16[128,2048]{1,0:T(8,128)(2,1)S(1)}, bf16[128,2048]{1,0:T(8,128)(2,1)}, u32[]{:S(2)}, u32[]{:S(2)}) collective-permute-start(bf16[128,2048]{1,0:T(8,128)(2,1)S(1)} %copy-done.14), channel_id=1, source_target_pairs={{0,2},{1,3},{2,0},{3,1},{4,6},{5,7},{6,4},{7,5},{8,10},{9,11},{10,... | collective-permute-start | bytes 1572872 | tf_op jit(solution)/shard_map/ppermute | solution.py:342
  61.9 26.5 %collective-permute-start.7 = (bf16[128,2048]{1,0:T(8,128)(2,1)}, bf16[128,2048]{1,0:T(8,128)(2,1)S(1)}, u32[]{:S(2)}, u32[]{:S(2)}) collective-permute-start(bf16[128,2048]{1,0:T(8,128)(2,1)} %collective-permute-done.3), channel_id=1, source_target_pairs={{2,0},{3,1},{4,6},{5,7},{10,8},{11,9},{12,14},{13,15},{18,16},{19,... | collective-permute-start | bytes 1572872 | tf_op jit(solution)/shard_map/ppermute | solution.py:371
  70.7 19.3 %collective-permute-start.31 = (bf16[128,2048]{1,0:T(8,128)(2,1)S(1)}, bf16[128,2048]{1,0:T(8,128)(2,1)S(1)}, u32[]{:S(2)}, u32[]{:S(2)}) collective-permute-start(bf16[128,2048]{1,0:T(8,128)(2,1)S(1)} %copy-done.11), channel_id=1, source_target_pairs={{2,4},{3,5},{4,2},{5,3},{10,12},{11,13},{12,10},{13,11},{18,20},{1... | collective-permute-start | bytes 1572872 | tf_op jit(solution)/shard_map/ppermute | solution.py:366
  73.5 25.7 %collective-permute-start.11 = (bf16[128,2048]{1,0:T(8,128)(2,1)}, bf16[128,2048]{1,0:T(8,128)(2,1)}, u32[]{:S(2)}, u32[]{:S(2)}) collective-permute-start(bf16[128,2048]{1,0:T(8,128)(2,1)} %collective-permute-done.9.refs_8_), channel_id=1, source_target_pairs={{0,16},{1,17},{2,18},{3,19},{4,20},{5,21},{6,22},{7,23},{8,24},{9,... | collective-permute-start | bytes 1572872 | tf_op jit(solution)/shard_map/ppermute | solution.py:346
  76.7 22.6 %collective-permute-start.10 = (bf16[128,2048]{1,0:T(8,128)(2,1)}, bf16[128,2048]{1,0:T(8,128)(2,1)S(1)}, u32[]{:S(2)}, u32[]{:S(2)}) collective-permute-start(bf16[128,2048]{1,0:T(8,128)(2,1)} %collective-permute-done.9.refs_8_), channel_id=1, source_target_pairs={{0,8},{1,9},{2,10},{3,11},{4,12},{5,13},{6,14},{7,15},{8,0},{9,1},... | collective-permute-start | bytes 1572872 | tf_op jit(solution)/shard_map/ppermute | solution.py:346
  90.0 26.9 %collective-permute-start.6 = (bf16[128,2048]{1,0:T(8,128)(2,1)S(1)}, bf16[128,2048]{1,0:T(8,128)(2,1)}, u32[]{:S(2)}, u32[]{:S(2)}) collective-permute-start(bf16[128,2048]{1,0:T(8,128)(2,1)S(1)} %broadcast_select_fusion.7.refs_4_), channel_id=1, source_target_pairs={{0,1},{1,0},{2,3},{3,2},{4,5},{5,4},{6,7},{7,6},{8,9},{9,8},{10,11... | collective-permute-start | bytes 1572872 | tf_op jit(solution)/shard_map/ppermute | solution.py:342
  99.3 30.1 %collective-permute-start.8 = (bf16[128,2048]{1,0:T(8,128)(2,1)}, bf16[128,2048]{1,0:T(8,128)(2,1)}, u32[]{:S(2)}, u32[]{:S(2)}) collective-permute-start(bf16[128,2048]{1,0:T(8,128)(2,1)} %broadcast_select_fusion.6.refs_6_), channel_id=1, source_target_pairs={{0,1},{1,0},{2,3},{3,2},{4,5},{5,4},{6,7},{7,6},{8,9},{9,8},{10,11... | collective-permute-start | bytes 1572872 | tf_op jit(solution)/shard_map/ppermute | solution.py:342
  104.6 58.0 %collective-permute-start.32 = (bf16[128,2048]{1,0:T(8,128)(2,1)S(1)}, bf16[128,2048]{1,0:T(8,128)(2,1)}, u32[]{:S(2)}, u32[]{:S(2)}) collective-permute-start(bf16[128,2048]{1,0:T(8,128)(2,1)S(1)} %collective-permute-done.31), channel_id=1, source_target_pairs={{2,0},{3,1},{4,6},{5,7},{10,8},{11,9},{12,14},{13,15},{18,16},{19,... | collective-permute-start | bytes 1572872 | tf_op jit(solution)/shard_map/ppermute | solution.py:369
  107.8 56.3 %collective-permute-start.29 = (bf16[128,2048]{1,0:T(8,128)(2,1)}, bf16[128,2048]{1,0:T(8,128)(2,1)S(1)}, u32[]{:S(2)}, u32[]{:S(2)}) collective-permute-start(bf16[128,2048]{1,0:T(8,128)(2,1)} %collective-permute-done.28), channel_id=1, source_target_pairs={{0,1},{1,0},{2,3},{3,2},{4,5},{5,4},{6,7},{7,6},{8,9},{9,8},{10,11... | collective-permute-start | bytes 1572872 | tf_op jit(solution)/shard_map/ppermute | solution.py:342
  109.2 75.5 %collective-permute-start.34 = (bf16[128,2048]{1,0:T(8,128)(2,1)S(1)}, bf16[128,2048]{1,0:T(8,128)(2,1)S(1)}, u32[]{:S(2)}, u32[]{:S(2)}) collective-permute-start(bf16[128,2048]{1,0:T(8,128)(2,1)S(1)} %collective-permute-done.30), channel_id=1, source_target_pairs={{2,0},{3,1},{4,6},{5,7},{10,8},{11,9},{12,14},{13,15},{18,16},{19,... | collective-permute-start | bytes 1572872 | tf_op jit(solution)/shard_map/ppermute | solution.py:371
  152.4 31.7 %collective-permute-start.19 = (bf16[1024,256]{1,0:T(8,128)(2,1)}, bf16[1024,256]{1,0:T(8,128)(2,1)}, u32[]{:S(2)}, u32[]{:S(2)}) collective-permute-start(bf16[1024,256]{1,0:T(8,128)(2,1)} %get-tuple-element.54.refs_0_), channel_id=1, source_target_pairs={{0,2},{1,3},{2,0},{3,1},{4,6},{5,7},{6,4},{7,5},{8,10},{9,11},{10,... | collective-permute-start | bytes 1572872 | tf_op jit(solution)/shard_map/ppermute | solution.py:342
  163.8 25.4 %collective-permute-start.33 = (bf16[128,2048]{1,0:T(8,128)(2,1)S(1)}, bf16[128,2048]{1,0:T(8,128)(2,1)S(1)}, u32[]{:S(2)}, u32[]{:S(2)}) collective-permute-start(bf16[128,2048]{1,0:T(8,128)(2,1)S(1)} %broadcast_select_fusion.5), channel_id=1, source_target_pairs={{0,1},{1,0},{2,3},{3,2},{4,5},{5,4},{6,7},{7,6},{8,9},{9,8},{10,11... | collective-permute-start | bytes 1572872 | tf_op jit(solution)/shard_map/ppermute | solution.py:342
  165.0 22.9 %collective-permute-start.22 = (bf16[1024,256]{1,0:T(8,128)(2,1)}, bf16[1024,256]{1,0:T(8,128)(2,1)S(1)}, u32[]{:S(2)}, u32[]{:S(2)}) collective-permute-start(bf16[1024,256]{1,0:T(8,128)(2,1)} %get-tuple-element.54.refs_0_), channel_id=1, source_target_pairs={{2,4},{3,5},{4,2},{5,3},{10,12},{11,13},{12,10},{13,11},{18,20},{1... | collective-permute-start | bytes 1572872 | tf_op jit(solution)/shard_map/ppermute | solution.py:366
  190.0 23.8 %collective-permute-start.25 = (bf16[1024,256]{1,0:T(8,128)(2,1)S(1)}, bf16[1024,256]{1,0:T(8,128)(2,1)S(1)}, u32[]{:S(2)}, u32[]{:S(2)}) collective-permute-start(bf16[1024,256]{1,0:T(8,128)(2,1)S(1)} %collective-permute-done.21), channel_id=1, source_target_pairs={{2,0},{3,1},{4,6},{5,7},{10,8},{11,9},{12,14},{13,15},{18,16},{19,... | collective-permute-start | bytes 1572872 | tf_op jit(solution)/shard_map/ppermute | solution.py:371
  192.4 35.5 %collective-permute-start.18 = (bf16[1024,256]{1,0:T(8,128)(2,1)}, bf16[1024,256]{1,0:T(8,128)(2,1)}, u32[]{:S(2)}, u32[]{:S(2)}) collective-permute-start(bf16[1024,256]{1,0:T(8,128)(2,1)} %get-tuple-element.54.refs_0_), channel_id=1, source_target_pairs={{0,1},{1,0},{2,3},{3,2},{4,5},{5,4},{6,7},{7,6},{8,9},{9,8},{10,11... | collective-permute-start | bytes 1572872 | tf_op jit(solution)/shard_map/ppermute | solution.py:342
  200.6 27.3 %collective-permute-start.20 = (bf16[1024,256]{1,0:T(8,128)(2,1)}, bf16[1024,256]{1,0:T(8,128)(2,1)S(1)}, u32[]{:S(2)}, u32[]{:S(2)}) collective-permute-start(bf16[1024,256]{1,0:T(8,128)(2,1)} %collective-permute-done.19.refs_2_), channel_id=1, source_target_pairs={{0,1},{1,0},{2,3},{3,2},{4,5},{5,4},{6,7},{7,6},{8,9},{9,8},{10,11... | collective-permute-start | bytes 1572872 | tf_op jit(solution)/shard_map/ppermute | solution.py:342
  202.7 30.8 %collective-permute-start.24 = (bf16[1024,256]{1,0:T(8,128)(2,1)S(1)}, bf16[1024,256]{1,0:T(8,128)(2,1)S(1)}, u32[]{:S(2)}, u32[]{:S(2)}) collective-permute-start(bf16[1024,256]{1,0:T(8,128)(2,1)S(1)} %broadcast_select_fusion.1.refs_4_), channel_id=1, source_target_pairs={{0,1},{1,0},{2,3},{3,2},{4,5},{5,4},{6,7},{7,6},{8,9},{9,8},{10,11... | collective-permute-start | bytes 1572872 | tf_op jit(solution)/shard_map/ppermute | solution.py:342
  213.9 28.2 %collective-permute-start.26 = (bf16[1024,256]{1,0:T(8,128)(2,1)S(1)}, bf16[1024,256]{1,0:T(8,128)(2,1)S(1)}, u32[]{:S(2)}, u32[]{:S(2)}) collective-permute-start(bf16[1024,256]{1,0:T(8,128)(2,1)S(1)} %broadcast_select_fusion.refs_6_), channel_id=1, source_target_pairs={{0,1},{1,0},{2,3},{3,2},{4,5},{5,4},{6,7},{7,6},{8,9},{9,8},{10,11... | collective-permute-start | bytes 1572872 | tf_op jit(solution)/shard_map/ppermute | solution.py:342
  295.7 29.1 %collective-permute-start.37 = (bf16[128,2048]{1,0:T(8,128)(2,1)S(1)}, bf16[128,2048]{1,0:T(8,128)(2,1)S(1)}, u32[]{:S(2)}, u32[]{:S(2)}) collective-permute-start(bf16[128,2048]{1,0:T(8,128)(2,1)S(1)} %get-tuple-element.109), channel_id=1, source_target_pairs={{0,1},{1,0},{2,3},{3,2},{4,5},{5,4},{6,7},{7,6},{8,9},{9,8},{10,11... | collective-permute-start | bytes 1572872 | tf_op jit(solution)/shard_map/ppermute | solution.py:342
  324.4 20.7 %collective-permute-start.36 = (bf16[128,2048]{1,0:T(8,128)(2,1)S(1)}, bf16[128,2048]{1,0:T(8,128)(2,1)S(1)}, u32[]{:S(2)}, u32[]{:S(2)}) collective-permute-start(bf16[128,2048]{1,0:T(8,128)(2,1)S(1)} %get-tuple-element.106), channel_id=1, source_target_pairs={{0,1},{1,0},{2,3},{3,2},{4,5},{5,4},{6,7},{7,6},{8,9},{9,8},{10,11... | collective-permute-start | bytes 1572872 | tf_op jit(solution)/shard_map/ppermute | solution.py:342
  325.0 31.3 %collective-permute-start.40 = (bf16[128,2048]{1,0:T(8,128)(2,1)S(1)}, bf16[128,2048]{1,0:T(8,128)(2,1)S(1)}, u32[]{:S(2)}, u32[]{:S(2)}) collective-permute-start(bf16[128,2048]{1,0:T(8,128)(2,1)S(1)} %add_convert_fusion.9), channel_id=1, source_target_pairs={{0,4},{1,5},{2,6},{3,7},{4,0},{5,1},{6,2},{7,3},{8,12},{9,13},{10,... | collective-permute-start | bytes 1572872 | tf_op jit(solution)/shard_map/ppermute | solution.py:342
  335.9 20.5 %collective-permute-start.42 = (bf16[128,2048]{1,0:T(8,128)(2,1)S(1)}, bf16[128,2048]{1,0:T(8,128)(2,1)S(1)}, u32[]{:S(2)}, u32[]{:S(2)}) collective-permute-start(bf16[128,2048]{1,0:T(8,128)(2,1)S(1)} %add_convert_fusion.8), channel_id=1, source_target_pairs={{0,2},{1,3},{2,0},{3,1},{4,6},{5,7},{6,4},{7,5},{8,10},{9,11},{10,... | collective-permute-start | bytes 1572872 | tf_op jit(solution)/shard_map/ppermute | solution.py:342
  368.9 24.9 %collective-permute-start.50 = (bf16[128,2048]{1,0:T(8,128)(2,1)S(1)}, bf16[128,2048]{1,0:T(8,128)(2,1)S(1)}, u32[]{:S(2)}, u32[]{:S(2)}) collective-permute-start(bf16[128,2048]{1,0:T(8,128)(2,1)S(1)} %collective-permute-done.46), channel_id=1, source_target_pairs={{2,0},{3,1},{4,6},{5,7},{10,8},{11,9},{12,14},{13,15},{18,16},{19,... | collective-permute-start | bytes 1572872 | tf_op jit(solution)/shard_map/ppermute | solution.py:371
  370.2 25.5 %collective-permute-start.43 = (bf16[128,2048]{1,0:T(8,128)(2,1)S(1)}, bf16[128,2048]{1,0:T(8,128)(2,1)S(1)}, u32[]{:S(2)}, u32[]{:S(2)}) collective-permute-start(bf16[128,2048]{1,0:T(8,128)(2,1)S(1)} %get-tuple-element.59.refs_0_), channel_id=1, source_target_pairs={{0,1},{1,0},{2,3},{3,2},{4,5},{5,4},{6,7},{7,6},{8,9},{9,8},{10,11... | collective-permute-start | bytes 1572872 | tf_op jit(solution)/shard_map/ppermute | solution.py:342
  372.2 24.1 %collective-permute-start.45 = (bf16[128,2048]{1,0:T(8,128)(2,1)S(1)}, bf16[128,2048]{1,0:T(8,128)(2,1)S(1)}, u32[]{:S(2)}, u32[]{:S(2)}) collective-permute-start(bf16[128,2048]{1,0:T(8,128)(2,1)S(1)} %collective-permute-done.44.refs_2_), channel_id=1, source_target_pairs={{0,1},{1,0},{2,3},{3,2},{4,5},{5,4},{6,7},{7,6},{8,9},{9,8},{10,11... | collective-permute-start | bytes 1572872 | tf_op jit(solution)/shard_map/ppermute | solution.py:342
  381.6 25.8 %collective-permute-start.49 = (bf16[128,2048]{1,0:T(8,128)(2,1)S(1)}, bf16[128,2048]{1,0:T(8,128)(2,1)S(1)}, u32[]{:S(2)}, u32[]{:S(2)}) collective-permute-start(bf16[128,2048]{1,0:T(8,128)(2,1)S(1)} %broadcast_select_fusion.3.refs_4_), channel_id=1, source_target_pairs={{0,1},{1,0},{2,3},{3,2},{4,5},{5,4},{6,7},{7,6},{8,9},{9,8},{10,11... | collective-permute-start | bytes 1572872 | tf_op jit(solution)/shard_map/ppermute | solution.py:342
  393.9 19.1 %collective-permute-start.51 = (bf16[128,2048]{1,0:T(8,128)(2,1)S(1)}, bf16[128,2048]{1,0:T(8,128)(2,1)S(1)}, u32[]{:S(2)}, u32[]{:S(2)}) collective-permute-start(bf16[128,2048]{1,0:T(8,128)(2,1)S(1)} %broadcast_select_fusion.2.refs_6_), channel_id=1, source_target_pairs={{0,1},{1,0},{2,3},{3,2},{4,5},{5,4},{6,7},{7,6},{8,9},{9,8},{10,11... | collective-permute-start | bytes 1572872 | tf_op jit(solution)/shard_map/ppermute | solution.py:342
  426.4 211.3 %reduce-scatter.5.cloned.1.call-start = ((), (), s32[]{:S(2)}) async-start(), calls=%async_computation.4 | async-start | bytes 11796480 | tf_op jit(solution)/shard_map/reduce_scatter | solution.py:903
  463.9 25.0 %collective-permute-start.70 = (f32[24,2048]{1,0:T(8,128)}, f32[24,2048]{1,0:T(8,128)S(1)}, u32[]{:S(2)}, u32[]{:S(2)}) collective-permute-start(f32[24,2048]{1,0:T(8,128)} %get-tuple-element.85), channel_id=1, source_target_pairs={{0,4},{1,5},{2,6},{3,7},{4,0},{5,1},{6,2},{7,3},{8,12},{9,13},{10,... | collective-permute-start | bytes 589832 | tf_op jit(solution)/shard_map/ppermute | solution.py:346
  481.6 40.8 %collective-permute-start.61 = (bf16[128,2048]{1,0:T(8,128)(2,1)S(1)}, bf16[128,2048]{1,0:T(8,128)(2,1)S(1)}, u32[]{:S(2)}, u32[]{:S(2)}) collective-permute-start(bf16[128,2048]{1,0:T(8,128)(2,1)S(1)} %copy-done.41), channel_id=1, source_target_pairs={{0,1},{1,0},{2,3},{3,2},{4,5},{5,4},{6,7},{7,6},{8,9},{9,8},{10,11... | collective-permute-start | bytes 1572872 | tf_op jit(solution)/shard_map/ppermute | solution.py:342
  485.7 21.9 %collective-permute-start.54 = (bf16[128,2048]{1,0:T(8,128)(2,1)S(1)}, bf16[128,2048]{1,0:T(8,128)(2,1)S(1)}, u32[]{:S(2)}, u32[]{:S(2)}) collective-permute-start(bf16[128,2048]{1,0:T(8,128)(2,1)S(1)} %get-tuple-element.104), channel_id=1, source_target_pairs={{0,1},{1,0},{2,3},{3,2},{4,5},{5,4},{6,7},{7,6},{8,9},{9,8},{10,11... | collective-permute-start | bytes 1572872 | tf_op jit(solution)/shard_map/ppermute | solution.py:342
  495.1 48.0 %collective-permute-start.66 = (bf16[2,128,2048]{2,1,0:T(8,128)(2,1)S(1)}, bf16[2,128,2048]{2,1,0:T(8,128)(2,1)S(1)}, u32[]{:S(2)}, u32[]{:S(2)}) collective-permute-start(bf16[2,128,2048]{2,1,0:T(8,128)(2,1)S(1)} %dynamic-slice_bitcast_fusion), channel_id=1, source_target_pairs={{0,8},{1,9},{2,10},{3,11},{4,12},{5,13},{6,14},{7,15},{8,0},{9,1},... | collective-permute-start | bytes 3145736 | tf_op jit(solution)/shard_map/ppermute | solution.py:346
  495.6 82.5 %collective-permute-start.59 = (bf16[128,2048]{1,0:T(8,128)(2,1)S(1)}, bf16[128,2048]{1,0:T(8,128)(2,1)S(1)}, u32[]{:S(2)}, u32[]{:S(2)}) collective-permute-start(bf16[128,2048]{1,0:T(8,128)(2,1)S(1)} %copy-done.37), channel_id=1, source_target_pairs={{0,1},{1,0},{2,3},{3,2},{4,5},{5,4},{6,7},{7,6},{8,9},{9,8},{10,11... | collective-permute-start | bytes 1572872 | tf_op jit(solution)/shard_map/ppermute | solution.py:342
  497.3 73.1 %collective-permute-start.64 = (bf16[128,2048]{1,0:T(8,128)(2,1)S(1)}, bf16[128,2048]{1,0:T(8,128)(2,1)S(1)}, u32[]{:S(2)}, u32[]{:S(2)}) collective-permute-start(bf16[128,2048]{1,0:T(8,128)(2,1)S(1)} %copy-done.38), channel_id=1, source_target_pairs={{0,1},{1,0},{2,3},{3,2},{4,5},{5,4},{6,7},{7,6},{8,9},{9,8},{10,11... | collective-permute-start | bytes 1572872 | tf_op jit(solution)/shard_map/ppermute | solution.py:342
  521.5 23.8 %collective-permute-start.53 = (bf16[128,2048]{1,0:T(8,128)(2,1)S(1)}, bf16[128,2048]{1,0:T(8,128)(2,1)S(1)}, u32[]{:S(2)}, u32[]{:S(2)}) collective-permute-start(bf16[128,2048]{1,0:T(8,128)(2,1)S(1)} %get-tuple-element.105), channel_id=1, source_target_pairs={{0,1},{1,0},{2,3},{3,2},{4,5},{5,4},{6,7},{7,6},{8,9},{9,8},{10,11... | collective-permute-start | bytes 1572872 | tf_op jit(solution)/shard_map/ppermute | solution.py:342
  545.3 65.5 %collective-permute-start.52 = (bf16[128,2048]{1,0:T(8,128)(2,1)S(1)}, bf16[128,2048]{1,0:T(8,128)(2,1)S(1)}, u32[]{:S(2)}, u32[]{:S(2)}) collective-permute-start(bf16[128,2048]{1,0:T(8,128)(2,1)S(1)} %get-tuple-element.102), channel_id=1, source_target_pairs={{0,1},{1,0},{2,3},{3,2},{4,5},{5,4},{6,7},{7,6},{8,9},{9,8},{10,11... | collective-permute-start | bytes 1572872 | tf_op jit(solution)/shard_map/ppermute | solution.py:342
  570.4 38.3 %collective-permute-start.63 = (bf16[128,2048]{1,0:T(8,128)(2,1)S(1)}, bf16[128,2048]{1,0:T(8,128)(2,1)S(1)}, u32[]{:S(2)}, u32[]{:S(2)}) collective-permute-start(bf16[128,2048]{1,0:T(8,128)(2,1)S(1)} %add_convert_fusion.2), channel_id=1, source_target_pairs={{0,4},{1,5},{2,6},{3,7},{4,0},{5,1},{6,2},{7,3},{8,12},{9,13},{10,... | collective-permute-start | bytes 1572872 | tf_op jit(solution)/shard_map/ppermute | solution.py:342
  575.3 26.0 %collective-permute-start.65 = (bf16[128,2048]{1,0:T(8,128)(2,1)S(1)}, bf16[128,2048]{1,0:T(8,128)(2,1)S(1)}, u32[]{:S(2)}, u32[]{:S(2)}) collective-permute-start(bf16[128,2048]{1,0:T(8,128)(2,1)S(1)} %add_convert_fusion.1), channel_id=1, source_target_pairs={{0,2},{1,3},{2,0},{3,1},{4,6},{5,7},{6,4},{7,5},{8,10},{9,11},{10,... | collective-permute-start | bytes 1572872 | tf_op jit(solution)/shard_map/ppermute | solution.py:342
  577.3 38.9 %collective-permute-start.56 = (bf16[128,2048]{1,0:T(8,128)(2,1)S(1)}, bf16[128,2048]{1,0:T(8,128)(2,1)S(1)}, u32[]{:S(2)}, u32[]{:S(2)}) collective-permute-start(bf16[128,2048]{1,0:T(8,128)(2,1)S(1)} %add_convert_fusion.6), channel_id=1, source_target_pairs={{0,4},{1,5},{2,6},{3,7},{4,0},{5,1},{6,2},{7,3},{8,12},{9,13},{10,... | collective-permute-start | bytes 1572872 | tf_op jit(solution)/shard_map/ppermute | solution.py:342
  578.1 38.1 %collective-permute-start.58 = (bf16[128,2048]{1,0:T(8,128)(2,1)S(1)}, bf16[128,2048]{1,0:T(8,128)(2,1)S(1)}, u32[]{:S(2)}, u32[]{:S(2)}) collective-permute-start(bf16[128,2048]{1,0:T(8,128)(2,1)S(1)} %add_convert_fusion.5), channel_id=1, source_target_pairs={{0,2},{1,3},{2,0},{3,1},{4,6},{5,7},{6,4},{7,5},{8,10},{9,11},{10,... | collective-permute-start | bytes 1572872 | tf_op jit(solution)/shard_map/ppermute | solution.py:342
  601.4 31.7 %collective-permute-start.68 = (bf16[128,2048]{1,0:T(8,128)(2,1)S(1)}, bf16[128,2048]{1,0:T(8,128)(2,1)S(1)}, u32[]{:S(2)}, u32[]{:S(2)}) collective-permute-start(bf16[128,2048]{1,0:T(8,128)(2,1)S(1)} %fusion.7), channel_id=1, source_target_pairs={{0,0},{1,8},{2,16},{3,24},{4,4},{5,12},{6,20},{7,28},{8,1},{9,9},{... | collective-permute-start | bytes 1572872 | tf_op jit(solution)/shard_map/ppermute | solution.py:353
  617.4 19.4 %collective-permute-start.69 = (bf16[64,2048]{1,0:T(8,128)(2,1)}, bf16[64,2048]{1,0:T(8,128)(2,1)S(1)}, u32[]{:S(2)}, u32[]{:S(2)}) collective-permute-start(bf16[64,2048]{1,0:T(8,128)(2,1)} %reduce-scatter.3.cloned.1.call-done), channel_id=1, source_target_pairs={{0,0},{1,8},{2,16},{3,24},{4,4},{5,12},{6,20},{7,28},{8,1},{9,9},{... | collective-permute-start | bytes 786440 | tf_op jit(solution)/shard_map/ppermute | solution.py:353
  (82 other events, 1253.5 us)
Sparse Core Ops, SparseCore 0:
  10.8 90.8 all-gather.5
  104.7 88.3 all-gather.3
  426.5 44.3 reduce-scatter.2
  473.3 82.1 reduce-scatter.4

commit v3 on v2

--- a/solution.py
+++ b/solution.py
@@ -396,9 +396,10 @@
     return blocks.transpose((0, 1, 4, 3, 2, 5, 6)).reshape((32,) + v.shape)
 
 
-def sum_small(v):
-    for b in (2, 1, 3, 4, 0):
-        v = v + hop(v, 1 << b)
+def sum_small(v, gate):
+    for b in (3, 4, 0, 1, 2):
+        got = hop(v, 1 << b)
+        v = v + (after(got, gate) if b in (1, 2) else got)
     return v
 
 
@@ -416,9 +417,12 @@
     return inner
 
 
-def kernel_call(kernel, grid, in_specs, out_specs, out_shape, flops, moved, exps=0, scratch=()):
+def kernel_call(
+    kernel, grid, in_specs, out_specs, out_shape, flops, moved, exps=0, scratch=(), aliases=None
+):
     return pl.pallas_call(
         kernel,
+        input_output_aliases=aliases or {},
         grid_spec=pltpu.PrefetchScalarGridSpec(
             num_scalar_prefetch=1,
             grid=grid,
@@ -437,7 +441,7 @@
 
 def take_pair(step, odd, chunks, block):
     half = block.shape[0] // 2
-    for i in range(4):
+    for i in range(2):
 
         @pl.when(step == i)
         def _():
@@ -449,24 +453,38 @@
     return ((c[0] >> 1) ^ d, 0)
 
 
+def far_pair_at(d, c):
+    return ((c[0] >> 1) ^ (d + 2), 0)
+
+
+def anywhere(arrays):
+    return [pl.BlockSpec(memory_space=pl.ANY)] * len(arrays)
+
+
 def projection_kernel(c_ref, *refs):
-    chunks = refs[:8]
-    packed = refs[8:12]
-    wgt, g1, gq, gk, cosine, sine = refs[12:18]
-    x_out, xn_out, q_out, k_out, v_out, qr_out, kr_out, gate_out, weights = refs[18:27]
-    block = refs[27]
+    chunks = refs[:4]
+    wgt, g1, gq, gk, cosine, sine = refs[4:10]
+    first = len(refs) == 24
+    if first:
+        packed = refs[10:14]
+        outs, weights, block = refs[14:22], refs[22], refs[23]
+    else:
+        weights = refs[10]
+        outs, block = refs[19:27], refs[27]
+    x_out, xn_out, q_out, k_out, v_out, qr_out, kr_out, gate_out = outs
     d = pl.program_id(0)
-    odd = c_ref[0] & 1
-
-    @pl.when(d == 0)
-    def _():
-        for e in range(4):
-            j = c_ref[1] ^ e
-            for start, size, first in ((0, 64, 0), (256, 32, 64), (384, 32, 96)):
-                at = pl.multiple_of(start + size * j, size)
-                weights[pl.ds(at, size)] = packed[e][first : first + size]
-
-    take_pair(d, odd, chunks, block)
+
+    if first:
+
+        @pl.when(d == 0)
+        def _():
+            for e in range(4):
+                j = c_ref[1] ^ e
+                for start, size, row in ((0, 64, 0), (256, 32, 64), (384, 32, 96)):
+                    at = pl.multiple_of(start + size * j, size)
+                    weights[pl.ds(at, size)] = packed[e][row : row + size]
+
+    take_pair(d, c_ref[0] & 1, chunks, block)
     x_out[...] = block[...]
     x = block[...].astype(F32)
     xn = (x * lax.rsqrt(jnp.mean(x * x, axis=-1, keepdims=True) + EPS) * g1[...]).astype(BF16)
@@ -486,42 +504,43 @@
     kr_out[...] = turned(made[:, 2 * HD : 3 * HD], gk[...])
 
 
-def projection(c, chunks, packed, wgt, g1, gq, gk, cosine, sine):
+def projection(c, chunks, packed, wgt, g1, gq, gk, cosine, sine, before=None):
     rows, width = chunks[0].shape
     length = 8 * rows
-    at = pair_at
-    return call(
+    at = far_pair_at if before else pair_at
+    given = before or packed
+    weights = full((512, width), pipeline_mode=pl.Buffered(1))
+    columns = ((width, BF16), (width, BF16), (256, F32), (HD, F32), (HD, BF16), (256, BF16), (HD, BF16), (16, F32))
+    out_specs = [pl.BlockSpec((2 * rows, n), at) for n, _ in columns]
+    out_shape = [struct((length, n), kind) for n, kind in columns]
+    if before:
+        given = [before[8], *before[:8]]
+        given_specs = [weights, *anywhere(before[:8])]
+    else:
+        given_specs = [full((128, width), pipeline_mode=pl.Buffered(1))] * 4
+        out_specs.append(full((512, width)))
+        out_shape.append(struct((512, width), BF16))
+    made = call(
         projection_kernel,
-        (4,),
-        [full((rows, width), pipeline_mode=pl.Buffered(1))] * 8
+        (2,),
+        [full((rows, width), pipeline_mode=pl.Buffered(1))] * 4
         + [
-            *[full((128, width), pipeline_mode=pl.Buffered(1))] * 4,
             full(wgt.shape),
             full((1, width)),
             full((1, HD)),
             full((1, HD)),
             pl.BlockSpec((2 * rows, HD), at),
             pl.BlockSpec((2 * rows, HD), at),
+            *given_specs,
         ],
-        [
-            *(pl.BlockSpec((2 * rows, n), at) for n in (width, width, 2 * HD, HD, HD, 2 * HD, HD, 16)),
-            full((512, width)),
-        ],
-        [
-            struct((length, width), BF16),
-            struct((length, width), BF16),
-            struct((length, 2 * HD), F32),
-            struct((length, HD), F32),
-            struct((length, HD), BF16),
-            struct((length, 2 * HD), BF16),
-            struct((length, HD), BF16),
-            struct((length, 16), F32),
-            struct((512, width), BF16),
-        ],
-        2 * length * width * 528,
-        20 * length * width,
+        out_specs,
+        out_shape,
+        length * width * 528,
+        10 * length * width,
         scratch=[pltpu.VMEM((2 * rows, width), BF16)],
-    )(c, *chunks, *packed, wgt, g1, gq, gk, cosine, sine)
+        aliases={12 + i: i for i in range(8)} if before else None,
+    )(c, *chunks, wgt, g1, gq, gk, cosine, sine, *given)
+    return [*made, before[8]] if before else made
 
 
 def head_column(ref):
@@ -619,9 +638,9 @@
 
 
 def mixed_back_kernel(c_ref, *refs):
-    chunks = refs[:8]
-    wo, attended, gate_ref = refs[8:11]
-    all_out, att_out, logit_out = refs[11:]
+    chunks = refs[:4]
+    wo, attended, gate_ref = refs[4:7]
+    all_out, att_out, logit_out = refs[-3:]
     take_pair(pl.program_id(0), c_ref[0] & 1, chunks, all_out)
     grad = dot(all_out[...], wo[0], LAST)
     gates = gate_ref[...]
@@ -636,24 +655,26 @@
     logit_out[...] = logits.astype(BF16)
 
 
-def mixed_back(c, chunks, wo, attended, gates):
+def mixed_back(c, chunks, wo, attended, gates, before=()):
     rows, width = chunks[0].shape
     length = 8 * rows
-    at = pair_at
+    at = far_pair_at if before else pair_at
     return call(
         mixed_back_kernel,
-        (4,),
-        [full((rows, width), pipeline_mode=pl.Buffered(1))] * 8
+        (2,),
+        [full((rows, width), pipeline_mode=pl.Buffered(1))] * 4
         + [
             pl.BlockSpec((1, 256, width), lambda d, c: (2 * (c[0] & 3) + (c[0] >> 2), 0, 0)),
             pl.BlockSpec((2 * rows, 256), at),
             pl.BlockSpec((2 * rows, 16), at),
+            *anywhere(before),
         ],
         [pl.BlockSpec((2 * rows, n), at) for n in (width, 256, 16)],
         [struct((length, n), BF16) for n in (width, 256, 16)],
-        512 * length * width,
-        6 * length * width,
-    )(c, *chunks, wo.reshape(8, 256, width), attended, gates)
+        256 * length * width,
+        3 * length * width,
+        aliases={8 + i: i for i in range(3)} if before else None,
+    )(c, *chunks, wo.reshape(8, 256, width), attended, gates, *before)
 
 
 def attention_back_kernel(c_ref, *refs):
@@ -873,8 +894,10 @@
     limit = limit[:, None]
     pos = pos[None, :]
 
+    shared = (packed, wgt, g1, gq, gk, cosine, sine)
+    near = projection(cs, x_chunks[:4], *shared)
     x_all, xn1, q_pre, k_pre, value, qr, kr, gates, w_qkv = projection(
-        cs, x_chunks, packed, wgt, g1, gq, gk, cosine, sine
+        cs, x_chunks[4:], *shared, before=near
     )
     cot_chunks = gather_ctx(cotangent)
     attended, mixed, lse = attention(cs, qr, kr, value, gates, limit, pos)
@@ -909,7 +932,10 @@
     grad_hidden1 = cotangent.astype(F32) + grad_h1_norm
     grad_gain2 = jnp.sum(gain2_terms, axis=0)
     branch_chunks = gather_ctx(after(grad_hidden1.astype(BF16), *ff_grads, branch_part))
-    grad_branch_all, grad_att, grad_logits = mixed_back(cs, branch_chunks, wo, attended, gates)
+    near = mixed_back(cs, branch_chunks[:4], wo, attended, gates)
+    grad_branch_all, grad_att, grad_logits = mixed_back(
+        cs, branch_chunks[4:], wo, attended, gates, before=near
+    )
     grad_wo = outer(mixed, grad_branch_all).astype(BF16)
     branch_part = after(branch_part, *branch_chunks)
     branch = scatter_ctx(jnp.split(branch_part, 8, axis=0))
@@ -949,7 +975,7 @@
     home = turn(pieces)
     g_wq, g_wk, g_wv = (v.astype(F32) for v in jnp.split(home, (64, 96), axis=0))
 
-    bundle = sum_small(bundle)
+    bundle = sum_small(bundle, pieces)
     blocks = lax.dynamic_slice_in_dim(bundle[:18], 64 * flat, 64, 1)
     heads = lax.dynamic_slice_in_dim(bundle[18, : 2 * HD].reshape(2, HD), 4 * flat, 4, 1)
     return (

time: 657 us -> 660 us (level)
  the two profiles are of different devices: /device:TPU:24 before, /device:TPU:8 now
where the time goes in v3:
time: 660 us; the launch traced here: 650 us
  waiting for transfers between devices  314 us (48%)
  starting transfers between devices  97.5 us (15%)
  Pallas kernels  83.6 us (13%)
  matrix products  62.3 us (9%)
  other arithmetic  42.2 us (6%)
  local copies, waits for them, and re-layouts  33.7 us (5%)
  between operations  16 us (2%)
    ppermute x41, waiting for transfers between devices, swap(): return lax.ppermute(v, 'ctx', [(c, c ^ d) for c in range(8)])  158 us
    ppermute x15, waiting for transfers between devices, hop(): return lax.ppermute(v, BOTH, [(i, i ^ d) for i in range(32)])  90.1 us
    ppermute x41, starting transfers between devices, swap(): return lax.ppermute(v, 'ctx', [(c, c ^ d) for c in range(8)])  39.4 us
    dot_general x7, matrix products, outer(): lax.dot_general(left, right, (((0,), (0,)), ((), ())), preferred_element_...  35.2 us
    ppermute x4, waiting for transfers between devices, gather_ctx(): relayed = lax.ppermute(z1, 'ctx', inner)  23.5 us
    pallas_call x1, Pallas kernels, hidden(): call(hidden_kernel, (4,), [pl.BlockSpec((256, 256), lambda i, c: (i, 0))]...  17.2 us
    pallas_call x2, Pallas kernels, projection(): call(projection_kernel, (2,), [full((rows, width), pipeline_mode=pl.Buffe...  16.5 us
    ppermute x3, waiting for transfers between devices, turn(): return lax.ppermute(v, BOTH, pairs)  16.5 us
  transfers between devices with their start and end apart: 79, of which 38 were waited for; matrix products, arithmetic and copies ran while one was open for 14% of the time, Pallas kernels for 9%

profile of v3, /device:TPU:8, one launch (start us, length us, event | category | flops | bytes accessed | tf_op | source)
XLA Modules:
  0.0 649.6 jit_solution(9836811225285974831)
XLA Ops:
  27.5 10.2 %collective-permute-done.7 = bf16[32,64]{1,0:T(8,128)(2,1)S(1)} collective-permute-done((bf16[32,64]{1,0:T(8,128)(2,1)S(1)}, bf16[32,64]{1,0:T(8,128)(2,1)S(1)}, u32[]{:S(2)}, u32[]{:S(2)}) %collective-permute-start.7) | collective-permute-done | bytes 4128 | tf_op jit(solution)/shard_map/ppermute | solution.py:346
  48.5 7.4 %collective-permute-done.11 = bf16[2,2,2,2,32,64]{5,4,1,2,3,0:T(8,128)(2,1)S(1)} collective-permute-done((bf16[2,2,2,2,32,64]{5,4,1,2,3,0:T(8,128)(2,1)S(1)}, bf16[2,2,2,2,32,64]{5,4,1,2,3,0:T(8,128)(2,1)S(1)}, u32[]{:S(2)}, u32[]{:S(2)}) %collective-permute-start.11) | collective-permute-done | bytes 65568 | tf_op jit(solution)/shard_map/ppermute | solution.py:346
  64.6 8.6 %collective-permute-done.14.refs_10_ = bf16[128,2048]{1,0:T(8,128)(2,1)S(1)} collective-permute-done((bf16[128,2048]{1,0:T(8,128)(2,1)S(1)}, bf16[128,2048]{1,0:T(8,128)(2,1)S(1)}, u32[]{:S(2)}, u32[]{:S(2)}) %collective-permute-start.14) | collective-permute-done | bytes 524320 | tf_op jit(solution)/shard_map/ppermute | solution.py:353
  89.0 10.7 %collective-permute-done.16.refs_12_ = bf16[128,2048]{1,0:T(8,128)(2,1)S(1)} collective-permute-done((bf16[128,2048]{1,0:T(8,128)(2,1)S(1)}, bf16[128,2048]{1,0:T(8,128)(2,1)S(1)}, u32[]{:S(2)}, u32[]{:S(2)}) %collective-permute-start.16) | collective-permute-done | bytes 524320 | tf_op jit(solution)/shard_map/ppermute | solution.py:346
  106.8 8.7 %collective-permute-done.30 = bf16[128,2048]{1,0:T(8,128)(2,1)} collective-permute-done((bf16[128,2048]{1,0:T(8,128)(2,1)}, bf16[128,2048]{1,0:T(8,128)(2,1)}, u32[]{:S(2)}, u32[]{:S(2)}) %collective-permute-start.30) | collective-permute-done | bytes 524320 | tf_op jit(solution)/shard_map/ppermute | solution.py:368
  121.9 8.5 %shard_map.263 = (bf16[1024,2048]{1,0:T(8,128)(2,1)}, bf16[1024,2048]{1,0:T(8,128)(2,1)}, f32[1024,256]{1,0:T(8,128)}, f32[1024,128]{1,0:T(8,128)}, bf16[1024,12...) custom-call(s32[2]{0:T(128)} %pad_add_fusion.c_ref, ...), custom_call_target="tpu_custom_call" | custom-call | flops 1107296256 | bytes 20971520 | tf_op jit(solution)/shard_map/pallas_call | solution.py:523
  131.2 8.0 %shard_map.264 = (bf16[1024,2048]{1,0:T(8,128)(2,1)}, bf16[1024,2048]{1,0:T(8,128)(2,1)}, f32[1024,256]{1,0:T(8,128)}, f32[1024,128]{1,0:T(8,128)}, bf16[1024,12...) custom-call(s32[2]{0:T(128)} %pad_add_fusion.c_ref, ...), custom_call_target="tpu_custom_call", output_to_operand_aliasing={{0}: (12, {}), {1}: (13, {}), {2}: (14, {}), {3}: (15, {}),... | custom-call | flops 1107296256 | bytes 20971520 | tf_op jit(solution)/shard_map/pallas_call | solution.py:523
  139.2 10.2 %shard_map.265 = (f32[1024,256]{1,0:T(8,128)}, bf16[1024,256]{1,0:T(8,128)(2,1)}, f32[2,1024,1]{2,1,0:T(8,128)}) custom-call(s32[2]{0:T(128)} %pad_add_fusion.c_ref, s32[1024,1]{1,0:T(8,128)} %max.19.limit_ref.refs_0_, s32[1,1024]{1,0:T(1,128)} %add.204.pos_ref.refs_1_, bf16[1024,256]{1,0:T(8,128)(2,1)} %get-tuple-element.72.q_ref.refs_2_, ...), custom_call_target="tpu_custom_call" | custom-call | flops 1073741824 | bytes 2097152 | tf_op jit(solution)/shard_map/pallas_call | solution.py:568
  157.6 21.9 %collective-permute-done.19.refs_2_ = bf16[1024,256]{1,0:T(8,128)(2,1)} collective-permute-done((bf16[1024,256]{1,0:T(8,128)(2,1)}, bf16[1024,256]{1,0:T(8,128)(2,1)}, u32[]{:S(2)}, u32[]{:S(2)}) %collective-permute-start.19) | collective-permute-done | bytes 524320 | tf_op jit(solution)/shard_map/ppermute | solution.py:342
  185.1 8.2 %collective-permute-done.22 = bf16[1024,256]{1,0:T(8,128)(2,1)S(1)} collective-permute-done((bf16[1024,256]{1,0:T(8,128)(2,1)}, bf16[1024,256]{1,0:T(8,128)(2,1)S(1)}, u32[]{:S(2)}, u32[]{:S(2)}) %collective-permute-start.22) | collective-permute-done | bytes 524320 | tf_op jit(solution)/shard_map/ppermute | solution.py:366
  195.7 6.9 %collective-permute-done.21 = bf16[1024,256]{1,0:T(8,128)(2,1)S(1)} collective-permute-done((bf16[1024,256]{1,0:T(8,128)(2,1)}, bf16[1024,256]{1,0:T(8,128)(2,1)S(1)}, u32[]{:S(2)}, u32[]{:S(2)}) %collective-permute-start.21) | collective-permute-done | bytes 524320 | tf_op jit(solution)/shard_map/ppermute | solution.py:368
  209.3 5.0 collective-permute-done.25
  215.4 5.6 fusion.22
  221.3 5.1 fusion.27
  226.4 4.7 collective-permute-done.20.refs_3_
  231.2 11.2 %collective-permute-done.24.refs_5_ = bf16[1024,256]{1,0:T(8,128)(2,1)} collective-permute-done((bf16[1024,256]{1,0:T(8,128)(2,1)}, bf16[1024,256]{1,0:T(8,128)(2,1)}, u32[]{:S(2)}, u32[]{:S(2)}) %collective-permute-start.24) | collective-permute-done | bytes 524320 | tf_op jit(solution)/shard_map/ppermute | solution.py:342
  242.4 9.0 %collective-permute-done.26.refs_7_ = bf16[1024,256]{1,0:T(8,128)(2,1)} collective-permute-done((bf16[1024,256]{1,0:T(8,128)(2,1)}, bf16[1024,256]{1,0:T(8,128)(2,1)}, u32[]{:S(2)}, u32[]{:S(2)}) %collective-permute-start.26) | collective-permute-done | bytes 524320 | tf_op jit(solution)/shard_map/ppermute | solution.py:342
  251.4 17.2 %shard_map.266 = (bf16[1024,2048]{1,0:T(8,128)(2,1)}, f32[128,2048]{1,0:T(8,128)}) custom-call(s32[2]{0:T(128)} %pad_add_fusion.c_ref, bf16[1024,256]{1,0:T(8,128)(2,1)} %get-tuple-element.76.refs_0_, bf16[1024,256]{1,0:T(8,128)(2,1)} %collective-permute-done.18.refs_1_, bf16[1024,256]{1,0:T(8,128)(2,1)} %collective-permute-done.19.refs_2_, ...), custom_call_target="tpu_custom_call" | custom-call | flops 8589934592 | bytes 25165824 | tf_op jit(solution)/shard_map/pallas_call | solution.py:623
  268.7 5.4 fusion.26
  278.6 15.6 %convolution_convert_fusion.2 = bf16[768,2048]{1,0:T(8,128)(2,1)} fusion(bf16[1024,768]{1,0:T(8,128)(2,1)S(1)} %get-tuple-element.125, bf16[1024,2048]{1,0:T(8,128)(2,1)S(1)} %copy-done.45), kind=kOutput, calls=%fused_computation.4 | convolution fusion | flops 3222798336 | bytes 8912896 | tf_op jit(solution)/shard_map/dot_general | solution.py:52
  303.6 4.9 convolution_convert_fusion.3
  308.6 7.8 %collective-permute-done.38 = bf16[128,2048]{1,0:T(8,128)(2,1)S(1)} collective-permute-done((bf16[128,2048]{1,0:T(8,128)(2,1)S(1)}, bf16[128,2048]{1,0:T(8,128)(2,1)S(1)}, u32[]{:S(2)}, u32[]{:S(2)}) %collective-permute-start.38) | collective-permute-done | bytes 524320 | tf_op jit(solution)/shard_map/ppermute | solution.py:342
  316.6 4.9 convolution_convert_fusion.1
  331.9 7.0 %collective-permute-done.41 = bf16[128,2048]{1,0:T(8,128)(2,1)S(1)} collective-permute-done((bf16[128,2048]{1,0:T(8,128)(2,1)S(1)}, bf16[128,2048]{1,0:T(8,128)(2,1)S(1)}, u32[]{:S(2)}, u32[]{:S(2)}) %collective-permute-start.41) | collective-permute-done | bytes 524320 | tf_op jit(solution)/shard_map/ppermute | solution.py:342
  339.1 5.0 convolution_convert_fusion
  347.0 7.0 %collective-permute-done.42 = bf16[128,2048]{1,0:T(8,128)(2,1)S(1)} collective-permute-done((bf16[128,2048]{1,0:T(8,128)(2,1)S(1)}, bf16[128,2048]{1,0:T(8,128)(2,1)S(1)}, u32[]{:S(2)}, u32[]{:S(2)}) %collective-permute-start.42) | collective-permute-done | bytes 524320 | tf_op jit(solution)/shard_map/ppermute | solution.py:342
  361.3 4.8 collective-permute-done.44.refs_2_
  366.0 4.7 collective-permute-start.46
  373.8 7.8 %collective-permute-done.46 = bf16[128,2048]{1,0:T(8,128)(2,1)S(1)} collective-permute-done((bf16[128,2048]{1,0:T(8,128)(2,1)S(1)}, bf16[128,2048]{1,0:T(8,128)(2,1)S(1)}, u32[]{:S(2)}, u32[]{:S(2)}) %collective-permute-start.46) | collective-permute-done | bytes 524320 | tf_op jit(solution)/shard_map/ppermute | solution.py:368
  385.6 7.1 %collective-permute-done.50 = bf16[128,2048]{1,0:T(8,128)(2,1)S(1)} collective-permute-done((bf16[128,2048]{1,0:T(8,128)(2,1)S(1)}, bf16[128,2048]{1,0:T(8,128)(2,1)S(1)}, u32[]{:S(2)}, u32[]{:S(2)}) %collective-permute-start.50) | collective-permute-done | bytes 524320 | tf_op jit(solution)/shard_map/ppermute | solution.py:371
  393.1 4.8 collective-permute-done.43.refs_1_
  397.9 11.2 %collective-permute-done.45.refs_3_ = bf16[128,2048]{1,0:T(8,128)(2,1)S(1)} collective-permute-done((bf16[128,2048]{1,0:T(8,128)(2,1)S(1)}, bf16[128,2048]{1,0:T(8,128)(2,1)S(1)}, u32[]{:S(2)}, u32[]{:S(2)}) %collective-permute-start.45) | collective-permute-done | bytes 524320 | tf_op jit(solution)/shard_map/ppermute | solution.py:342
  409.9 5.1 shard_map.267
  415.0 5.4 collective-permute-done.49.refs_1_
  420.4 8.3 %collective-permute-done.51.refs_3_ = bf16[128,2048]{1,0:T(8,128)(2,1)} collective-permute-done((bf16[128,2048]{1,0:T(8,128)(2,1)S(1)}, bf16[128,2048]{1,0:T(8,128)(2,1)}, u32[]{:S(2)}, u32[]{:S(2)}) %collective-permute-start.51) | collective-permute-done | bytes 524320 | tf_op jit(solution)/shard_map/ppermute | solution.py:342
  428.7 5.2 shard_map.268
  438.8 7.8 %pad_maximum_fusion = bf16[4,576,2048]{2,1,0:T(8,128)(2,1)} fusion(bf16[4,192,2048]{2,1,0:T(8,128)(2,1)} %bitcast.113, bf16[4,192,2048]{2,1,0:T(8,128)(2,1)} %bitcast.111, bf16[4,192,2048]{2,1,0:T(8,128)(2,1)} %bitcast.112), kind=kLoop, calls=%fused_computation | loop fusion | flops 28311552 | bytes 18874368 | tf_op jit(solution)/shard_map/concatenate | solution.py:925
  451.7 14.3 %shard_map.269 = (bf16[1024,256]{1,0:T(8,128)(2,1)}, bf16[1024,128]{1,0:T(8,128)(2,1)}, bf16[1024,128]{1,0:T(8,128)(2,1)}, f32[8,128]{1,0:T(8,128)}) custom-call(s32[2]{0:T(128)} %pad_add_fusion.c_ref, s32[1024,1]{1,0:T(8,128)} %max.19.limit_ref.refs_0_, s32[1,1024]{1,0:T(1,128)} %add.204.pos_ref.refs_1_, bf16[1024,256]{1,0:T(8,128)(2,1)} %get-tuple-element.72.q_ref.refs_2_, ...), custom_call_target="tpu_custom_call" | custom-call | flops 2684354560 | bytes 5242880 | tf_op jit(solution)/shard_map/pallas_call | solution.py:730
  467.4 6.9 %shard_map.270 = (bf16[128,2048]{1,0:T(8,128)(2,1)}, bf16[128,2048]{1,0:T(8,128)(2,1)}, bf16[128,2048]{1,0:T(8,128)(2,1)}, bf16[128,2048]{1,0:T(8,128)(2,1)}, f32[24,2048]{1,0:T(8,128)}) custom-call(s32[2]{0:T(128)} %pad_add_fusion.c_ref, bf16[1024,256]{1,0:T(8,128)(2,1)} %get-tuple-element.92.refs_0_, bf16[1024,128]{1,0:T(8,128)(2,1)} %get-tuple-element.93.refs_1_, ...), custom_call_target="tpu_custom_call" | custom-call | flops 1107296256 | bytes 8388608 | tf_op jit(solution)/shard_map/pallas_call | solution.py:807
  474.3 8.0 %shard_map.271 = (bf16[128,2048]{1,0:T(8,128)(2,1)}, bf16[128,2048]{1,0:T(8,128)(2,1)}, bf16[128,2048]{1,0:T(8,128)(2,1)}, bf16[128,2048]{1,0:T(8,128)(2,1)}, f32[24,2048]{1,0:T(8,128)}) custom-call(s32[2]{0:T(128)} %pad_add_fusion.c_ref, bf16[1024,256]{1,0:T(8,128)(2,1)} %get-tuple-element.92.refs_0_, bf16[1024,128]{1,0:T(8,128)(2,1)} %get-tuple-element.93.refs_1_, ...), custom_call_target="tpu_custom_call" | custom-call | flops 1107296256 | bytes 8388608 | tf_op jit(solution)/shard_map/pallas_call | solution.py:807
  492.3 8.9 %collective-permute-done.71 = f32[24,2048]{1,0:T(8,128)S(1)} collective-permute-done((f32[24,2048]{1,0:T(8,128)S(1)}, f32[24,2048]{1,0:T(8,128)S(1)}, u32[]{:S(2)}, u32[]{:S(2)}) %collective-permute-start.71) | collective-permute-done | bytes 196640 | tf_op jit(solution)/shard_map/ppermute | solution.py:346
  504.7 14.5 %collective-permute-done.72 = f32[24,2048]{1,0:T(8,128)S(1)} collective-permute-done((f32[24,2048]{1,0:T(8,128)S(1)}, f32[24,2048]{1,0:T(8,128)S(1)}, u32[]{:S(2)}, u32[]{:S(2)}) %collective-permute-start.72) | collective-permute-done | bytes 196640 | tf_op jit(solution)/shard_map/ppermute | solution.py:346
  526.3 28.3 %collective-permute-done.60 = bf16[128,2048]{1,0:T(8,128)(2,1)S(1)} collective-permute-done((bf16[128,2048]{1,0:T(8,128)(2,1)}, bf16[128,2048]{1,0:T(8,128)(2,1)S(1)}, u32[]{:S(2)}, u32[]{:S(2)}) %collective-permute-start.60) | collective-permute-done | bytes 524320 | tf_op jit(solution)/shard_map/ppermute | solution.py:342
  562.3 5.7 collective-permute-done.67
  568.2 18.9 %collective-permute-done.73 = f32[24,2048]{1,0:T(8,128)S(1)} collective-permute-done((f32[24,2048]{1,0:T(8,128)S(1)}, f32[24,2048]{1,0:T(8,128)S(1)}, u32[]{:S(2)}, u32[]{:S(2)}) %collective-permute-start.73) | collective-permute-done | bytes 196640 | tf_op jit(solution)/shard_map/ppermute | solution.py:346
  597.0 18.6 %collective-permute-done.58 = bf16[128,2048]{1,0:T(8,128)(2,1)S(1)} collective-permute-done((bf16[128,2048]{1,0:T(8,128)(2,1)S(1)}, bf16[128,2048]{1,0:T(8,128)(2,1)S(1)}, u32[]{:S(2)}, u32[]{:S(2)}) %collective-permute-start.58) | collective-permute-done | bytes 524320 | tf_op jit(solution)/shard_map/ppermute | solution.py:342
  617.9 6.7 %collective-permute-done.74 = f32[24,2048]{1,0:T(8,128)S(1)} collective-permute-done((f32[24,2048]{1,0:T(8,128)S(1)}, f32[24,2048]{1,0:T(8,128)S(1)}, u32[]{:S(2)}, u32[]{:S(2)}) %collective-permute-start.74) | collective-permute-done | bytes 196640 | tf_op jit(solution)/shard_map/ppermute | solution.py:346
  630.0 7.9 %collective-permute-done.69 = bf16[64,2048]{1,0:T(8,128)(2,1)S(1)} collective-permute-done((bf16[64,2048]{1,0:T(8,128)(2,1)}, bf16[64,2048]{1,0:T(8,128)(2,1)S(1)}, u32[]{:S(2)}, u32[]{:S(2)}) %collective-permute-start.69) | collective-permute-done | bytes 262176 | tf_op jit(solution)/shard_map/ppermute | solution.py:353
  (333 shorter events, 197.6 us)
Async XLA Ops:
  7.3 208.1 %all-gather.6.cloned.1.call-start = ((), (), s32[]{:S(2)}) async-start(), calls=%async_computation.5 | async-start | bytes 11796480 | tf_op jit(solution)/shard_map/all_gather | solution.py:881
  10.7 240.7 %all-gather.4.cloned.1.call-start = ((), (), s32[]{:S(2)}) async-start(), calls=%async_computation.2 | async-start | bytes 8650752 | tf_op jit(solution)/shard_map/all_gather | solution.py:883
  11.4 615.0 %reduce-scatter.3.cloned.1.call-start = ((), (), s32[]{:S(2)}) async-start(), calls=%async_computation.3 | async-start | bytes 1310720 | tf_op jit(solution)/shard_map/reduce_scatter | solution.py:960
  11.5 63.6 %collective-permute-start.28 = (bf16[128,2048]{1,0:T(8,128)(2,1)S(1)}, bf16[128,2048]{1,0:T(8,128)(2,1)}, u32[]{:S(2)}, u32[]{:S(2)}) collective-permute-start(bf16[128,2048]{1,0:T(8,128)(2,1)S(1)} %copy-done.12), channel_id=1, source_target_pairs={{0,2},{1,3},{2,0},{3,1},{4,6},{5,7},{6,4},{7,5},{8,10},{9,11},{10,... | collective-permute-start | bytes 1572872 | tf_op jit(solution)/shard_map/ppermute | solution.py:342
  11.6 70.4 %collective-permute-start.27 = (bf16[128,2048]{1,0:T(8,128)(2,1)S(1)}, bf16[128,2048]{1,0:T(8,128)(2,1)}, u32[]{:S(2)}, u32[]{:S(2)}) collective-permute-start(bf16[128,2048]{1,0:T(8,128)(2,1)S(1)} %copy-done.12), channel_id=1, source_target_pairs={{0,1},{1,0},{2,3},{3,2},{4,5},{5,4},{6,7},{7,6},{8,9},{9,8},{10,11... | collective-permute-start | bytes 1572872 | tf_op jit(solution)/shard_map/ppermute | solution.py:342
  13.5 47.6 %collective-permute-start.2 = (bf16[128,2048]{1,0:T(8,128)(2,1)S(1)}, bf16[128,2048]{1,0:T(8,128)(2,1)}, u32[]{:S(2)}, u32[]{:S(2)}) collective-permute-start(bf16[128,2048]{1,0:T(8,128)(2,1)S(1)} %copy-done.2), channel_id=1, source_target_pairs={{2,4},{3,5},{4,2},{5,3},{10,12},{11,13},{12,10},{13,11},{18,20},{1... | collective-permute-start | bytes 1572872 | tf_op jit(solution)/shard_map/ppermute | solution.py:366
  18.1 40.9 %collective-permute-start = (bf16[128,2048]{1,0:T(8,128)(2,1)S(1)}, bf16[128,2048]{1,0:T(8,128)(2,1)S(1)}, u32[]{:S(2)}, u32[]{:S(2)}) collective-permute-start(bf16[128,2048]{1,0:T(8,128)(2,1)S(1)} %copy-done.2), channel_id=1, source_target_pairs={{0,2},{1,3},{2,0},{3,1},{4,6},{5,7},{6,4},{7,5},{8,10},{9,11},{10,... | collective-permute-start | bytes 1572872 | tf_op jit(solution)/shard_map/ppermute | solution.py:342
  61.2 22.6 %collective-permute-start.3 = (bf16[128,2048]{1,0:T(8,128)(2,1)}, bf16[128,2048]{1,0:T(8,128)(2,1)}, u32[]{:S(2)}, u32[]{:S(2)}) collective-permute-start(bf16[128,2048]{1,0:T(8,128)(2,1)} %collective-permute-done.2), channel_id=1, source_target_pairs={{2,0},{3,1},{4,6},{5,7},{10,8},{11,9},{12,14},{13,15},{18,16},{19,... | collective-permute-start | bytes 1572872 | tf_op jit(solution)/shard_map/ppermute | solution.py:369
  75.1 24.6 %collective-permute-start.16 = (bf16[128,2048]{1,0:T(8,128)(2,1)S(1)}, bf16[128,2048]{1,0:T(8,128)(2,1)S(1)}, u32[]{:S(2)}, u32[]{:S(2)}) collective-permute-start(bf16[128,2048]{1,0:T(8,128)(2,1)S(1)} %collective-permute-done.14.refs_10_), channel_id=1, source_target_pairs={{0,16},{1,17},{2,18},{3,19},{4,20},{5,21},{6,22},{7,23},{8,24},{9,... | collective-permute-start | bytes 1572872 | tf_op jit(solution)/shard_map/ppermute | solution.py:346
  77.1 24.5 %collective-permute-start.5 = (bf16[128,2048]{1,0:T(8,128)(2,1)}, bf16[128,2048]{1,0:T(8,128)(2,1)}, u32[]{:S(2)}, u32[]{:S(2)}) collective-permute-start(bf16[128,2048]{1,0:T(8,128)(2,1)} %collective-permute-done.1), channel_id=1, source_target_pairs={{2,0},{3,1},{4,6},{5,7},{10,8},{11,9},{12,14},{13,15},{18,16},{19,... | collective-permute-start | bytes 1572872 | tf_op jit(solution)/shard_map/ppermute | solution.py:371
  88.7 30.8 %collective-permute-start.13 = (bf16[128,2048]{1,0:T(8,128)(2,1)S(1)}, bf16[128,2048]{1,0:T(8,128)(2,1)S(1)}, u32[]{:S(2)}, u32[]{:S(2)}) collective-permute-start(bf16[128,2048]{1,0:T(8,128)(2,1)S(1)} %collective-permute-done.refs_2_), channel_id=1, source_target_pairs={{0,1},{1,0},{2,3},{3,2},{4,5},{5,4},{6,7},{7,6},{8,9},{9,8},{10,11... | collective-permute-start | bytes 1572872 | tf_op jit(solution)/shard_map/ppermute | solution.py:342
  102.8 27.6 %collective-permute-start.4 = (bf16[128,2048]{1,0:T(8,128)(2,1)S(1)}, bf16[128,2048]{1,0:T(8,128)(2,1)S(1)}, u32[]{:S(2)}, u32[]{:S(2)}) collective-permute-start(bf16[128,2048]{1,0:T(8,128)(2,1)S(1)} %broadcast_select_fusion.7.refs_0_), channel_id=1, source_target_pairs={{0,1},{1,0},{2,3},{3,2},{4,5},{5,4},{6,7},{7,6},{8,9},{9,8},{10,11... | collective-permute-start | bytes 1572872 | tf_op jit(solution)/shard_map/ppermute | solution.py:342
  104.4 26.7 %collective-permute-start.6 = (bf16[128,2048]{1,0:T(8,128)(2,1)S(1)}, bf16[128,2048]{1,0:T(8,128)(2,1)}, u32[]{:S(2)}, u32[]{:S(2)}) collective-permute-start(bf16[128,2048]{1,0:T(8,128)(2,1)S(1)} %broadcast_select_fusion.6.refs_2_), channel_id=1, source_target_pairs={{0,1},{1,0},{2,3},{3,2},{4,5},{5,4},{6,7},{7,6},{8,9},{9,8},{10,11... | collective-permute-start | bytes 1572872 | tf_op jit(solution)/shard_map/ppermute | solution.py:342
  115.6 33.9 %collective-permute-start.32 = (bf16[128,2048]{1,0:T(8,128)(2,1)}, bf16[128,2048]{1,0:T(8,128)(2,1)}, u32[]{:S(2)}, u32[]{:S(2)}) collective-permute-start(bf16[128,2048]{1,0:T(8,128)(2,1)} %collective-permute-done.31), channel_id=1, source_target_pairs={{2,0},{3,1},{4,6},{5,7},{10,8},{11,9},{12,14},{13,15},{18,16},{19,... | collective-permute-start | bytes 1572872 | tf_op jit(solution)/shard_map/ppermute | solution.py:369
  119.5 32.9 %collective-permute-start.29 = (bf16[128,2048]{1,0:T(8,128)(2,1)}, bf16[128,2048]{1,0:T(8,128)(2,1)}, u32[]{:S(2)}, u32[]{:S(2)}) collective-permute-start(bf16[128,2048]{1,0:T(8,128)(2,1)} %collective-permute-done.28), channel_id=1, source_target_pairs={{0,1},{1,0},{2,3},{3,2},{4,5},{5,4},{6,7},{7,6},{8,9},{9,8},{10,11... | collective-permute-start | bytes 1572872 | tf_op jit(solution)/shard_map/ppermute | solution.py:342
  119.7 63.3 %collective-permute-start.34 = (bf16[128,2048]{1,0:T(8,128)(2,1)}, bf16[128,2048]{1,0:T(8,128)(2,1)}, u32[]{:S(2)}, u32[]{:S(2)}) collective-permute-start(bf16[128,2048]{1,0:T(8,128)(2,1)} %collective-permute-done.30), channel_id=1, source_target_pairs={{2,0},{3,1},{4,6},{5,7},{10,8},{11,9},{12,14},{13,15},{18,16},{19,... | collective-permute-start | bytes 1572872 | tf_op jit(solution)/shard_map/ppermute | solution.py:371
  149.5 30.0 %collective-permute-start.19 = (bf16[1024,256]{1,0:T(8,128)(2,1)}, bf16[1024,256]{1,0:T(8,128)(2,1)}, u32[]{:S(2)}, u32[]{:S(2)}) collective-permute-start(bf16[1024,256]{1,0:T(8,128)(2,1)} %get-tuple-element.76.refs_0_), channel_id=1, source_target_pairs={{0,2},{1,3},{2,0},{3,1},{4,6},{5,7},{6,4},{7,5},{8,10},{9,11},{10,... | collective-permute-start | bytes 1572872 | tf_op jit(solution)/shard_map/ppermute | solution.py:342
  150.6 44.2 %collective-permute-start.33 = (bf16[128,2048]{1,0:T(8,128)(2,1)S(1)}, bf16[128,2048]{1,0:T(8,128)(2,1)S(1)}, u32[]{:S(2)}, u32[]{:S(2)}) collective-permute-start(bf16[128,2048]{1,0:T(8,128)(2,1)S(1)} %broadcast_select_fusion.5), channel_id=1, source_target_pairs={{0,1},{1,0},{2,3},{3,2},{4,5},{5,4},{6,7},{7,6},{8,9},{9,8},{10,11... | collective-permute-start | bytes 1572872 | tf_op jit(solution)/shard_map/ppermute | solution.py:342
  154.3 39.0 %collective-permute-start.22 = (bf16[1024,256]{1,0:T(8,128)(2,1)}, bf16[1024,256]{1,0:T(8,128)(2,1)S(1)}, u32[]{:S(2)}, u32[]{:S(2)}) collective-permute-start(bf16[1024,256]{1,0:T(8,128)(2,1)} %get-tuple-element.76.refs_0_), channel_id=1, source_target_pairs={{2,4},{3,5},{4,2},{5,3},{10,12},{11,13},{12,10},{13,11},{18,20},{1... | collective-permute-start | bytes 1572872 | tf_op jit(solution)/shard_map/ppermute | solution.py:366
  179.5 23.1 %collective-permute-start.21 = (bf16[1024,256]{1,0:T(8,128)(2,1)}, bf16[1024,256]{1,0:T(8,128)(2,1)S(1)}, u32[]{:S(2)}, u32[]{:S(2)}) collective-permute-start(bf16[1024,256]{1,0:T(8,128)(2,1)} %collective-permute-done.19.refs_2_), channel_id=1, source_target_pairs={{2,4},{3,5},{4,2},{5,3},{10,12},{11,13},{12,10},{13,11},{18,20},{1... | collective-permute-start | bytes 1572872 | tf_op jit(solution)/shard_map/ppermute | solution.py:368
  184.1 21.5 %collective-permute-start.35 = (bf16[128,2048]{1,0:T(8,128)(2,1)S(1)}, bf16[128,2048]{1,0:T(8,128)(2,1)S(1)}, u32[]{:S(2)}, u32[]{:S(2)}) collective-permute-start(bf16[128,2048]{1,0:T(8,128)(2,1)S(1)} %broadcast_select_fusion.4), channel_id=1, source_target_pairs={{0,1},{1,0},{2,3},{3,2},{4,5},{5,4},{6,7},{7,6},{8,9},{9,8},{10,11... | collective-permute-start | bytes 1572872 | tf_op jit(solution)/shard_map/ppermute | solution.py:342
  204.8 21.6 %collective-permute-start.18 = (bf16[1024,256]{1,0:T(8,128)(2,1)}, bf16[1024,256]{1,0:T(8,128)(2,1)}, u32[]{:S(2)}, u32[]{:S(2)}) collective-permute-start(bf16[1024,256]{1,0:T(8,128)(2,1)} %get-tuple-element.76.refs_0_), channel_id=1, source_target_pairs={{0,1},{1,0},{2,3},{3,2},{4,5},{5,4},{6,7},{7,6},{8,9},{9,8},{10,11... | collective-permute-start | bytes 1572872 | tf_op jit(solution)/shard_map/ppermute | solution.py:342
  206.4 24.7 %collective-permute-start.20 = (bf16[1024,256]{1,0:T(8,128)(2,1)}, bf16[1024,256]{1,0:T(8,128)(2,1)}, u32[]{:S(2)}, u32[]{:S(2)}) collective-permute-start(bf16[1024,256]{1,0:T(8,128)(2,1)} %collective-permute-done.19.refs_2_), channel_id=1, source_target_pairs={{0,1},{1,0},{2,3},{3,2},{4,5},{5,4},{6,7},{7,6},{8,9},{9,8},{10,11... | collective-permute-start | bytes 1572872 | tf_op jit(solution)/shard_map/ppermute | solution.py:342
  208.5 33.9 %collective-permute-start.24 = (bf16[1024,256]{1,0:T(8,128)(2,1)}, bf16[1024,256]{1,0:T(8,128)(2,1)}, u32[]{:S(2)}, u32[]{:S(2)}) collective-permute-start(bf16[1024,256]{1,0:T(8,128)(2,1)} %broadcast_select_fusion.1.refs_4_), channel_id=1, source_target_pairs={{0,1},{1,0},{2,3},{3,2},{4,5},{5,4},{6,7},{7,6},{8,9},{9,8},{10,11... | collective-permute-start | bytes 1572872 | tf_op jit(solution)/shard_map/ppermute | solution.py:342
  215.1 36.2 %collective-permute-start.26 = (bf16[1024,256]{1,0:T(8,128)(2,1)}, bf16[1024,256]{1,0:T(8,128)(2,1)}, u32[]{:S(2)}, u32[]{:S(2)}) collective-permute-start(bf16[1024,256]{1,0:T(8,128)(2,1)} %broadcast_select_fusion.refs_6_), channel_id=1, source_target_pairs={{0,1},{1,0},{2,3},{3,2},{4,5},{5,4},{6,7},{7,6},{8,9},{9,8},{10,11... | collective-permute-start | bytes 1572872 | tf_op jit(solution)/shard_map/ppermute | solution.py:342
  301.9 25.7 %collective-permute-start.37 = (bf16[128,2048]{1,0:T(8,128)(2,1)S(1)}, bf16[128,2048]{1,0:T(8,128)(2,1)S(1)}, u32[]{:S(2)}, u32[]{:S(2)}) collective-permute-start(bf16[128,2048]{1,0:T(8,128)(2,1)S(1)} %get-tuple-element.135), channel_id=1, source_target_pairs={{0,1},{1,0},{2,3},{3,2},{4,5},{5,4},{6,7},{7,6},{8,9},{9,8},{10,11... | collective-permute-start | bytes 1572872 | tf_op jit(solution)/shard_map/ppermute | solution.py:342
  322.0 25.0 %collective-permute-start.36 = (bf16[128,2048]{1,0:T(8,128)(2,1)S(1)}, bf16[128,2048]{1,0:T(8,128)(2,1)S(1)}, u32[]{:S(2)}, u32[]{:S(2)}) collective-permute-start(bf16[128,2048]{1,0:T(8,128)(2,1)S(1)} %get-tuple-element.132), channel_id=1, source_target_pairs={{0,1},{1,0},{2,3},{3,2},{4,5},{5,4},{6,7},{7,6},{8,9},{9,8},{10,11... | collective-permute-start | bytes 1572872 | tf_op jit(solution)/shard_map/ppermute | solution.py:342
  327.9 26.1 %collective-permute-start.40 = (bf16[128,2048]{1,0:T(8,128)(2,1)S(1)}, bf16[128,2048]{1,0:T(8,128)(2,1)S(1)}, u32[]{:S(2)}, u32[]{:S(2)}) collective-permute-start(bf16[128,2048]{1,0:T(8,128)(2,1)S(1)} %add_convert_fusion.9), channel_id=1, source_target_pairs={{0,4},{1,5},{2,6},{3,7},{4,0},{5,1},{6,2},{7,3},{8,12},{9,13},{10,... | collective-permute-start | bytes 1572872 | tf_op jit(solution)/shard_map/ppermute | solution.py:342
  383.4 25.7 %collective-permute-start.45 = (bf16[128,2048]{1,0:T(8,128)(2,1)S(1)}, bf16[128,2048]{1,0:T(8,128)(2,1)S(1)}, u32[]{:S(2)}, u32[]{:S(2)}) collective-permute-start(bf16[128,2048]{1,0:T(8,128)(2,1)S(1)} %collective-permute-done.44.refs_2_), channel_id=1, source_target_pairs={{0,1},{1,0},{2,3},{3,2},{4,5},{5,4},{6,7},{7,6},{8,9},{9,8},{10,11... | collective-permute-start | bytes 1572872 | tf_op jit(solution)/shard_map/ppermute | solution.py:342
  385.2 35.3 %collective-permute-start.49 = (bf16[128,2048]{1,0:T(8,128)(2,1)S(1)}, bf16[128,2048]{1,0:T(8,128)(2,1)}, u32[]{:S(2)}, u32[]{:S(2)}) collective-permute-start(bf16[128,2048]{1,0:T(8,128)(2,1)S(1)} %broadcast_select_fusion.3.refs_0_), channel_id=1, source_target_pairs={{0,1},{1,0},{2,3},{3,2},{4,5},{5,4},{6,7},{7,6},{8,9},{9,8},{10,11... | collective-permute-start | bytes 1572872 | tf_op jit(solution)/shard_map/ppermute | solution.py:342
  392.7 36.1 %collective-permute-start.51 = (bf16[128,2048]{1,0:T(8,128)(2,1)S(1)}, bf16[128,2048]{1,0:T(8,128)(2,1)}, u32[]{:S(2)}, u32[]{:S(2)}) collective-permute-start(bf16[128,2048]{1,0:T(8,128)(2,1)S(1)} %broadcast_select_fusion.2.refs_2_), channel_id=1, source_target_pairs={{0,1},{1,0},{2,3},{3,2},{4,5},{5,4},{6,7},{7,6},{8,9},{9,8},{10,11... | collective-permute-start | bytes 1572872 | tf_op jit(solution)/shard_map/ppermute | solution.py:342
  438.6 200.2 %reduce-scatter.5.cloned.1.call-start = ((), (), s32[]{:S(2)}) async-start(), calls=%async_computation.4 | async-start | bytes 11796480 | tf_op jit(solution)/shard_map/reduce_scatter | solution.py:926
  449.6 39.7 %collective-permute-start.54 = (bf16[128,2048]{1,0:T(8,128)(2,1)}, bf16[128,2048]{1,0:T(8,128)(2,1)}, u32[]{:S(2)}, u32[]{:S(2)}) collective-permute-start(bf16[128,2048]{1,0:T(8,128)(2,1)} %get-tuple-element.130), channel_id=1, source_target_pairs={{0,1},{1,0},{2,3},{3,2},{4,5},{5,4},{6,7},{7,6},{8,9},{9,8},{10,11... | collective-permute-start | bytes 1572872 | tf_op jit(solution)/shard_map/ppermute | solution.py:342
  450.0 70.8 %collective-permute-start.53 = (bf16[128,2048]{1,0:T(8,128)(2,1)}, bf16[128,2048]{1,0:T(8,128)(2,1)}, u32[]{:S(2)}, u32[]{:S(2)}) collective-permute-start(bf16[128,2048]{1,0:T(8,128)(2,1)} %get-tuple-element.131), channel_id=1, source_target_pairs={{0,1},{1,0},{2,3},{3,2},{4,5},{5,4},{6,7},{7,6},{8,9},{9,8},{10,11... | collective-permute-start | bytes 1572872 | tf_op jit(solution)/shard_map/ppermute | solution.py:342
  489.1 35.5 %collective-permute-start.66 = (bf16[2,128,2048]{2,1,0:T(8,128)(2,1)}, bf16[2,128,2048]{2,1,0:T(8,128)(2,1)}, u32[]{:S(2)}, u32[]{:S(2)}) collective-permute-start(bf16[2,128,2048]{2,1,0:T(8,128)(2,1)} %dynamic-slice_bitcast_fusion), channel_id=1, source_target_pairs={{0,8},{1,9},{2,10},{3,11},{4,12},{5,13},{6,14},{7,15},{8,0},{9,1},... | collective-permute-start | bytes 3145736 | tf_op jit(solution)/shard_map/ppermute | solution.py:346
  491.5 29.8 %collective-permute-start.55 = (bf16[128,2048]{1,0:T(8,128)(2,1)}, bf16[128,2048]{1,0:T(8,128)(2,1)}, u32[]{:S(2)}, u32[]{:S(2)}) collective-permute-start(bf16[128,2048]{1,0:T(8,128)(2,1)} %add_convert_fusion.7), channel_id=1, source_target_pairs={{0,2},{1,3},{2,0},{3,1},{4,6},{5,7},{6,4},{7,5},{8,10},{9,11},{10,... | collective-permute-start | bytes 1572872 | tf_op jit(solution)/shard_map/ppermute | solution.py:342
  501.1 95.8 %collective-permute-start.52 = (bf16[128,2048]{1,0:T(8,128)(2,1)}, bf16[128,2048]{1,0:T(8,128)(2,1)S(1)}, u32[]{:S(2)}, u32[]{:S(2)}) collective-permute-start(bf16[128,2048]{1,0:T(8,128)(2,1)} %get-tuple-element.128), channel_id=1, source_target_pairs={{0,1},{1,0},{2,3},{3,2},{4,5},{5,4},{6,7},{7,6},{8,9},{9,8},{10,11... | collective-permute-start | bytes 1572872 | tf_op jit(solution)/shard_map/ppermute | solution.py:342
  519.1 38.3 %collective-permute-start.57 = (bf16[128,2048]{1,0:T(8,128)(2,1)}, bf16[128,2048]{1,0:T(8,128)(2,1)S(1)}, u32[]{:S(2)}, u32[]{:S(2)}) collective-permute-start(bf16[128,2048]{1,0:T(8,128)(2,1)} %get-tuple-element.129), channel_id=1, source_target_pairs={{0,1},{1,0},{2,3},{3,2},{4,5},{5,4},{6,7},{7,6},{8,9},{9,8},{10,11... | collective-permute-start | bytes 1572872 | tf_op jit(solution)/shard_map/ppermute | solution.py:342
  520.9 36.4 %collective-permute-start.64 = (bf16[128,2048]{1,0:T(8,128)(2,1)}, bf16[128,2048]{1,0:T(8,128)(2,1)S(1)}, u32[]{:S(2)}, u32[]{:S(2)}) collective-permute-start(bf16[128,2048]{1,0:T(8,128)(2,1)} %get-tuple-element.106), channel_id=1, source_target_pairs={{0,1},{1,0},{2,3},{3,2},{4,5},{5,4},{6,7},{7,6},{8,9},{9,8},{10,11... | collective-permute-start | bytes 1572872 | tf_op jit(solution)/shard_map/ppermute | solution.py:342
  521.3 33.4 %collective-permute-start.60 = (bf16[128,2048]{1,0:T(8,128)(2,1)}, bf16[128,2048]{1,0:T(8,128)(2,1)S(1)}, u32[]{:S(2)}, u32[]{:S(2)}) collective-permute-start(bf16[128,2048]{1,0:T(8,128)(2,1)} %get-tuple-element.102), channel_id=1, source_target_pairs={{0,1},{1,0},{2,3},{3,2},{4,5},{5,4},{6,7},{7,6},{8,9},{9,8},{10,11... | collective-permute-start | bytes 1572872 | tf_op jit(solution)/shard_map/ppermute | solution.py:342
  524.6 31.8 %collective-permute-start.62 = (bf16[128,2048]{1,0:T(8,128)(2,1)S(1)}, bf16[128,2048]{1,0:T(8,128)(2,1)S(1)}, u32[]{:S(2)}, u32[]{:S(2)}) collective-permute-start(bf16[128,2048]{1,0:T(8,128)(2,1)S(1)} %add_convert_fusion.3), channel_id=1, source_target_pairs={{0,2},{1,3},{2,0},{3,1},{4,6},{5,7},{6,4},{7,5},{8,10},{9,11},{10,... | collective-permute-start | bytes 1572872 | tf_op jit(solution)/shard_map/ppermute | solution.py:342
  554.7 32.4 %collective-permute-start.59 = (bf16[128,2048]{1,0:T(8,128)(2,1)S(1)}, bf16[128,2048]{1,0:T(8,128)(2,1)S(1)}, u32[]{:S(2)}, u32[]{:S(2)}) collective-permute-start(bf16[128,2048]{1,0:T(8,128)(2,1)S(1)} %copy-done.41), channel_id=1, source_target_pairs={{0,1},{1,0},{2,3},{3,2},{4,5},{5,4},{6,7},{7,6},{8,9},{9,8},{10,11... | collective-permute-start | bytes 1572872 | tf_op jit(solution)/shard_map/ppermute | solution.py:342
  557.3 34.7 %collective-permute-start.63 = (bf16[128,2048]{1,0:T(8,128)(2,1)S(1)}, bf16[128,2048]{1,0:T(8,128)(2,1)S(1)}, u32[]{:S(2)}, u32[]{:S(2)}) collective-permute-start(bf16[128,2048]{1,0:T(8,128)(2,1)S(1)} %add_convert_fusion.2), channel_id=1, source_target_pairs={{0,4},{1,5},{2,6},{3,7},{4,0},{5,1},{6,2},{7,3},{8,12},{9,13},{10,... | collective-permute-start | bytes 1572872 | tf_op jit(solution)/shard_map/ppermute | solution.py:342
  557.5 31.0 %collective-permute-start.65 = (bf16[128,2048]{1,0:T(8,128)(2,1)S(1)}, bf16[128,2048]{1,0:T(8,128)(2,1)S(1)}, u32[]{:S(2)}, u32[]{:S(2)}) collective-permute-start(bf16[128,2048]{1,0:T(8,128)(2,1)S(1)} %add_convert_fusion.1), channel_id=1, source_target_pairs={{0,2},{1,3},{2,0},{3,1},{4,6},{5,7},{6,4},{7,5},{8,10},{9,11},{10,... | collective-permute-start | bytes 1572872 | tf_op jit(solution)/shard_map/ppermute | solution.py:342
  587.1 28.6 %collective-permute-start.56 = (bf16[128,2048]{1,0:T(8,128)(2,1)S(1)}, bf16[128,2048]{1,0:T(8,128)(2,1)S(1)}, u32[]{:S(2)}, u32[]{:S(2)}) collective-permute-start(bf16[128,2048]{1,0:T(8,128)(2,1)S(1)} %add_convert_fusion.6), channel_id=1, source_target_pairs={{0,4},{1,5},{2,6},{3,7},{4,0},{5,1},{6,2},{7,3},{8,12},{9,13},{10,... | collective-permute-start | bytes 1572872 | tf_op jit(solution)/shard_map/ppermute | solution.py:342
  587.1 28.5 %collective-permute-start.58 = (bf16[128,2048]{1,0:T(8,128)(2,1)S(1)}, bf16[128,2048]{1,0:T(8,128)(2,1)S(1)}, u32[]{:S(2)}, u32[]{:S(2)}) collective-permute-start(bf16[128,2048]{1,0:T(8,128)(2,1)S(1)} %add_convert_fusion.5), channel_id=1, source_target_pairs={{0,2},{1,3},{2,0},{3,1},{4,6},{5,7},{6,4},{7,5},{8,10},{9,11},{10,... | collective-permute-start | bytes 1572872 | tf_op jit(solution)/shard_map/ppermute | solution.py:342
  588.5 39.9 %collective-permute-start.68 = (bf16[128,2048]{1,0:T(8,128)(2,1)S(1)}, bf16[128,2048]{1,0:T(8,128)(2,1)S(1)}, u32[]{:S(2)}, u32[]{:S(2)}) collective-permute-start(bf16[128,2048]{1,0:T(8,128)(2,1)S(1)} %fusion.7), channel_id=1, source_target_pairs={{0,0},{1,8},{2,16},{3,24},{4,4},{5,12},{6,20},{7,28},{8,1},{9,9},{... | collective-permute-start | bytes 1572872 | tf_op jit(solution)/shard_map/ppermute | solution.py:353
  591.9 32.6 %collective-permute-start.74 = (f32[24,2048]{1,0:T(8,128)S(1)}, f32[24,2048]{1,0:T(8,128)S(1)}, u32[]{:S(2)}, u32[]{:S(2)}) collective-permute-start(f32[24,2048]{1,0:T(8,128)S(1)} %add.246), channel_id=1, source_target_pairs={{0,4},{1,5},{2,6},{3,7},{4,0},{5,1},{6,2},{7,3},{8,12},{9,13},{10,... | collective-permute-start | bytes 589832 | tf_op jit(solution)/shard_map/ppermute | solution.py:346
  (78 other events, 1372.5 us)
Sparse Core Ops, SparseCore 0:
  10.8 90.1 all-gather.5
  104.0 87.8 all-gather.3
  438.7 23.2 reduce-scatter.2
  464.4 82.1 reduce-scatter.4
